TPU v7x, 256 devices: a whole 4x4x8 slice. The times are simulated.
256 devices in a mesh: lon: 64 (over z, y_hi, x), lat: 4 (over y_lo, core).
Axes of the slice: x: 4, y: 4 (y_hi: 2, y_lo: 2; y = y_hi * 2 + y_lo), z: 8, core: 2. Of those that a mesh axis runs over, the one named last changes fastest.
Arguments:
- thermal_anomaly: float32 [32, 512, 512], P(None, 'lon', 'lat'), may hold values from -5 to 5
- saltiness_anomaly: float32 [32, 512, 512], P(None, 'lon', 'lat'), may hold values from -5 to 5
- zonal_flow: float32 [32, 512, 512], P(None, 'lon', 'lat'), may hold values from -1.2 to 1.2
- meridional_flow: float32 [32, 512, 512], P(None, 'lon', 'lat'), may hold values from -1.2 to 1.2
- submerged_strata_number: int32 [512, 512], P('lon', 'lat'), may hold values from 1 to 32
- sea_indicator: int32 [512, 512], P('lon', 'lat'), may hold values 0 or 1
- strata_thickness: float32 [32], replicated, may hold values from 0.5 to 2
- earlier_sea_elevation: float32 [512, 512], P('lon', 'lat'), may hold values from -3 to 3
- sea_drive_term: float32 [512, 512], P('lon', 'lat'), may hold values from -10 to 10
Outputs:
- new_temperature: float32 [32, 512, 512], P(None, 'lon', 'lat')
- new_salinity: float32 [32, 512, 512], P(None, 'lon', 'lat')
- new_u_velocity: float32 [32, 512, 512], P(None, 'lon', 'lat')
- new_v_velocity: float32 [32, 512, 512], P(None, 'lon', 'lat')
- new_surface: float32 [512, 512], P('lon', 'lat')
- residual_rms: float32 [], replicated
All inputs are finite; a program needn't handle non-finite values. No bound on the sum of `sea_indicator` on one device may be relied on, other than what follows from the above.
Results may differ from a plain program's by a relative error of at most 0.0003.
Values sent between devices are 32-bit elements; how exact they have to be, the bound alone decides.
No kernel may reach another device: no remote copies, remote signals or barrier semaphores. Data moves between devices by JAX's collectives and lax.ppermute only.
A program may use at most 128 MiB of HBM per device.

v0:
```python
import jax
import jax.numpy as jnp
from jax import lax
from jax.sharding import Mesh
from jax.sharding import PartitionSpec as P

ITERS = 4
LAT = ("lat_0", "lat_1")
LON = ("lon_0", "lon_1", "lon_2")
LON_LAT = ("lon_0", "lon_1", "lon_2", "lat_0", "lat_1")


DIFFUSION = 0.15
MIXING = 0.1
EXPANSION = 0.2
CONTRACTION = 0.15
PRESSURE_SCALE = 0.02
CORIOLIS = 0.5
FRICTION = 0.01
DIVERGENCE = 0.3
STORAGE = 0.1
SPECTRUM_LOW = 0.1
SPECTRUM_HIGH = 1.9
GRAVITY = 0.3
EPSILON = 1e-06


def extended(x, sides, width, wrap):
    for axis, dim in sides:
        devices, length = (lax.axis_size(axis), x.shape[dim])
        up = [(i, (i + 1) % devices) for i in range(devices if wrap else devices - 1)]
        down = [(j, i) for i, j in up]
        last = lax.slice_in_dim(x, length - width, length, axis=dim)
        initial = lax.slice_in_dim(x, 0, width, axis=dim)
        before = lax.ppermute(last, axis, up)
        after = lax.ppermute(initial, axis, down)
        x = jnp.concatenate([before, x, after], axis=dim)
    return x


def joined_along(pieces, dim):
    lengths = list(pieces.shape[1:])
    lengths[dim] *= pieces.shape[0]
    return jnp.moveaxis(pieces, 0, dim).reshape(lengths)


def from_everyone(x, axis):
    copies = jnp.broadcast_to(x, (lax.axis_size(axis), *x.shape))
    return lax.all_to_all(copies, axis, split_axis=0, concat_axis=0, tiled=True)


def collect(x, axis, dim):
    return joined_along(from_everyone(x, axis), dim)


def over_axes(x, axes):
    for axis in axes:
        x = lax.psum(x, axis)
    return x


def extend(field, sign_rows, width):
    meridian_points = field.shape[2]
    station_indices = field.shape[1]
    widened = extended(field, ((LAT, 2),), width, False)
    top_rows = field[:, :, meridian_points - width :]
    whole_rows = collect(top_rows, LON, 1)
    offset = lax.axis_index(LON) * station_indices
    mirrored = lax.dynamic_slice_in_dim(jnp.flip(whole_rows, 1), offset, station_indices, 1)
    folded = jnp.flip(mirrored, 2) * sign_rows[:, None, None]
    at_pole = lax.axis_index(LAT) == lax.axis_size(LAT) - 1
    northern = jnp.where(at_pole, folded, widened[:, :, meridian_points + width :])
    widened = lax.dynamic_update_slice_in_dim(widened, northern, meridian_points + width, 2)
    return extended(widened, ((LON, 1),), width, True)


def center(field):
    return field[:, 1:-1, 1:-1]


def to_east(field):
    return field[:, 2:, 1:-1]


def to_west(field):
    return field[:, :-2, 1:-1]


def to_north(field):
    return field[:, 1:-1, 2:]


def to_south(field):
    return field[:, 1:-1, :-2]


def shrink(field):
    return field[:, 1:-1, 1:-1]


def level_mask(strata_bottoms, strata_indices):
    level_index = jnp.arange(strata_indices).astype(strata_bottoms.dtype)[:, None, None]
    return jnp.where(level_index + 0.5 < strata_bottoms, 1.0, 0.0).astype(strata_bottoms.dtype)


def laplace(field, mask):
    middle = center(field)
    total = to_east(mask) * (to_east(field) - middle) + to_west(mask) * (to_west(field) - middle)
    total = (
        total
        + to_north(mask) * (to_north(field) - middle)
        + to_south(mask) * (to_south(field) - middle)
    )
    return center(mask) * total


def tracer_step(tracer, u_field, v_field, mask, thickness):
    middle = center(tracer)
    wet_mid = center(mask)
    u_mid = center(u_field)
    v_mid = center(v_field)
    flux_east = (
        wet_mid
        * to_east(mask)
        * (
            0.5 * (u_mid + to_east(u_field)) * 0.5 * (middle + to_east(tracer))
            - DIFFUSION * (to_east(tracer) - middle)
        )
    )
    flux_west = (
        wet_mid
        * to_west(mask)
        * (
            0.5 * (to_west(u_field) + u_mid) * 0.5 * (to_west(tracer) + middle)
            - DIFFUSION * (middle - to_west(tracer))
        )
    )
    flux_north = (
        wet_mid
        * to_north(mask)
        * (
            0.5 * (v_mid + to_north(v_field)) * 0.5 * (middle + to_north(tracer))
            - DIFFUSION * (to_north(tracer) - middle)
        )
    )
    flux_south = (
        wet_mid
        * to_south(mask)
        * (
            0.5 * (to_south(v_field) + v_mid) * 0.5 * (to_south(tracer) + middle)
            - DIFFUSION * (middle - to_south(tracer))
        )
    )
    horizontal = flux_west - flux_east + flux_south - flux_north
    spacing = 0.5 * (thickness[1:] + thickness[:-1])
    vflux = wet_mid[1:] * wet_mid[:-1] * (middle[1:] - middle[:-1]) / spacing[:, None, None]
    zero_plane = jnp.zeros_like(middle[:1])
    upper_flux = jnp.concatenate([vflux, zero_plane], axis=0)
    lower_flux = jnp.concatenate([zero_plane, vflux], axis=0)
    vertical = MIXING * (upper_flux - lower_flux) / thickness[:, None, None]
    return wet_mid * (middle + horizontal + vertical)


def pressure_gradients(temp_rim, salt_rim, mask, thickness):
    density = (CONTRACTION * salt_rim - EXPANSION * temp_rim) * thickness[:, None, None] * mask
    pressure = jnp.cumsum(density, axis=0)
    middle = center(pressure)
    wet_mid = center(mask)
    grad_x = (
        0.5
        * wet_mid
        * (
            to_east(mask) * (to_east(pressure) - middle)
            + to_west(mask) * (middle - to_west(pressure))
        )
    )
    grad_y = (
        0.5
        * wet_mid
        * (
            to_north(mask) * (to_north(pressure) - middle)
            + to_south(mask) * (middle - to_south(pressure))
        )
    )
    return (grad_x, grad_y)


def baroclinic(narrow, mask_narrow, lap_u, lap_v, thickness, coriolis, strata_indices):
    temp_rim = narrow[:strata_indices]
    salt_rim = narrow[strata_indices : 2 * strata_indices]
    u_rim = narrow[2 * strata_indices : 3 * strata_indices]
    v_rim = narrow[3 * strata_indices : 4 * strata_indices]
    new_temp = tracer_step(temp_rim, u_rim, v_rim, mask_narrow, thickness)
    new_salt = tracer_step(salt_rim, u_rim, v_rim, mask_narrow, thickness)
    grad_x, grad_y = pressure_gradients(temp_rim, salt_rim, mask_narrow, thickness)
    friction_u = laplace(lap_u, mask_narrow)
    friction_v = laplace(lap_v, mask_narrow)
    wet_mid = center(mask_narrow)
    u_mid = center(u_rim)
    v_mid = center(v_rim)
    u_star = wet_mid * (u_mid + coriolis * v_mid - PRESSURE_SCALE * grad_x - FRICTION * friction_u)
    v_star = wet_mid * (v_mid - coriolis * u_mid - PRESSURE_SCALE * grad_y - FRICTION * friction_v)
    height = jnp.sum(thickness[:, None, None] * mask_narrow, axis=0, keepdims=True)
    return (new_temp, new_salt, u_star, v_star, height, wet_mid)


def solver_weights(height, strata_indices):
    middle = center(height)
    w_east = jnp.minimum(middle, to_east(height)) / strata_indices
    w_west = jnp.minimum(middle, to_west(height)) / strata_indices
    w_north = jnp.minimum(middle, to_north(height)) / strata_indices
    w_south = jnp.minimum(middle, to_south(height)) / strata_indices
    diagonal = STORAGE + w_east + w_west + w_north + w_south
    return (w_east, w_west, w_north, w_south, diagonal)


def apply_operator(weights, field_rim):
    w_east, w_west, w_north, w_south, diagonal = weights
    coupled = (
        w_east * to_east(field_rim)
        + w_west * to_west(field_rim)
        + w_north * to_north(field_rim)
        + w_south * to_south(field_rim)
    )
    return diagonal * center(field_rim) - coupled


def line_factor(w_west, w_east, diagonal):
    count = diagonal.shape[0]
    position = jnp.arange(count).reshape((count,) + (1,) * (diagonal.ndim - 1))
    lower_band = jnp.where(position > 0, -w_west, 0.0)
    upper_band = jnp.where(position < count - 1, -w_east, 0.0)

    def forward(previous, inputs):
        lower_row, diag_row, upper_row = inputs
        inverse = 1.0 / (diag_row - lower_row * previous)
        factor = upper_row * inverse
        return (factor, (factor, inverse))

    _, (factors, pivots) = lax.scan(
        forward, jnp.zeros_like(diagonal[0]), (lower_band, diagonal, upper_band)
    )
    return (lower_band, factors, pivots)


def line_solve(lower_band, factors, pivots, values):

    def forward(previous, inputs):
        lower_row, inverse, value_row = inputs
        current = (value_row - lower_row * previous) * inverse
        return (current, current)

    _, partial_rows = lax.scan(forward, jnp.zeros_like(values[0]), (lower_band, pivots, values))

    def backward(following, inputs):
        factor, partial_row = inputs
        current = partial_row - factor * following
        return (current, current)

    _, solved = lax.scan(backward, jnp.zeros_like(values[0]), (factors, partial_rows), reverse=True)
    return solved


def global_rms(residual, cells):
    total = over_axes(jnp.sum(residual * residual), LON_LAT)
    return jnp.sqrt(total / cells + EPSILON)


def per_device(
    thermal_anomaly,
    saltiness_anomaly,
    zonal_flow,
    meridional_flow,
    submerged_strata_number,
    sea_indicator,
    strata_thickness,
    earlier_sea_elevation,
    sea_drive_term,
):
    strata_indices = thermal_anomaly.shape[0]
    station_indices = thermal_anomaly.shape[1]
    meridian_points = thermal_anomaly.shape[2]
    real_number_kind = thermal_anomaly.dtype
    wet_surface = sea_indicator.astype(real_number_kind)
    strata_bottoms = (submerged_strata_number * sea_indicator).astype(real_number_kind)[None]
    joined_tracers = jnp.concatenate(
        [thermal_anomaly, saltiness_anomaly, zonal_flow, meridional_flow, strata_bottoms], axis=0
    )
    sign_rows = jnp.concatenate(
        [
            jnp.ones(2 * strata_indices, real_number_kind),
            -jnp.ones(2 * strata_indices, real_number_kind),
            jnp.ones(1, real_number_kind),
        ]
    )
    wide_rim = extend(joined_tracers, sign_rows, 2)
    mask_wide = level_mask(wide_rim[4 * strata_indices :], strata_indices)
    narrow = shrink(wide_rim)
    mask_narrow = shrink(mask_wide)
    lap_u = laplace(wide_rim[2 * strata_indices : 3 * strata_indices], mask_wide)
    lap_v = laplace(wide_rim[3 * strata_indices : 4 * strata_indices], mask_wide)
    lat_index = (lax.axis_index(LAT) * meridian_points + jnp.arange(meridian_points)).astype(
        real_number_kind
    )
    total_lat = lax.axis_size(LAT) * meridian_points
    coriolis = CORIOLIS * (2.0 * (lat_index + 0.5) / total_lat - 1.0)
    new_temp, new_salt, u_star, v_star, height, wet_mid = baroclinic(
        narrow, mask_narrow, lap_u, lap_v, strata_thickness, coriolis, strata_indices
    )
    weights = solver_weights(height, strata_indices)
    lower_band, factors, pivots = line_factor(weights[1][0], weights[0][0], weights[4][0])

    def precondition(values):
        return line_solve(lower_band, factors, pivots, values[0])[None]

    transport_u = jnp.sum(strata_thickness[:, None, None] * u_star, axis=0, keepdims=True)
    transport_v = jnp.sum(strata_thickness[:, None, None] * v_star, axis=0, keepdims=True)
    start_field = (wet_surface * earlier_sea_elevation)[None]
    surface_signs = jnp.array([-1.0, -1.0, 1.0], real_number_kind)
    plus_one = jnp.ones(1, real_number_kind)
    moved = extend(
        jnp.concatenate([transport_u, transport_v, start_field], axis=0), surface_signs, 1
    )
    divergence = 0.5 * (to_east(moved[0:1]) - to_west(moved[0:1])) + 0.5 * (
        to_north(moved[1:2]) - to_south(moved[1:2])
    )
    right_side = wet_surface[None] * (sea_drive_term[None] - DIVERGENCE * divergence)
    solution = center(moved[2:3])
    residual = right_side - apply_operator(weights, moved[2:3])
    spectrum_mid = 0.5 * (SPECTRUM_HIGH + SPECTRUM_LOW)
    spectrum_half = 0.5 * (SPECTRUM_HIGH - SPECTRUM_LOW)
    spectrum_ratio = spectrum_mid / spectrum_half
    direction = precondition(residual) / spectrum_mid
    cheby_rho = 1.0 / spectrum_ratio
    for step_index in range(ITERS):
        solution = solution + direction
        if step_index + 1 < ITERS:
            residual = residual - apply_operator(weights, extend(direction, plus_one, 1))
        if step_index + 1 < ITERS:
            rho_next = 1.0 / (2.0 * spectrum_ratio - cheby_rho)
            direction = (
                rho_next * cheby_rho * direction
                + 2.0 * rho_next / spectrum_half * precondition(residual)
            )
            cheby_rho = rho_next
    cells = lax.axis_size(LON) * station_indices * lax.axis_size(LAT) * meridian_points
    final_rim = extend(solution, plus_one, 1)
    residual_rms = global_rms(right_side - apply_operator(weights, final_rim), cells)
    slope_x = 0.5 * (to_east(final_rim) - to_west(final_rim))
    slope_y = 0.5 * (to_north(final_rim) - to_south(final_rim))
    new_u = wet_mid * (u_star - GRAVITY * slope_x)
    new_v = wet_mid * (v_star - GRAVITY * slope_y)
    return (new_temp, new_salt, new_u, new_v, solution[0], residual_rms)


def solution(mesh):
    finer = Mesh(mesh.devices.reshape(8, 2, 4, 2, 2), ("lon_0", "lon_1", "lon_2", "lat_0", "lat_1"))
    return jax.shard_map(
        per_device,
        mesh=finer,
        in_specs=(
            P(None, LON, LAT),
            P(None, LON, LAT),
            P(None, LON, LAT),
            P(None, LON, LAT),
            P(LON, LAT),
            P(LON, LAT),
            P(),
            P(LON, LAT),
            P(LON, LAT),
        ),
        out_specs=(
            P(None, LON, LAT),
            P(None, LON, LAT),
            P(None, LON, LAT),
            P(None, LON, LAT),
            P(LON, LAT),
            P(),
        ),
        check_vma=False,
    )
```

profile of v0, /device:TPU:1, one launch (start us, length us, event | category | flops | bytes accessed | tf_op | source)
XLA Modules:
  0.0 311.2 jit_solution(4487948480448817182)
XLA Ops:
  6.7 15.2 %all-to-all-start = ((f32[64,129,8,2]{1,2,3,0:T(8,128)}), f32[64,129,8,2]{1,2,3,0:T(8,128)S(1)}, u32[]{:S(2)}, u32[]{:S(2)}) async-start(f32[64,129,8,2]{1,2,3,0:T(8,128)} %broadcast_in_dim.137), calls=%async_computation | async-start | bytes 2097152 | tf_op jit(solution)/shard_map/all_to_all | solution.py:49
  22.0 3.1 %collective-permute-start = (f32[129,8,2]{0,1,2:T(8,128)S(1)}, f32[129,8,2]{0,1,2:T(8,128)S(1)}, u32[]{:S(2)}, u32[]{:S(2)}) collective-permute-start(f32[129,8,2]{0,1,2:T(8,128)S(1)} %copy.114), channel_id=1, source_target_pairs={{0,1},{1,2},{2,3},{4,5},{5,6},{6,7},{8,9},{9,10},{10,11},{12,13},{... | collective-permute-start | bytes 24776 | tf_op jit(solution)/shard_map/ppermute | solution.py:35
  25.4 1.9 collective-permute-start.1
  27.9 3.2 %collective-permute-done.1 = f32[129,8,2]{0,1,2:T(8,128)S(1)} collective-permute-done((f32[129,8,2]{0,1,2:T(8,128)S(1)}, f32[129,8,2]{0,1,2:T(8,128)S(1)}, u32[]{:S(2)}, u32[]{:S(2)}) %collective-permute-start.1) | collective-permute-done | bytes 8288 | tf_op jit(solution)/shard_map/ppermute | solution.py:36
  32.3 1.5 pad_maximum_fusion.1
  33.8 14.3 %all-to-all-done = f32[64,129,8,2]{1,2,3,0:T(8,128)S(1)} async-done(((f32[64,129,8,2]{1,2,3,0:T(8,128)}), f32[64,129,8,2]{1,2,3,0:T(8,128)S(1)}, u32[]{:S(2)}, u32[]{:S(2)}) %all-to-all-start) | async-done | bytes 528416 | tf_op jit(solution)/shard_map/all_to_all | solution.py:49
  49.3 25.6 %dynamic_update_slice.73 = f32[129,8,132]{2,1,0:T(8,128)S(1)} dynamic-update-slice(f32[129,8,132]{2,1,0:T(8,128)S(1)} %pad_maximum_fusion.1, f32[129,8,2]{2,1,0:T(8,128)S(1)} %copy.120, s32[]{:T(128)} %constant.277.clone.1, s32[]{:T(128)} %constant.277.clone.1, s32[]{:T(128)} %constant.287.clone.1) | dynamic-update-slice | bytes 16516 | tf_op jit(solution)/shard_map/dynamic_update_slice | solution.py:73
  75.9 6.5 %collective-permute-start.3 = (f32[129,2,132]{2,1,0:T(2,128)S(1)}, f32[129,2,132]{2,1,0:T(2,128)S(1)}, u32[]{:S(2)}, u32[]{:S(2)}) collective-permute-start(f32[129,2,132]{2,1,0:T(2,128)S(1)} %get-tuple-element.947), channel_id=1, source_target_pairs={{4,0},{8,4},{12,8},{16,12},{20,16},{24,20},{28,24},{32,28},{36,32}... | collective-permute-start | bytes 408680 | tf_op jit(solution)/shard_map/ppermute | solution.py:36
  82.4 3.8 %collective-permute-done.2 = f32[129,2,132]{2,1,0:T(2,128)S(1)} collective-permute-done((f32[129,2,132]{2,1,0:T(2,128)S(1)}, f32[129,2,132]{2,1,0:T(2,128)S(1)}, u32[]{:S(2)}, u32[]{:S(2)}) %collective-permute-start.2) | collective-permute-done | bytes 136256 | tf_op jit(solution)/shard_map/ppermute | solution.py:35
  87.5 1.3 multiply_reduce_fusion
  91.8 11.7 %all-to-all-start.1 = ((f32[64,3,8,1]{2,3,1,0:T(1,128)}), f32[64,3,8,1]{2,3,1,0:T(1,128)S(1)}, u32[]{:S(2)}, u32[]{:S(2)}) async-start(f32[64,3,8,1]{2,3,1,0:T(1,128)} %broadcast_in_dim.143), calls=%async_computation.1 | async-start | bytes 196608 | tf_op jit(solution)/shard_map/all_to_all | solution.py:49
  103.5 5.7 %collective-permute-start.5 = (f32[3,8,1]{2,1,0:T(8,128)S(1)}, f32[3,8,1]{2,1,0:T(8,128)S(1)}, u32[]{:S(2)}, u32[]{:S(2)}) collective-permute-start(f32[3,8,1]{2,1,0:T(8,128)S(1)} %get-tuple-element.957), channel_id=1, source_target_pairs={{1,0},{2,1},{3,2},{5,4},{6,5},{7,6},{9,8},{10,9},{11,10},{13,12},{... | collective-permute-start | bytes 296 | tf_op jit(solution)/shard_map/ppermute | solution.py:36
  109.2 2.4 collective-permute-start.4
  112.3 2.2 all-to-all-done.1
  114.9 3.9 %rev.27 = f32[3,512,1]{2,1,0:T(8,128)} reverse(f32[3,512,1]{2,1,0:T(8,128)S(1)} %reshape.67), dimensions={1} | reverse | bytes 12288 | tf_op jit(solution)/shard_map/jit(_flip)/rev | solution.py:69
  119.8 5.7 %collective-permute-start.6 = (f32[3,1,130]{2,1,0:T(1,128)S(1)}, f32[3,1,130]{2,1,0:T(1,128)S(1)}, u32[]{:S(2)}, u32[]{:S(2)}) collective-permute-start(f32[3,1,130]{2,1,0:T(1,128)S(1)} %get-tuple-element.954), channel_id=1, source_target_pairs={{4,0},{8,4},{12,8},{16,12},{20,16},{24,20},{28,24},{32,28},{36,32}... | collective-permute-start | bytes 4688 | tf_op jit(solution)/shard_map/ppermute | solution.py:36
  126.4 7.3 %collective-permute-done.7 = f32[3,1,130]{2,1,0:T(1,128)S(1)} collective-permute-done((f32[3,1,130]{2,1,0:T(1,128)S(1)}, f32[3,1,130]{2,1,0:T(1,128)S(1)}, u32[]{:S(2)}, u32[]{:S(2)}) %collective-permute-start.7) | collective-permute-done | bytes 1592 | tf_op jit(solution)/shard_map/ppermute | solution.py:35
  135.8 5.0 %all-to-all-start.2 = ((f32[64,1,8,1]{2,3,1,0:T(1,128)}), f32[64,1,8,1]{2,3,1,0:T(1,128)S(1)}, u32[]{:S(2)}, u32[]{:S(2)}) async-start(f32[64,1,8,1]{2,3,1,0:T(1,128)} %broadcast_in_dim.150), calls=%async_computation.2 | async-start | bytes 65536 | tf_op jit(solution)/shard_map/all_to_all | solution.py:49
  140.8 3.9 %collective-permute-start.9 = (f32[1,8,1]{2,1,0:T(8,128)S(1)}, f32[1,8,1]{2,1,0:T(8,128)S(1)}, u32[]{:S(2)}, u32[]{:S(2)}) collective-permute-start(f32[1,8,1]{2,1,0:T(8,128)S(1)} %get-tuple-element.979), channel_id=1, source_target_pairs={{1,0},{2,1},{3,2},{5,4},{6,5},{7,6},{9,8},{10,9},{11,10},{13,12},{... | collective-permute-start | bytes 104 | tf_op jit(solution)/shard_map/ppermute | solution.py:36
  144.7 3.3 %collective-permute-start.8 = (f32[1,8,1]{2,1,0:T(8,128)S(1)}, f32[1,8,1]{2,1,0:T(8,128)S(1)}, u32[]{:S(2)}, u32[]{:S(2)}) collective-permute-start(f32[1,8,1]{2,1,0:T(8,128)S(1)} %get-tuple-element.980), channel_id=1, source_target_pairs={{0,1},{1,2},{2,3},{4,5},{5,6},{6,7},{8,9},{9,10},{10,11},{12,13},{... | collective-permute-start | bytes 104 | tf_op jit(solution)/shard_map/ppermute | solution.py:35
  148.9 2.7 all-to-all-done.2
  153.2 5.3 %collective-permute-start.10 = (f32[1,1,130]{2,1,0:T(1,128)S(1)}, f32[1,1,130]{2,1,0:T(1,128)S(1)}, u32[]{:S(2)}, u32[]{:S(2)}) collective-permute-start(f32[1,1,130]{2,1,0:T(1,128)S(1)} %get-tuple-element.967), channel_id=1, source_target_pairs={{4,0},{8,4},{12,8},{16,12},{20,16},{24,20},{28,24},{32,28},{36,32}... | collective-permute-start | bytes 1568 | tf_op jit(solution)/shard_map/ppermute | solution.py:36
  159.2 7.4 %collective-permute-done.11 = f32[1,1,130]{2,1,0:T(1,128)S(1)} collective-permute-done((f32[1,1,130]{2,1,0:T(1,128)S(1)}, f32[1,1,130]{2,1,0:T(1,128)S(1)}, u32[]{:S(2)}, u32[]{:S(2)}) %collective-permute-start.11) | collective-permute-done | bytes 552 | tf_op jit(solution)/shard_map/ppermute | solution.py:35
  168.8 5.0 %all-to-all-start.3 = ((f32[64,1,8,1]{2,3,1,0:T(1,128)}), f32[64,1,8,1]{2,3,1,0:T(1,128)S(1)}, u32[]{:S(2)}, u32[]{:S(2)}) async-start(f32[64,1,8,1]{2,3,1,0:T(1,128)} %broadcast_in_dim.151), calls=%async_computation.3 | async-start | bytes 65536 | tf_op jit(solution)/shard_map/all_to_all | solution.py:49
  173.8 2.2 collective-permute-start.13
  176.0 5.0 %collective-permute-start.12 = (f32[1,8,1]{2,1,0:T(8,128)S(1)}, f32[1,8,1]{2,1,0:T(8,128)S(1)}, u32[]{:S(2)}, u32[]{:S(2)}) collective-permute-start(f32[1,8,1]{2,1,0:T(8,128)S(1)} %get-tuple-element.977), channel_id=1, source_target_pairs={{0,1},{1,2},{2,3},{4,5},{5,6},{6,7},{8,9},{9,10},{10,11},{12,13},{... | collective-permute-start | bytes 104 | tf_op jit(solution)/shard_map/ppermute | solution.py:35
  181.8 2.7 all-to-all-done.3
  185.7 5.3 %collective-permute-start.14 = (f32[1,1,130]{2,1,0:T(1,128)S(1)}, f32[1,1,130]{2,1,0:T(1,128)S(1)}, u32[]{:S(2)}, u32[]{:S(2)}) collective-permute-start(f32[1,1,130]{2,1,0:T(1,128)S(1)} %get-tuple-element.965), channel_id=1, source_target_pairs={{4,0},{8,4},{12,8},{16,12},{20,16},{24,20},{28,24},{32,28},{36,32}... | collective-permute-start | bytes 1568 | tf_op jit(solution)/shard_map/ppermute | solution.py:36
  191.7 7.4 %collective-permute-done.15 = f32[1,1,130]{2,1,0:T(1,128)S(1)} collective-permute-done((f32[1,1,130]{2,1,0:T(1,128)S(1)}, f32[1,1,130]{2,1,0:T(1,128)S(1)}, u32[]{:S(2)}, u32[]{:S(2)}) %collective-permute-start.15) | collective-permute-done | bytes 552 | tf_op jit(solution)/shard_map/ppermute | solution.py:35
  201.2 5.0 %all-to-all-start.4 = ((f32[64,1,8,1]{2,3,1,0:T(1,128)}), f32[64,1,8,1]{2,3,1,0:T(1,128)S(1)}, u32[]{:S(2)}, u32[]{:S(2)}) async-start(f32[64,1,8,1]{2,3,1,0:T(1,128)} %broadcast_in_dim.152), calls=%async_computation.4 | async-start | bytes 65536 | tf_op jit(solution)/shard_map/all_to_all | solution.py:49
  206.3 1.9 collective-permute-start.17
  208.2 5.3 %collective-permute-start.16 = (f32[1,8,1]{2,1,0:T(8,128)S(1)}, f32[1,8,1]{2,1,0:T(8,128)S(1)}, u32[]{:S(2)}, u32[]{:S(2)}) collective-permute-start(f32[1,8,1]{2,1,0:T(8,128)S(1)} %get-tuple-element.974), channel_id=1, source_target_pairs={{0,1},{1,2},{2,3},{4,5},{5,6},{6,7},{8,9},{9,10},{10,11},{12,13},{... | collective-permute-start | bytes 104 | tf_op jit(solution)/shard_map/ppermute | solution.py:35
  214.3 2.7 all-to-all-done.4
  218.2 5.3 %collective-permute-start.18 = (f32[1,1,130]{2,1,0:T(1,128)S(1)}, f32[1,1,130]{2,1,0:T(1,128)S(1)}, u32[]{:S(2)}, u32[]{:S(2)}) collective-permute-start(f32[1,1,130]{2,1,0:T(1,128)S(1)} %get-tuple-element.963), channel_id=1, source_target_pairs={{4,0},{8,4},{12,8},{16,12},{20,16},{24,20},{28,24},{32,28},{36,32}... | collective-permute-start | bytes 1568 | tf_op jit(solution)/shard_map/ppermute | solution.py:36
  224.2 7.4 %collective-permute-done.19 = f32[1,1,130]{2,1,0:T(1,128)S(1)} collective-permute-done((f32[1,1,130]{2,1,0:T(1,128)S(1)}, f32[1,1,130]{2,1,0:T(1,128)S(1)}, u32[]{:S(2)}, u32[]{:S(2)}) %collective-permute-start.19) | collective-permute-done | bytes 552 | tf_op jit(solution)/shard_map/ppermute | solution.py:35
  233.8 5.3 %all-to-all-start.5 = ((f32[64,1,8,1]{2,3,1,0:T(1,128)}), f32[64,1,8,1]{2,3,1,0:T(1,128)S(1)}, u32[]{:S(2)}, u32[]{:S(2)}) async-start(f32[64,1,8,1]{2,3,1,0:T(1,128)} %broadcast_in_dim.153), calls=%async_computation.5 | async-start | bytes 65536 | tf_op jit(solution)/shard_map/all_to_all | solution.py:49
  239.1 1.9 collective-permute-start.21
  241.0 5.3 %collective-permute-start.20 = (f32[1,8,1]{2,1,0:T(8,128)S(1)}, f32[1,8,1]{2,1,0:T(8,128)S(1)}, u32[]{:S(2)}, u32[]{:S(2)}) collective-permute-start(f32[1,8,1]{2,1,0:T(8,128)S(1)} %get-tuple-element.971), channel_id=1, source_target_pairs={{0,1},{1,2},{2,3},{4,5},{5,6},{6,7},{8,9},{9,10},{10,11},{12,13},{... | collective-permute-start | bytes 104 | tf_op jit(solution)/shard_map/ppermute | solution.py:35
  247.1 2.7 all-to-all-done.5
  250.9 5.3 %collective-permute-start.22 = (f32[1,1,130]{2,1,0:T(1,128)S(1)}, f32[1,1,130]{2,1,0:T(1,128)S(1)}, u32[]{:S(2)}, u32[]{:S(2)}) collective-permute-start(f32[1,1,130]{2,1,0:T(1,128)S(1)} %get-tuple-element.962), channel_id=1, source_target_pairs={{4,0},{8,4},{12,8},{16,12},{20,16},{24,20},{28,24},{32,28},{36,32}... | collective-permute-start | bytes 1568 | tf_op jit(solution)/shard_map/ppermute | solution.py:36
  257.0 7.4 %collective-permute-done.23 = f32[1,1,130]{2,1,0:T(1,128)S(1)} collective-permute-done((f32[1,1,130]{2,1,0:T(1,128)S(1)}, f32[1,1,130]{2,1,0:T(1,128)S(1)}, u32[]{:S(2)}, u32[]{:S(2)}) %collective-permute-start.23) | collective-permute-done | bytes 552 | tf_op jit(solution)/shard_map/ppermute | solution.py:35
  265.1 11.5 %psum.35 = f32[]{:T(128)} all-reduce(f32[]{:T(128)} %fusion.111), channel_id=1, replica_groups=mesh['lon_0'=8,'lon_1'=2,'lon_2'=4,'lat_0'=2,'lat_1'=2] {'lon_0'}, use_global_device_ids=true, to_apply=%region_23.24 | all-reduce | flops 1 | bytes 8 | tf_op jit(solution)/shard_map/psum | solution.py:58
  276.6 5.9 %psum.36 = f32[]{:T(128)} all-reduce(f32[]{:T(128)} %psum.35), channel_id=1, replica_groups=mesh['lon_0'=8,'lon_1'=2,'lon_2'=4,'lat_0'=2,'lat_1'=2] {'lon_1'}, use_global_device_ids=true, to_apply=%region_24.25 | all-reduce | flops 1 | bytes 8 | tf_op jit(solution)/shard_map/psum | solution.py:58
  282.8 6.6 %psum.37 = f32[]{:T(128)} all-reduce(f32[]{:T(128)} %psum.36), channel_id=1, replica_groups=mesh['lon_0'=8,'lon_1'=2,'lon_2'=4,'lat_0'=2,'lat_1'=2] {'lon_2'}, use_global_device_ids=true, to_apply=%region_25.26 | all-reduce | flops 1 | bytes 8 | tf_op jit(solution)/shard_map/psum | solution.py:58
  289.5 1.4 add_multiply_fusion
  290.9 4.4 %psum.38 = f32[]{:T(128)} all-reduce(f32[]{:T(128)} %psum.37), channel_id=1, replica_groups=mesh['lon_0'=8,'lon_1'=2,'lon_2'=4,'lat_0'=2,'lat_1'=2] {'lat_0'}, use_global_device_ids=true, to_apply=%region_26.27 | all-reduce | flops 1 | bytes 8 | tf_op jit(solution)/shard_map/psum | solution.py:58
  295.3 1.4 add_multiply_fusion.1
  296.8 11.7 %psum.39 = f32[]{:T(128)} all-reduce(f32[]{:T(128)} %psum.38), channel_id=1, replica_groups=mesh['lon_0'=8,'lon_1'=2,'lon_2'=4,'lat_0'=2,'lat_1'=2] {'lat_1'}, use_global_device_ids=true, to_apply=%region_27.28 | all-reduce | flops 1 | bytes 8 | tf_op jit(solution)/shard_map/psum | solution.py:58
  (306 shorter events, 42.8 us)
Async XLA Ops:
  6.7 20.7 %copy-start.1 = (s32[8,128]{1,0:T(8,128)S(1)}, s32[8,128]{1,0:T(8,128)}, u32[]{:S(2)}) copy-start(s32[8,128]{1,0:T(8,128)} %param.33) | copy-start | bytes 12292
  6.7 20.7 %copy-start.4 = (f32[8,128]{1,0:T(8,128)S(1)}, f32[8,128]{1,0:T(8,128)}, u32[]{:S(2)}) copy-start(f32[8,128]{1,0:T(8,128)} %param.35) | copy-start | bytes 12292
  6.7 41.4 %all-to-all-start = ((f32[64,129,8,2]{1,2,3,0:T(8,128)}), f32[64,129,8,2]{1,2,3,0:T(8,128)S(1)}, u32[]{:S(2)}, u32[]{:S(2)}) async-start(f32[64,129,8,2]{1,2,3,0:T(8,128)} %broadcast_in_dim.137), calls=%async_computation | async-start | bytes 2097152 | tf_op jit(solution)/shard_map/all_to_all | solution.py:49
  22.0 5.5 %collective-permute-start = (f32[129,8,2]{0,1,2:T(8,128)S(1)}, f32[129,8,2]{0,1,2:T(8,128)S(1)}, u32[]{:S(2)}, u32[]{:S(2)}) collective-permute-start(f32[129,8,2]{0,1,2:T(8,128)S(1)} %copy.114), channel_id=1, source_target_pairs={{0,1},{1,2},{2,3},{4,5},{5,6},{6,7},{8,9},{9,10},{10,11},{12,13},{... | collective-permute-start | bytes 24776 | tf_op jit(solution)/shard_map/ppermute | solution.py:35
  25.4 5.6 %collective-permute-start.1 = (f32[129,8,2]{0,1,2:T(8,128)S(1)}, f32[129,8,2]{0,1,2:T(8,128)S(1)}, u32[]{:S(2)}, u32[]{:S(2)}) collective-permute-start(f32[129,8,2]{0,1,2:T(8,128)S(1)} %copy.115), channel_id=1, source_target_pairs={{1,0},{2,1},{3,2},{5,4},{6,5},{7,6},{9,8},{10,9},{11,10},{13,12},{... | collective-permute-start | bytes 24776 | tf_op jit(solution)/shard_map/ppermute | solution.py:36
  48.2 0.7 copy-start.5
  75.1 11.0 %collective-permute-start.2 = (f32[129,2,132]{2,1,0:T(2,128)S(1)}, f32[129,2,132]{2,1,0:T(2,128)S(1)}, u32[]{:S(2)}, u32[]{:S(2)}) collective-permute-start(f32[129,2,132]{2,1,0:T(2,128)S(1)} %get-tuple-element.946), channel_id=1, source_target_pairs={{0,4},{4,8},{8,12},{12,16},{16,20},{20,24},{24,28},{28,32},{32,36}... | collective-permute-start | bytes 408680 | tf_op jit(solution)/shard_map/ppermute | solution.py:35
  75.9 10.3 %collective-permute-start.3 = (f32[129,2,132]{2,1,0:T(2,128)S(1)}, f32[129,2,132]{2,1,0:T(2,128)S(1)}, u32[]{:S(2)}, u32[]{:S(2)}) collective-permute-start(f32[129,2,132]{2,1,0:T(2,128)S(1)} %get-tuple-element.947), channel_id=1, source_target_pairs={{4,0},{8,4},{12,8},{16,12},{20,16},{24,20},{28,24},{32,28},{36,32}... | collective-permute-start | bytes 408680 | tf_op jit(solution)/shard_map/ppermute | solution.py:36
  86.3 0.7 copy-start.3
  91.8 22.8 %all-to-all-start.1 = ((f32[64,3,8,1]{2,3,1,0:T(1,128)}), f32[64,3,8,1]{2,3,1,0:T(1,128)S(1)}, u32[]{:S(2)}, u32[]{:S(2)}) async-start(f32[64,3,8,1]{2,3,1,0:T(1,128)} %broadcast_in_dim.143), calls=%async_computation.1 | async-start | bytes 196608 | tf_op jit(solution)/shard_map/all_to_all | solution.py:49
  103.5 8.3 %collective-permute-start.5 = (f32[3,8,1]{2,1,0:T(8,128)S(1)}, f32[3,8,1]{2,1,0:T(8,128)S(1)}, u32[]{:S(2)}, u32[]{:S(2)}) collective-permute-start(f32[3,8,1]{2,1,0:T(8,128)S(1)} %get-tuple-element.957), channel_id=1, source_target_pairs={{1,0},{2,1},{3,2},{5,4},{6,5},{7,6},{9,8},{10,9},{11,10},{13,12},{... | collective-permute-start | bytes 296 | tf_op jit(solution)/shard_map/ppermute | solution.py:36
  109.2 3.1 collective-permute-start.4
  114.6 4.2 %copy-start.6 = (f32[3]{0:T(128)S(1)}, f32[3]{0:T(128)}, u32[]{:S(2)}) copy-start(f32[3]{0:T(128)} %constant.310.clone) | copy-start | bytes 40
  114.9 18.8 %copy-start.2 = (f32[8,128]{1,0:T(8,128)S(1)}, f32[8,128]{1,0:T(8,128)}, u32[]{:S(2)}) copy-start(f32[8,128]{1,0:T(8,128)} %param.36) | copy-start | bytes 12292
  119.8 6.6 %collective-permute-start.6 = (f32[3,1,130]{2,1,0:T(1,128)S(1)}, f32[3,1,130]{2,1,0:T(1,128)S(1)}, u32[]{:S(2)}, u32[]{:S(2)}) collective-permute-start(f32[3,1,130]{2,1,0:T(1,128)S(1)} %get-tuple-element.954), channel_id=1, source_target_pairs={{4,0},{8,4},{12,8},{16,12},{20,16},{24,20},{28,24},{32,28},{36,32}... | collective-permute-start | bytes 4688 | tf_op jit(solution)/shard_map/ppermute | solution.py:36
  125.5 8.2 %collective-permute-start.7 = (f32[3,1,130]{2,1,0:T(1,128)S(1)}, f32[3,1,130]{2,1,0:T(1,128)S(1)}, u32[]{:S(2)}, u32[]{:S(2)}) collective-permute-start(f32[3,1,130]{2,1,0:T(1,128)S(1)} %get-tuple-element.955), channel_id=1, source_target_pairs={{0,4},{4,8},{8,12},{12,16},{16,20},{20,24},{24,28},{28,32},{32,36}... | collective-permute-start | bytes 4688 | tf_op jit(solution)/shard_map/ppermute | solution.py:35
  135.8 15.8 %all-to-all-start.2 = ((f32[64,1,8,1]{2,3,1,0:T(1,128)}), f32[64,1,8,1]{2,3,1,0:T(1,128)S(1)}, u32[]{:S(2)}, u32[]{:S(2)}) async-start(f32[64,1,8,1]{2,3,1,0:T(1,128)} %broadcast_in_dim.150), calls=%async_computation.2 | async-start | bytes 65536 | tf_op jit(solution)/shard_map/all_to_all | solution.py:49
  140.8 7.2 %collective-permute-start.9 = (f32[1,8,1]{2,1,0:T(8,128)S(1)}, f32[1,8,1]{2,1,0:T(8,128)S(1)}, u32[]{:S(2)}, u32[]{:S(2)}) collective-permute-start(f32[1,8,1]{2,1,0:T(8,128)S(1)} %get-tuple-element.979), channel_id=1, source_target_pairs={{1,0},{2,1},{3,2},{5,4},{6,5},{7,6},{9,8},{10,9},{11,10},{13,12},{... | collective-permute-start | bytes 104 | tf_op jit(solution)/shard_map/ppermute | solution.py:36
  144.7 4.1 %collective-permute-start.8 = (f32[1,8,1]{2,1,0:T(8,128)S(1)}, f32[1,8,1]{2,1,0:T(8,128)S(1)}, u32[]{:S(2)}, u32[]{:S(2)}) collective-permute-start(f32[1,8,1]{2,1,0:T(8,128)S(1)} %get-tuple-element.980), channel_id=1, source_target_pairs={{0,1},{1,2},{2,3},{4,5},{5,6},{6,7},{8,9},{9,10},{10,11},{12,13},{... | collective-permute-start | bytes 104 | tf_op jit(solution)/shard_map/ppermute | solution.py:35
  153.2 6.1 %collective-permute-start.10 = (f32[1,1,130]{2,1,0:T(1,128)S(1)}, f32[1,1,130]{2,1,0:T(1,128)S(1)}, u32[]{:S(2)}, u32[]{:S(2)}) collective-permute-start(f32[1,1,130]{2,1,0:T(1,128)S(1)} %get-tuple-element.967), channel_id=1, source_target_pairs={{4,0},{8,4},{12,8},{16,12},{20,16},{24,20},{28,24},{32,28},{36,32}... | collective-permute-start | bytes 1568 | tf_op jit(solution)/shard_map/ppermute | solution.py:36
  158.5 8.1 %collective-permute-start.11 = (f32[1,1,130]{2,1,0:T(1,128)S(1)}, f32[1,1,130]{2,1,0:T(1,128)S(1)}, u32[]{:S(2)}, u32[]{:S(2)}) collective-permute-start(f32[1,1,130]{2,1,0:T(1,128)S(1)} %get-tuple-element.968), channel_id=1, source_target_pairs={{0,4},{4,8},{8,12},{12,16},{16,20},{20,24},{24,28},{28,32},{32,36}... | collective-permute-start | bytes 1568 | tf_op jit(solution)/shard_map/ppermute | solution.py:35
  168.8 15.8 %all-to-all-start.3 = ((f32[64,1,8,1]{2,3,1,0:T(1,128)}), f32[64,1,8,1]{2,3,1,0:T(1,128)S(1)}, u32[]{:S(2)}, u32[]{:S(2)}) async-start(f32[64,1,8,1]{2,3,1,0:T(1,128)} %broadcast_in_dim.151), calls=%async_computation.3 | async-start | bytes 65536 | tf_op jit(solution)/shard_map/all_to_all | solution.py:49
  173.8 7.2 %collective-permute-start.13 = (f32[1,8,1]{2,1,0:T(8,128)S(1)}, f32[1,8,1]{2,1,0:T(8,128)S(1)}, u32[]{:S(2)}, u32[]{:S(2)}) collective-permute-start(f32[1,8,1]{2,1,0:T(8,128)S(1)} %get-tuple-element.976), channel_id=1, source_target_pairs={{1,0},{2,1},{3,2},{5,4},{6,5},{7,6},{9,8},{10,9},{11,10},{13,12},{... | collective-permute-start | bytes 104 | tf_op jit(solution)/shard_map/ppermute | solution.py:36
  176.0 5.7 %collective-permute-start.12 = (f32[1,8,1]{2,1,0:T(8,128)S(1)}, f32[1,8,1]{2,1,0:T(8,128)S(1)}, u32[]{:S(2)}, u32[]{:S(2)}) collective-permute-start(f32[1,8,1]{2,1,0:T(8,128)S(1)} %get-tuple-element.977), channel_id=1, source_target_pairs={{0,1},{1,2},{2,3},{4,5},{5,6},{6,7},{8,9},{9,10},{10,11},{12,13},{... | collective-permute-start | bytes 104 | tf_op jit(solution)/shard_map/ppermute | solution.py:35
  185.7 6.0 %collective-permute-start.14 = (f32[1,1,130]{2,1,0:T(1,128)S(1)}, f32[1,1,130]{2,1,0:T(1,128)S(1)}, u32[]{:S(2)}, u32[]{:S(2)}) collective-permute-start(f32[1,1,130]{2,1,0:T(1,128)S(1)} %get-tuple-element.965), channel_id=1, source_target_pairs={{4,0},{8,4},{12,8},{16,12},{20,16},{24,20},{28,24},{32,28},{36,32}... | collective-permute-start | bytes 1568 | tf_op jit(solution)/shard_map/ppermute | solution.py:36
  191.0 8.1 %collective-permute-start.15 = (f32[1,1,130]{2,1,0:T(1,128)S(1)}, f32[1,1,130]{2,1,0:T(1,128)S(1)}, u32[]{:S(2)}, u32[]{:S(2)}) collective-permute-start(f32[1,1,130]{2,1,0:T(1,128)S(1)} %get-tuple-element.966), channel_id=1, source_target_pairs={{0,4},{4,8},{8,12},{12,16},{16,20},{20,24},{24,28},{28,32},{32,36}... | collective-permute-start | bytes 1568 | tf_op jit(solution)/shard_map/ppermute | solution.py:35
  201.2 15.8 %all-to-all-start.4 = ((f32[64,1,8,1]{2,3,1,0:T(1,128)}), f32[64,1,8,1]{2,3,1,0:T(1,128)S(1)}, u32[]{:S(2)}, u32[]{:S(2)}) async-start(f32[64,1,8,1]{2,3,1,0:T(1,128)} %broadcast_in_dim.152), calls=%async_computation.4 | async-start | bytes 65536 | tf_op jit(solution)/shard_map/all_to_all | solution.py:49
  206.3 7.2 %collective-permute-start.17 = (f32[1,8,1]{2,1,0:T(8,128)S(1)}, f32[1,8,1]{2,1,0:T(8,128)S(1)}, u32[]{:S(2)}, u32[]{:S(2)}) collective-permute-start(f32[1,8,1]{2,1,0:T(8,128)S(1)} %get-tuple-element.973), channel_id=1, source_target_pairs={{1,0},{2,1},{3,2},{5,4},{6,5},{7,6},{9,8},{10,9},{11,10},{13,12},{... | collective-permute-start | bytes 104 | tf_op jit(solution)/shard_map/ppermute | solution.py:36
  208.2 6.0 %collective-permute-start.16 = (f32[1,8,1]{2,1,0:T(8,128)S(1)}, f32[1,8,1]{2,1,0:T(8,128)S(1)}, u32[]{:S(2)}, u32[]{:S(2)}) collective-permute-start(f32[1,8,1]{2,1,0:T(8,128)S(1)} %get-tuple-element.974), channel_id=1, source_target_pairs={{0,1},{1,2},{2,3},{4,5},{5,6},{6,7},{8,9},{9,10},{10,11},{12,13},{... | collective-permute-start | bytes 104 | tf_op jit(solution)/shard_map/ppermute | solution.py:35
  218.2 6.0 %collective-permute-start.18 = (f32[1,1,130]{2,1,0:T(1,128)S(1)}, f32[1,1,130]{2,1,0:T(1,128)S(1)}, u32[]{:S(2)}, u32[]{:S(2)}) collective-permute-start(f32[1,1,130]{2,1,0:T(1,128)S(1)} %get-tuple-element.963), channel_id=1, source_target_pairs={{4,0},{8,4},{12,8},{16,12},{20,16},{24,20},{28,24},{32,28},{36,32}... | collective-permute-start | bytes 1568 | tf_op jit(solution)/shard_map/ppermute | solution.py:36
  223.5 8.1 %collective-permute-start.19 = (f32[1,1,130]{2,1,0:T(1,128)S(1)}, f32[1,1,130]{2,1,0:T(1,128)S(1)}, u32[]{:S(2)}, u32[]{:S(2)}) collective-permute-start(f32[1,1,130]{2,1,0:T(1,128)S(1)} %get-tuple-element.964), channel_id=1, source_target_pairs={{0,4},{4,8},{8,12},{12,16},{16,20},{20,24},{24,28},{28,32},{32,36}... | collective-permute-start | bytes 1568 | tf_op jit(solution)/shard_map/ppermute | solution.py:35
  233.0 49.9 %copy-start = (f32[1,8,128]{2,1,0:T(8,128)}, f32[1,8,128]{2,1,0:T(8,128)S(1)}, u32[]{:S(2)}) copy-start(f32[1,8,128]{2,1,0:T(8,128)S(1)} %bitcast_add_fusion) | copy-start | bytes 12292
  233.8 16.0 %all-to-all-start.5 = ((f32[64,1,8,1]{2,3,1,0:T(1,128)}), f32[64,1,8,1]{2,3,1,0:T(1,128)S(1)}, u32[]{:S(2)}, u32[]{:S(2)}) async-start(f32[64,1,8,1]{2,3,1,0:T(1,128)} %broadcast_in_dim.153), calls=%async_computation.5 | async-start | bytes 65536 | tf_op jit(solution)/shard_map/all_to_all | solution.py:49
  239.1 7.2 %collective-permute-start.21 = (f32[1,8,1]{2,1,0:T(8,128)S(1)}, f32[1,8,1]{2,1,0:T(8,128)S(1)}, u32[]{:S(2)}, u32[]{:S(2)}) collective-permute-start(f32[1,8,1]{2,1,0:T(8,128)S(1)} %get-tuple-element.970), channel_id=1, source_target_pairs={{1,0},{2,1},{3,2},{5,4},{6,5},{7,6},{9,8},{10,9},{11,10},{13,12},{... | collective-permute-start | bytes 104 | tf_op jit(solution)/shard_map/ppermute | solution.py:36
  241.0 6.0 %collective-permute-start.20 = (f32[1,8,1]{2,1,0:T(8,128)S(1)}, f32[1,8,1]{2,1,0:T(8,128)S(1)}, u32[]{:S(2)}, u32[]{:S(2)}) collective-permute-start(f32[1,8,1]{2,1,0:T(8,128)S(1)} %get-tuple-element.971), channel_id=1, source_target_pairs={{0,1},{1,2},{2,3},{4,5},{5,6},{6,7},{8,9},{9,10},{10,11},{12,13},{... | collective-permute-start | bytes 104 | tf_op jit(solution)/shard_map/ppermute | solution.py:35
  250.9 6.0 %collective-permute-start.22 = (f32[1,1,130]{2,1,0:T(1,128)S(1)}, f32[1,1,130]{2,1,0:T(1,128)S(1)}, u32[]{:S(2)}, u32[]{:S(2)}) collective-permute-start(f32[1,1,130]{2,1,0:T(1,128)S(1)} %get-tuple-element.962), channel_id=1, source_target_pairs={{4,0},{8,4},{12,8},{16,12},{20,16},{24,20},{28,24},{32,28},{36,32}... | collective-permute-start | bytes 1568 | tf_op jit(solution)/shard_map/ppermute | solution.py:36
  256.2 8.1 %collective-permute-start.23 = (f32[1,1,130]{2,1,0:T(1,128)S(1)}, f32[1,1,130]{2,1,0:T(1,128)S(1)}, u32[]{:S(2)}, u32[]{:S(2)}) collective-permute-start(f32[1,1,130]{2,1,0:T(1,128)S(1)} %get-tuple-element.961), channel_id=1, source_target_pairs={{0,4},{4,8},{8,12},{12,16},{16,20},{20,24},{24,28},{28,32},{32,36}... | collective-permute-start | bytes 1568 | tf_op jit(solution)/shard_map/ppermute | solution.py:35
where the time goes:
time: 313 us; the launch traced here: 311 us
  starting transfers between devices  124 us (40%)
  waiting for transfers between devices  77.5 us (25%)
  local copies, waits for them, and re-layouts  47.8 us (15%)
  blocking collectives  40.2 us (13%)
  other arithmetic  17.6 us (6%)
  between operations  3.19 us (1%)
    ppermute x12, starting transfers between devices, extended(): after = lax.ppermute(initial, axis, down)  51.1 us
    all_to_all x6, starting transfers between devices, from_everyone(): return lax.all_to_all(copies, axis, split_axis=0, concat_axis=0, tiled=True)  47.3 us
    ppermute x12, waiting for transfers between devices, extended(): before = lax.ppermute(last, axis, up)  44.1 us
    psum x5, blocking collectives, over_axes(): x = lax.psum(x, axis)  40.2 us
    all_to_all x6, waiting for transfers between devices, from_everyone(): return lax.all_to_all(copies, axis, split_axis=0, concat_axis=0, tiled=True)  27.3 us
    dynamic_update_slice x6, local copies, waits for them, and re-layouts, extend(): lax.dynamic_update_slice_in_dim(widened, northern, meridian_points + widt...  26.3 us
    ppermute x12, starting transfers between devices, extended(): before = lax.ppermute(last, axis, up)  25.2 us
  transfers between devices with their start and end apart: 30, of which 22 were waited for; matrix products, arithmetic and copies ran while one was open for 2% of the time, Pallas kernels for 0%

commit v1 on v0

v1 whole, which is shorter than its diff:
```python
import functools

import jax
import jax.numpy as jnp
from jax import lax
from jax.experimental import pallas as pl
from jax.experimental.pallas import tpu as pltpu
from jax.sharding import PartitionSpec as P

DIFFUSION = 0.15
MIXING = 0.1
EXPANSION = 0.2
CONTRACTION = 0.15
PRESSURE_SCALE = 0.02
CORIOLIS = 0.5
FRICTION = 0.01
DIVERGENCE = 0.3
STORAGE = 0.1
SPECTRUM_LOW = 0.1
SPECTRUM_HIGH = 1.9
GRAVITY = 0.3
EPSILON = 1e-06
ITERS = 4
F32 = jnp.float32

VMEM = pl.BlockSpec(memory_space=pltpu.VMEM)
SMEM = pl.BlockSpec(memory_space=pltpu.SMEM)


def lanes(shape=(8, 128)):
    return lax.broadcasted_iota(jnp.int32, shape, 1)


def subs(shape=(8, 128)):
    return lax.broadcasted_iota(jnp.int32, shape, 0)


def roll_lane(x, shift):
    return pltpu.roll(x, shift % x.shape[1], 1)


def roll_sub(x, shift):
    return pltpu.roll(x, shift % x.shape[0], 0)


def north(x, ghost):
    return roll_lane(jnp.where(lanes() == 0, ghost, x), -1)


def south(x, ghost):
    return roll_lane(jnp.where(lanes() == 127, ghost, x), 1)


def east(x, ghost):
    return roll_sub(jnp.where(subs() == 0, ghost, x), -1)


def west(x, ghost):
    return roll_sub(jnp.where(subs() == 7, ghost, x), 1)


def around(x, lat_ghost, lon_ghost):
    return (east(x, lon_ghost), west(x, lon_ghost), north(x, lat_ghost), south(x, lat_ghost))


def one_of(index, values):
    found = index == values[0]
    for value in values[1:]:
        found = found | (index == value)
    return found


def lat_pack_kernel(t_ref, s_ref, u_ref, v_ref, d_ref, m_ref, z_ref, out_ref):
    levels = t_ref.shape[0]
    lane = lanes()
    is_v = (lane >= 2) & (lane <= 5)
    is_t = (lane == 7) | (lane == 8)
    is_s = (lane == 9) | (lane == 10)
    for k in range(levels):
        x = jnp.where(is_v, roll_lane(v_ref[k], 4), u_ref[k])
        x = jnp.where(is_t, roll_lane(t_ref[k], 8), x)
        out_ref[k] = jnp.where(is_s, roll_lane(s_ref[k], 10), x)
    sea = m_ref[...].astype(F32)
    out_ref[levels] = (d_ref[...] * m_ref[...]).astype(F32)
    out_ref[levels + 1] = sea * z_ref[...]


def lon_pack_kernel(info_ref, t_ref, s_ref, u_ref, v_ref, d_ref, m_ref, z_ref, a_ref, b_ref, g_ref, w_ref, e_ref):
    levels = t_ref.shape[0]
    lane, sub = lanes(), subs()
    is_even, is_top = info_ref[0], info_ref[1]
    from_north = one_of(lane, (0, 1, 4, 5, 8, 10))
    second = one_of(lane, (1, 5))
    flow_sign = jnp.where(lane < 6, -1.0, 1.0).astype(F32)

    @pl.when(is_even == 1)
    def _():
        for k in range(levels + 2):
            g_ref[k] = jnp.where(from_north, a_ref[k], b_ref[k])

    @pl.when((is_even == 0) & (is_top == 0))
    def _():
        for k in range(levels + 2):
            g_ref[k] = jnp.where(from_north, b_ref[k], a_ref[k])

    @pl.when(is_top == 1)
    def _():
        for k in range(levels + 2):
            turned = jnp.concatenate([b_ref[k, 7 - i : 8 - i, :] for i in range(8)], axis=0)
            turned = jnp.where(second, roll_lane(turned, 3), roll_lane(turned, 1))
            if k < levels:
                turned = turned * flow_sign
            g_ref[k] = jnp.where(from_north, turned, a_ref[k])

    for k in range(levels):
        u, v, t, s, g = u_ref[k], v_ref[k], t_ref[k], s_ref[k], g_ref[k]
        v4, t2, s6 = roll_sub(v, 4), roll_sub(t, 2), roll_sub(s, 6)
        x = jnp.where((sub >= 4) & (sub <= 5), v4, u)
        x = jnp.where(sub == 2, t2, x)
        x = jnp.where(sub == 6, s6, x)
        w_ref[k] = jnp.where(sub == 3, roll_sub(g, 3), x)
        x = jnp.where((sub >= 2) & (sub <= 3), v4, u)
        x = jnp.where(sub == 1, t2, x)
        x = jnp.where(sub == 5, s6, x)
        e_ref[k] = jnp.where(sub == 0, roll_sub(g, 1), x)
    depth = (d_ref[...] * m_ref[...]).astype(F32)
    start = m_ref[...].astype(F32) * z_ref[...]
    for k, x in ((levels, depth), (levels + 1, start)):
        w_ref[k] = jnp.where(sub == 3, roll_sub(g_ref[k], 3), x)
        e_ref[k] = jnp.where(sub == 0, roll_sub(g_ref[k], 1), x)


def lon_ghost(e, w, sub):
    return jnp.where(one_of(sub, (0, 1, 4, 5)), e, w)


def corner_ghost(e, w, sub):
    return jnp.where(sub == 0, roll_sub(e, -3), roll_sub(w, -1))


def lap(x, near, masks):
    total = jnp.where(masks[0], near[0] - x, 0.0)
    for i in range(1, 4):
        total = total + jnp.where(masks[i], near[i] - x, 0.0)
    return total


def floats(i):
    return i.astype(F32)


def momentum_kernel(
    info_ref, th_ref, t_ref, s_ref, u_ref, v_ref, d_ref, m_ref, z_ref, f_ref, g_ref, e_ref, w_ref, us_ref, vs_ref, flat_ref, st_ref
):
    levels = t_ref.shape[0]
    lane, sub = lanes(), subs()
    depth = (d_ref[...] * m_ref[...]).astype(F32)
    depth_g = g_ref[levels]
    depth_h = lon_ghost(e_ref[levels], w_ref[levels], sub)
    depth_c = corner_ghost(e_ref[levels], w_ref[levels], sub)
    low_x = [jnp.minimum(depth, n) for n in around(depth, depth_g, depth_h)]
    low_g = [jnp.minimum(depth_g, n) for n in around(depth_g, depth, depth_c)]
    low_h = [jnp.minimum(depth_h, n) for n in around(depth_h, depth_c, depth)]
    lat_index = (lane + info_ref[2] * 128).astype(F32)
    coriolis = CORIOLIS * (2.0 * (lat_index + 0.5) / (128.0 * info_ref[4].astype(F32)) - 1.0)
    zero = jnp.zeros((8, 128), F32)

    def level(k, carry):
        p, p_g, p_h, h, h_g, h_h, tu, tv = carry
        th = th_ref[k]
        kf = floats(k) + 0.5
        u, v, t, s = u_ref[k], v_ref[k], t_ref[k], s_ref[k]
        g, e, w = g_ref[k], e_ref[k], w_ref[k]
        u_h = lon_ghost(e, w, sub)
        v_h = roll_sub(u_h, 4)
        t_h = roll_sub(jnp.where(sub == 2, e, w), -2)
        s_h = roll_sub(jnp.where(sub == 6, e, w), -6)
        u_c = corner_ghost(e, w, sub)
        v_c = roll_lane(u_c, -4)
        v_g, t_g, s_g = roll_lane(g, -4), roll_lane(g, -8), roll_lane(g, -10)
        m_x = [x > kf for x in low_x]
        m_g = [x > kf for x in low_g]
        m_h = [x > kf for x in low_h]
        wet, wet_g, wet_h = depth > kf, depth_g > kf, depth_h > kf
        drags = []
        for x, x_g, x_h, x_c in ((u, g, u_h, u_c), (v, v_g, v_h, v_c)):
            l = lap(x, around(x, x_g, x_h), m_x)
            l_g = lap(x_g, around(x_g, x, x_c), m_g)
            l_h = lap(x_h, around(x_h, x_c, x), m_h)
            drags.append(lap(l, around(l, l_g, l_h), m_x))
        p = p + jnp.where(wet, (CONTRACTION * s - EXPANSION * t) * th, 0.0)
        p_g = p_g + jnp.where(wet_g, (CONTRACTION * s_g - EXPANSION * t_g) * th, 0.0)
        p_h = p_h + jnp.where(wet_h, (CONTRACTION * s_h - EXPANSION * t_h) * th, 0.0)
        p_e, p_w, p_n, p_s = around(p, p_g, p_h)
        grad_x = 0.5 * (jnp.where(m_x[0], p_e - p, 0.0) + jnp.where(m_x[1], p - p_w, 0.0))
        grad_y = 0.5 * (jnp.where(m_x[2], p_n - p, 0.0) + jnp.where(m_x[3], p - p_s, 0.0))
        us = jnp.where(wet, u + coriolis * v - PRESSURE_SCALE * grad_x - FRICTION * drags[0], 0.0)
        vs = jnp.where(wet, v - coriolis * u - PRESSURE_SCALE * grad_y - FRICTION * drags[1], 0.0)
        us_ref[k] = us
        vs_ref[k] = vs
        h = h + jnp.where(wet, th, 0.0)
        h_g = h_g + jnp.where(wet_g, th, 0.0)
        h_h = h_h + jnp.where(wet_h, th, 0.0)
        return (p, p_g, p_h, h, h_g, h_h, tu + th * us, tv + th * vs)

    _, _, _, h, h_g, h_h, tu, tv = lax.fori_loop(0, levels, level, (zero,) * 8)
    sea = m_ref[...].astype(F32)
    start = sea * z_ref[...]
    start_g = g_ref[levels + 1]
    start_h = lon_ghost(e_ref[levels + 1], w_ref[levels + 1], sub)
    diag, coupled = STORAGE + zero, zero
    for n, x in zip(around(h, h_g, h_h), around(start, start_g, start_h)):
        weight = jnp.minimum(h, n) * (1.0 / levels)
        diag = diag + weight
        coupled = coupled + weight * x
    flat_ref[0] = h
    flat_ref[1] = sea * f_ref[...] - (diag * start - coupled)
    flat_ref[2] = tu
    flat_ref[3] = tv
    st_ref[0] = start
    st_ref[1] = start_g
    st_ref[2] = start_h


def tracer_kernel(th_ref, t_ref, s_ref, u_ref, v_ref, d_ref, m_ref, g_ref, e_ref, w_ref, nt_ref, ns_ref):
    levels = t_ref.shape[0]
    lane, sub = lanes(), subs()
    depth = (d_ref[...] * m_ref[...]).astype(F32)
    depth_g = g_ref[levels]
    depth_h = lon_ghost(e_ref[levels], w_ref[levels], sub)
    low = [jnp.minimum(depth, n) for n in around(depth, depth_g, depth_h)]
    zero = jnp.zeros((8, 128), F32)

    def level(k, carry):
        above_t, above_s = carry
        kf = floats(k) + 0.5
        below = jnp.minimum(k + 1, levels - 1)
        th, th_below = th_ref[k], th_ref[below]
        u, v, t, s = u_ref[k], v_ref[k], t_ref[k], s_ref[k]
        g, e, w = g_ref[k], e_ref[k], w_ref[k]
        u_h = lon_ghost(e, w, sub)
        v_g = roll_lane(g, -4)
        wet = depth > kf
        wet_below = (depth > kf + 1.0) & (k + 1 < levels)
        inv_space = 1.0 / jnp.full((8, 128), 0.5 * (th + th_below), F32)
        inv_th = MIXING / jnp.full((8, 128), th, F32)
        flow = [0.25 * x for x in (u + east(u, u_h), west(u, u_h) + u, v + north(v, v_g), south(v, v_g) + v)]
        masks = [x > kf for x in low]
        fluxes = []
        for q, q_g, q_h, q_ref, above, out_ref in (
            (t, roll_lane(g, -8), roll_sub(jnp.where(sub == 2, e, w), -2), t_ref, above_t, nt_ref),
            (s, roll_lane(g, -10), roll_sub(jnp.where(sub == 6, e, w), -6), s_ref, above_s, ns_ref),
        ):
            q_e, q_w, q_n, q_s = around(q, q_g, q_h)
            f_e = jnp.where(masks[0], flow[0] * (q + q_e) - DIFFUSION * (q_e - q), 0.0)
            f_w = jnp.where(masks[1], flow[1] * (q_w + q) - DIFFUSION * (q - q_w), 0.0)
            f_n = jnp.where(masks[2], flow[2] * (q + q_n) - DIFFUSION * (q_n - q), 0.0)
            f_s = jnp.where(masks[3], flow[3] * (q_s + q) - DIFFUSION * (q - q_s), 0.0)
            vflux = jnp.where(wet_below, (q_ref[below] - q) * inv_space, 0.0)
            vertical = (vflux - above) * inv_th
            out_ref[k] = jnp.where(wet, q + (f_w - f_e + f_s - f_n) + vertical, 0.0)
            fluxes.append(vflux)
        return tuple(fluxes)

    lax.fori_loop(0, levels, level, (zero, zero))


def turn(x, cells):
    lane = lanes()
    x = jnp.concatenate([x[7 - i : 8 - i] for i in range(8)], axis=0)
    out = roll_lane(x, 1)
    for j in range(1, cells):
        out = jnp.where(lane == j, roll_lane(x, 1 + 2 * j), out)
    return out


def chunk_kernel(info_ref, flat_ref, a_ref, b_ref, out_ref):
    lane, sub = lanes(), subs()
    even = jnp.full((8, 128), info_ref[0], jnp.int32) == 1
    top = jnp.full((8, 128), info_ref[1], jnp.int32) == 1
    own, ghost = [], []
    for f in range(4):
        a, b = a_ref[f], b_ref[f]
        turned = turn(b, 5)
        if f >= 2:
            turned = -turned
        n = jnp.where(even, a, jnp.where(top, turned, b))
        s = jnp.where(even, b, a)
        own.append(flat_ref[f])
        ghost.append(jnp.where(lane < 64, n, s))
    rights = []
    for x, other in ((own, ghost), (ghost, own)):
        h, base, tu, tv = x
        tu_e = jnp.where(sub == 7, 0.0, roll_sub(tu, -1))
        tu_w = jnp.where(sub == 0, 0.0, roll_sub(tu, 1))
        tv_n, tv_s = north(tv, other[3]), south(tv, other[3])
        rights.append(base - jnp.where(h > 0.0, (0.5 * DIVERGENCE) * ((tu_e - tu_w) + (tv_n - tv_s)), 0.0))
    halo = jnp.where(lane < 16, roll_lane(ghost[0], 8), jnp.where(lane < 32, roll_lane(rights[1], 24), roll_lane(ghost[2], 40)))
    halo = jnp.where(lane < 64, halo, roll_lane(roll_sub(halo, 4), 64))
    halo = jnp.where(sub < 4, halo, jnp.where(sub == 4, roll_sub(own[2], 4), roll_sub(own[2], -2)))
    out_ref[0] = own[0]
    out_ref[1] = rights[0]
    out_ref[2] = halo


def slab_kernel(info_ref, in_ref, st_ref, sum_ref, surf_ref, slope_ref, h_s, we_s, wn_s, ws_s, dg_s, fac_s, inv_s, r_s, d_s, z_s):
    blocks = in_ref.shape[0] // 24
    inv_levels = info_ref[5].astype(F32)
    inv_levels = 1.0 / jnp.full((8, 128), inv_levels, F32)[0:1, 0:1]

    def rows(i):
        return in_ref[pl.ds(i, blocks, stride=24), :]

    tu = [None] * 8
    for p in range(8):
        packed = rows(16 + p % 4)
        at = 64 * (p // 4)
        h_s[p, :, 0:128] = rows(p)
        h_s[p, :, 128:256] = roll_lane(packed, -8 - at)
        r_s[p, :, 0:128] = rows(8 + p)
        r_s[p, :, 128:256] = roll_lane(packed, -24 - at)
        if p in (0, 7):
            tu[p] = jnp.concatenate([rows(20 if p == 0 else 21), roll_lane(packed, -40 - at)], axis=1)
    r_s[0] = r_s[0] + jnp.where(h_s[0] > 0.0, (0.5 * DIVERGENCE) * roll_sub(tu[7], 1), 0.0)
    r_s[7] = r_s[7] - jnp.where(h_s[7] > 0.0, (0.5 * DIVERGENCE) * roll_sub(tu[0], -1), 0.0)
    for p in range(8):
        h = h_s[p]
        h_e = h_s[p + 1] if p < 7 else roll_sub(h_s[0], -1)
        we_s[p] = jnp.minimum(h, h_e) * inv_levels
        wn = jnp.minimum(h, roll_lane(h, -1)) * inv_levels
        wn_s[p] = wn
        ws_s[p] = roll_lane(wn, 1)
    for p in range(8):
        w_w = we_s[p - 1] if p > 0 else roll_sub(we_s[7], 1)
        diag = STORAGE + we_s[p] + w_w + wn_s[p] + ws_s[p]
        dg_s[p] = diag
        if p > 0:
            diag = diag + we_s[p - 1] * fac_s[p - 1]
        inv = 1.0 / diag
        inv_s[p] = inv
        fac_s[p] = -we_s[p] * inv

    mid = 0.5 * (SPECTRUM_HIGH + SPECTRUM_LOW)
    half = 0.5 * (SPECTRUM_HIGH - SPECTRUM_LOW)
    ratio = mid / half

    def solve(scale_old, scale_new, first):
        y = [None] * 8
        y[0] = r_s[0] * inv_s[0]
        for p in range(1, 8):
            y[p] = (r_s[p] + we_s[p - 1] * y[p - 1]) * inv_s[p]
        x = None
        for p in range(7, -1, -1):
            x = y[p] if x is None else y[p] - fac_s[p] * x
            if first:
                d = x * scale_new
                z_s[p] = d
            else:
                d = scale_old * d_s[p] + scale_new * x
                z_s[p] = z_s[p] + d
            d_s[p] = d

    def subtract():
        for p in range(8):
            d = d_s[p]
            d_e = d_s[p + 1] if p < 7 else roll_sub(d_s[0], -1)
            d_w = d_s[p - 1] if p > 0 else roll_sub(d_s[7], 1)
            w_w = we_s[p - 1] if p > 0 else roll_sub(we_s[7], 1)
            coupled = we_s[p] * d_e + w_w * d_w + wn_s[p] * roll_lane(d, -1) + ws_s[p] * roll_lane(d, 1)
            r_s[p] = r_s[p] - (dg_s[p] * d - coupled)

    solve(0.0, 1.0 / mid, True)
    rho = 1.0 / ratio
    for _ in range(ITERS - 1):
        subtract()
        rho_next = 1.0 / (2.0 * ratio - rho)
        solve(rho_next * rho, 2.0 * rho_next / half, False)
        rho = rho_next
    subtract()
    total = jnp.zeros((blocks, 128), F32)
    for p in range(8):
        x = r_s[p, :, 0:128]
        total = total + x * x
    sum_ref[...] = jnp.sum(jnp.sum(total, axis=0, keepdims=True), axis=1, keepdims=True) + jnp.zeros((1, 128), F32)

    here = info_ref[3]
    right = jnp.where(here + 1 == blocks, 0, here + 1)
    left = jnp.where(here == 0, blocks - 1, here - 1)
    both = jnp.concatenate([z_s[p, pl.ds(here, 1), :] for p in range(8)], axis=0)
    x, x_g = both[:, 0:128], both[:, 128:256]
    sub = subs()
    x_e = jnp.broadcast_to(z_s[0, pl.ds(right, 1), :][:, 0:128], (8, 128))
    x_w = jnp.broadcast_to(z_s[7, pl.ds(left, 1), :][:, 0:128], (8, 128))
    x_h = jnp.where(sub < 4, x_e, x_w)
    x, x_g, x_h = x + st_ref[0], x_g + st_ref[1], x_h + st_ref[2]
    e, w, n, s = around(x, x_g, x_h)
    surf_ref[...] = x
    slope_ref[0] = (0.5 * GRAVITY) * (e - w)
    slope_ref[1] = (0.5 * GRAVITY) * (n - s)


def velocity_kernel(us_ref, vs_ref, d_ref, m_ref, slope_ref, nu_ref, nv_ref):
    depth = (d_ref[...] * m_ref[...]).astype(F32)
    slope_x, slope_y = slope_ref[0], slope_ref[1]
    for k in range(us_ref.shape[0]):
        wet = depth > k + 0.5
        nu_ref[k] = jnp.where(wet, us_ref[k] - slope_x, 0.0)
        nv_ref[k] = jnp.where(wet, vs_ref[k] - slope_y, 0.0)


def call(kernel, name, outs, in_specs, scratch=()):
    return pl.pallas_call(
        kernel,
        name=name,
        out_shape=outs,
        in_specs=in_specs,
        out_specs=jax.tree.map(lambda _: VMEM, outs),
        scratch_shapes=list(scratch),
        compiler_params=pltpu.CompilerParams(vmem_limit_bytes=48 << 20),
    )


def per_device(lon_size, lat_size, temp, salt, u, v, strata, sea, thickness, elevation, drive):
    levels = temp.shape[0]
    lon, lat = lax.axis_index("lon"), lax.axis_index("lat")
    top = lat_size - 1
    info = jnp.stack(
        [1 - lat % 2, (lat == top).astype(jnp.int32), lat, lon, jnp.int32(lat_size), jnp.int32(levels)]
    ).astype(jnp.int32)
    pairs_a = [(i, i ^ 1) for i in range(lat_size)]
    pairs_b = []
    for a in range(lon_size):
        for i in range(1, top, 2):
            pairs_b += [(a * lat_size + i, a * lat_size + i + 1), (a * lat_size + i + 1, a * lat_size + i)]
        pairs_b.append((a * lat_size + top, (lon_size - 1 - a) * lat_size + top))
    up = [(i, (i + 1) % lon_size) for i in range(lon_size)]
    down = [(j, i) for i, j in up]

    def lat_swap(x):
        return lax.ppermute(x, "lat", pairs_a), lax.ppermute(x, ("lon", "lat"), pairs_b)

    field = jax.ShapeDtypeStruct((levels, 8, 128), F32)
    message = jax.ShapeDtypeStruct((levels + 2, 8, 128), F32)

    def tiles(n):
        return jax.ShapeDtypeStruct((n, 8, 128), F32)

    packed = call(lat_pack_kernel, "lat_pack", message, [VMEM] * 7)(temp, salt, u, v, strata, sea, elevation)
    got_a, got_b = lat_swap(packed)
    ghost, westward, eastward = call(lon_pack_kernel, "lon_pack", (message,) * 3, [SMEM] + [VMEM] * 9)(
        info, temp, salt, u, v, strata, sea, elevation, got_a, got_b
    )
    from_east = lax.ppermute(westward, "lon", down)
    from_west = lax.ppermute(eastward, "lon", up)
    u_star, v_star, flat, start = call(
        momentum_kernel, "momentum", (field, field, tiles(4), tiles(3)), [SMEM, SMEM] + [VMEM] * 11
    )(info, thickness, temp, salt, u, v, strata, sea, elevation, drive, ghost, from_east, from_west)
    flat_a, flat_b = lat_swap(flat)
    chunk = call(chunk_kernel, "chunk", tiles(3), [SMEM] + [VMEM] * 3)(info, flat, flat_a, flat_b)
    copies = jnp.broadcast_to(chunk[None], (lon_size, 3, 8, 128))
    ring = lax.all_to_all(copies, "lon", 0, 0, tiled=True).reshape(lon_size * 24, 128)
    new_temp, new_salt = call(tracer_kernel, "tracers", (field, field), [SMEM] + [VMEM] * 9)(
        thickness, temp, salt, u, v, strata, sea, ghost, from_east, from_west
    )
    total, surface, slope = call(
        slab_kernel,
        "slab",
        (jax.ShapeDtypeStruct((1, 128), F32), jax.ShapeDtypeStruct((8, 128), F32), tiles(2)),
        [SMEM, VMEM, VMEM],
        [pltpu.VMEM((8, lon_size, 256), F32)] * 10,
    )(info, ring, start)
    total = total + lax.ppermute(total, "lat", pairs_a)
    gap = 2
    while gap < lat_size:
        total = total + lax.ppermute(total, "lat", [(i, i ^ gap) for i in range(lat_size)])
        gap *= 2
    cells = lon_size * 8 * lat_size * 128
    rms = jnp.sqrt(total[0, 0] / cells + EPSILON)
    new_u, new_v = call(velocity_kernel, "velocity", (field, field), [VMEM] * 5)(u_star, v_star, strata, sea, slope)
    return (new_temp, new_salt, new_u, new_v, surface, rms)


def solution(mesh):
    cube, flat = P(None, "lon", "lat"), P("lon", "lat")
    return jax.shard_map(
        functools.partial(per_device, mesh.shape["lon"], mesh.shape["lat"]),
        mesh=mesh,
        in_specs=(cube, cube, cube, cube, flat, flat, P(), flat, flat),
        out_specs=(cube, cube, cube, cube, flat, P()),
        check_vma=False,
    )
```

time: 313 us -> 102 us (0.33)
  starting transfers between devices: 124 us -> 31 us
  waiting for transfers between devices: 77.5 us -> 15.4 us
  local copies, waits for them, and re-layouts: 47.8 us -> 5.85 us
  Pallas kernels: 0 us -> 20.1 us
  other arithmetic: 17.6 us -> 0.01 us
  blocking collectives: 40.2 us -> 26.9 us
    all_to_all x6 -> x0, starting transfers between devices: 47.3 us -> none  [from_everyone(): return lax.all_to_all(copies, axis, split_axis=0, concat_axis=0, tiled=True)]
    ppermute x24 -> x8, starting transfers between devices: 76.3 us -> 31 us  [the longest x1 10.9 us: per_device(): lax.ppermute(total, 'lat', [(i, i ^ gap) for i in range(lat_size)])]
    psum x5 -> x0, blocking collectives: 40.2 us -> none  [over_axes(): x = lax.psum(x, axis)]
    ppermute x24 -> x8, waiting for transfers between devices: 50.2 us -> 15.4 us  [the longest x1 7.91 us: per_device(): from_west = lax.ppermute(eastward, 'lon', up)]
    dynamic_update_slice x86 -> x0, local copies, waits for them, and re-layouts: 29.2 us -> none  [the longest x6 26.3 us: extend(): lax.dynamic_update_slice_in_dim(widened, northern, meridian_points + widt...]
    all_to_all x6 -> x0, waiting for transfers between devices: 27.3 us -> none  [from_everyone(): return lax.all_to_all(copies, axis, split_axis=0, concat_axis=0, tiled=True)]
    all_to_all x0 -> x1, blocking collectives: none -> 26.9 us  [per_device(): lax.all_to_all(copies, 'lon', 0, 0, tiled=True).reshape(lon_size * 24, 128)]
    pallas_call x0 -> x7, Pallas kernels: none -> 20.1 us  [the longest x1 7.71 us: per_device(): call(momentum_kernel, 'momentum', (field, field, tiles(4), tiles(3)), [SM...]
  transfers between devices with their start and end apart: 30 -> 8, of which waited for: 22 -> 5; matrix products, arithmetic and copies ran while one was open for 2% -> 0% of each run, Pallas kernels for 0% -> 7%
where the time goes in v1:
time: 102 us; the launch traced here: 101 us
  starting transfers between devices  31 us (30%)
  blocking collectives  26.9 us (26%)
  Pallas kernels  20.1 us (20%)
  waiting for transfers between devices  15.4 us (15%)
  local copies, waits for them, and re-layouts  5.85 us (6%)
  between operations  2.02 us (2%)
    all_to_all x1, blocking collectives, per_device(): lax.all_to_all(copies, 'lon', 0, 0, tiled=True).reshape(lon_size * 24, 128)  26.9 us
    ppermute x1, starting transfers between devices, per_device(): lax.ppermute(total, 'lat', [(i, i ^ gap) for i in range(lat_size)])  10.9 us
    ppermute x1, starting transfers between devices, per_device(): from_east = lax.ppermute(westward, 'lon', down)  10.4 us
    ppermute x2, starting transfers between devices, lat_swap(): lax.ppermute(x, ('lon', 'lat'), pairs_b)  8.1 us
    ppermute x1, waiting for transfers between devices, per_device(): from_west = lax.ppermute(eastward, 'lon', up)  7.91 us
    pallas_call x1, Pallas kernels, per_device(): call(momentum_kernel, 'momentum', (field, field, tiles(4), tiles(3)), [SM...  7.71 us
    pallas_call x1, Pallas kernels, per_device(): call(tracer_kernel, 'tracers', (field, field), [SMEM] + [VMEM] * 9)  6.08 us
    unnamed x32, local copies, waits for them, and re-layouts  5.71 us
  transfers between devices with their start and end apart: 8, of which 5 were waited for; matrix products, arithmetic and copies ran while one was open for 0% of the time, Pallas kernels for 7%

profile of v1, /device:TPU:1, one launch (start us, length us, event | category | flops | bytes accessed | tf_op | source)
XLA Modules:
  0.0 101.3 jit_solution(15835345405179093453)
XLA Ops:
  0.6 0.0 copy-start
  0.6 0.9 copy-done
  1.5 0.0 copy-start.2
  1.5 0.9 copy-done.2
  2.4 0.9 copy-done.4
  3.3 0.9 copy-done.6
  4.3 0.7 copy-done.8
  4.9 0.7 copy-done.10
  5.6 0.7 copy-done.12
  6.3 0.2 lat_pack.1
  6.5 4.7 %collective-permute-start.1 = (f32[34,8,128]{2,1,0:T(8,128)S(1)}, f32[34,8,128]{2,1,0:T(8,128)S(1)}, u32[]{:S(2)}, u32[]{:S(2)}) collective-permute-start(f32[34,8,128]{2,1,0:T(8,128)S(1)} %lat_pack.1), channel_id=1, source_target_pairs={{1,2},{2,1},{3,255},{5,6},{6,5},{7,251},{9,10},{10,9},{11,247},{13... | collective-permute-start | bytes 417800 | tf_op jit(solution)/shard_map/ppermute | solution.py:440
  11.2 0.1 collective-permute-start
  11.3 0.0 copy-start.13
  11.4 0.0 copy-start.11
  11.4 0.0 copy-start.9
  11.4 0.1 stack.23.info_ref
  11.5 2.5 %collective-permute-done.1.b_ref = f32[34,8,128]{2,1,0:T(8,128)S(1)} collective-permute-done((f32[34,8,128]{2,1,0:T(8,128)S(1)}, f32[34,8,128]{2,1,0:T(8,128)S(1)}, u32[]{:S(2)}, u32[]{:S(2)}) %collective-permute-start.1) | collective-permute-done | bytes 139296 | tf_op jit(solution)/shard_map/ppermute | solution.py:440
  14.0 0.0 collective-permute-done.a_ref
  14.0 0.0 copy-done.1
  14.0 0.0 copy-done.3
  14.0 0.0 copy-done.5
  14.0 0.0 copy-done.7
  14.0 0.0 copy-done.13
  14.0 0.0 copy-done.11
  14.0 0.0 copy-done.9
  14.0 0.6 lon_pack.1
  14.7 0.0 copy-start.14
  14.7 10.4 %collective-permute-start.2 = (f32[34,8,128]{2,1,0:T(8,128)S(1)}, f32[34,8,128]{2,1,0:T(8,128)S(1)}, u32[]{:S(2)}, u32[]{:S(2)}) collective-permute-start(f32[34,8,128]{2,1,0:T(8,128)S(1)} %get-tuple-element.21), channel_id=1, source_target_pairs={{4,0},{8,4},{12,8},{16,12},{20,16},{24,20},{28,24},{32,28},{36,32}... | collective-permute-start | bytes 417800 | tf_op jit(solution)/shard_map/ppermute | solution.py:453
  25.0 0.0 collective-permute-start.3
  25.0 2.6 %collective-permute-done.2.e_ref = f32[34,8,128]{2,1,0:T(8,128)S(1)} collective-permute-done((f32[34,8,128]{2,1,0:T(8,128)S(1)}, f32[34,8,128]{2,1,0:T(8,128)S(1)}, u32[]{:S(2)}, u32[]{:S(2)}) %collective-permute-start.2) | collective-permute-done | bytes 139296 | tf_op jit(solution)/shard_map/ppermute | solution.py:453
  27.7 7.9 %collective-permute-done.3.w_ref = f32[34,8,128]{2,1,0:T(8,128)S(1)} collective-permute-done((f32[34,8,128]{2,1,0:T(8,128)S(1)}, f32[34,8,128]{2,1,0:T(8,128)S(1)}, u32[]{:S(2)}, u32[]{:S(2)}) %collective-permute-start.3) | collective-permute-done | bytes 139296 | tf_op jit(solution)/shard_map/ppermute | solution.py:454
  35.6 0.0 copy-done.14
  35.6 0.0 copy-done.15
  35.6 7.7 %momentum.1 = (f32[32,8,128]{2,1,0:T(8,128)S(1)}, f32[32,8,128]{2,1,0:T(8,128)S(1)}, f32[4,8,128]{2,1,0:T(8,128)S(1)}, f32[3,8,128]{2,1,0:T(8,128)S(1)}) custom-call(s32[6]{0:T(128)S(1)} %stack.23.info_ref, f32[32]{0:T(128)S(1)} %copy-done.15, f32[32,8,128]{2,1,0:T(8,128)S(1)} %copy-done.1, f32[32,8,128]{2,1,0:T(8,128)S(1)} %copy-done.3, ...), custom_call_target="tpu_custom_call" | custom-call | tf_op jit(solution)/shard_map/momentum/pallas_call | solution.py:455
  43.3 3.4 %collective-permute-start.5 = (f32[4,8,128]{2,1,0:T(8,128)S(1)}, f32[4,8,128]{2,1,0:T(8,128)S(1)}, u32[]{:S(2)}, u32[]{:S(2)}) collective-permute-start(f32[4,8,128]{2,1,0:T(8,128)S(1)} %get-tuple-element.27.flat_ref), channel_id=1, source_target_pairs={{1,2},{2,1},{3,255},{5,6},{6,5},{7,251},{9,10},{10,9},{11,247},{13... | collective-permute-start | bytes 49160 | tf_op jit(solution)/shard_map/ppermute | solution.py:440
  46.7 0.1 collective-permute-start.4
  46.8 1.6 %collective-permute-done.5.b_ref = f32[4,8,128]{2,1,0:T(8,128)S(1)} collective-permute-done((f32[4,8,128]{2,1,0:T(8,128)S(1)}, f32[4,8,128]{2,1,0:T(8,128)S(1)}, u32[]{:S(2)}, u32[]{:S(2)}) %collective-permute-start.5) | collective-permute-done | bytes 16416 | tf_op jit(solution)/shard_map/ppermute | solution.py:440
  48.3 0.0 collective-permute-done.4.a_ref
  48.3 0.8 chunk.1
  49.2 0.1 broadcast_in_dim.2
  49.2 26.9 %all_to_all.5 = f32[64,3,8,128]{3,2,1,0:T(8,128)S(1)} all-to-all(f32[64,3,8,128]{3,2,1,0:T(8,128)S(1)} %broadcast_in_dim.2), channel_id=1, replica_groups=mesh['lon'=64,'lat'=4] {'lon'}, dimensions={0} | all-to-all | bytes 1572864 | tf_op jit(solution)/shard_map/all_to_all | solution.py:461
  76.1 4.0 %slab.1 = (f32[1,128]{1,0:T(1,128)S(1)}, f32[8,128]{1,0:T(8,128)}, f32[2,8,128]{2,1,0:T(8,128)S(1)}) custom-call(s32[6]{0:T(128)S(1)} %stack.23.info_ref, f32[1536,128]{1,0:T(8,128)S(1)} %bitcast.7, f32[3,8,128]{2,1,0:T(8,128)S(1)} %get-tuple-element.28.st_ref), custom_call_target="tpu_custom_call" | custom-call | tf_op jit(solution)/shard_map/slab/pallas_call | solution.py:465
  80.1 1.4 %collective-permute-start.6 = (f32[1,128]{1,0:T(1,128)S(1)}, f32[1,128]{1,0:T(1,128)S(1)}, u32[]{:S(2)}, u32[]{:S(2)}) collective-permute-start(f32[1,128]{1,0:T(1,128)S(1)} %get-tuple-element.33), channel_id=1, source_target_pairs={{0,1},{1,0},{2,3},{3,2},{4,5},{5,4},{6,7},{7,6},{8,9},{9,8},{10,11... | collective-permute-start | bytes 1544 | tf_op jit(solution)/shard_map/ppermute | solution.py:472
  81.5 0.8 collective-permute-done.6
  82.4 10.9 %collective-permute-start.7 = (f32[1,128]{1,0:T(1,128)S(1)}, f32[1,128]{1,0:T(1,128)S(1)}, u32[]{:S(2)}, u32[]{:S(2)}) collective-permute-start(f32[1,128]{1,0:T(1,128)S(1)} %add.15), channel_id=1, source_target_pairs={{0,2},{1,3},{2,0},{3,1},{4,6},{5,7},{6,4},{7,5},{8,10},{9,11},{10,... | collective-permute-start | bytes 1544 | tf_op jit(solution)/shard_map/ppermute | solution.py:475
  93.3 6.1 %tracers.1 = (f32[32,8,128]{2,1,0:T(8,128)}, f32[32,8,128]{2,1,0:T(8,128)}) custom-call(f32[32]{0:T(128)S(1)} %copy-done.15, f32[32,8,128]{2,1,0:T(8,128)S(1)} %copy-done.1, f32[32,8,128]{2,1,0:T(8,128)S(1)} %copy-done.3, f32[32,8,128]{2,1,0:T(8,128)S(1)} %copy-done.5, f32[32,8,128]{2,1,0:T(8,128)S(1)} %copy-done.7, s32[8,128]{1,0:T(8,128)S(1)} %copy-done.9, ...), custom_call_target="tpu_custom_call" | custom-call | tf_op jit(solution)/shard_map/tracers/pallas_call | solution.py:462
  99.3 0.7 velocity.1
  100.1 0.0 collective-permute-done.7
  (12 shorter events, 0.0 us)
Async XLA Ops:
  0.6 0.9 copy-start
  1.5 0.9 copy-start.2
  2.4 0.9 copy-start.4
  3.3 0.9 copy-start.6
  4.3 0.7 copy-start.8
  4.9 0.7 copy-start.10
  5.6 0.7 copy-start.12
  6.3 7.7 %copy-start.1 = (f32[32,8,128]{2,1,0:T(8,128)S(1)}, f32[32,8,128]{2,1,0:T(8,128)}, u32[]{:S(2)}) copy-start(f32[32,8,128]{2,1,0:T(8,128)} %t_ref.7) | copy-start | bytes 393220
  6.3 7.7 %copy-start.3 = (f32[32,8,128]{2,1,0:T(8,128)S(1)}, f32[32,8,128]{2,1,0:T(8,128)}, u32[]{:S(2)}) copy-start(f32[32,8,128]{2,1,0:T(8,128)} %s_ref.7) | copy-start | bytes 393220
  6.3 7.7 %copy-start.5 = (f32[32,8,128]{2,1,0:T(8,128)S(1)}, f32[32,8,128]{2,1,0:T(8,128)}, u32[]{:S(2)}) copy-start(f32[32,8,128]{2,1,0:T(8,128)} %u_ref.7) | copy-start | bytes 393220
  6.3 7.7 %copy-start.7 = (f32[32,8,128]{2,1,0:T(8,128)S(1)}, f32[32,8,128]{2,1,0:T(8,128)}, u32[]{:S(2)}) copy-start(f32[32,8,128]{2,1,0:T(8,128)} %v_ref.7) | copy-start | bytes 393220
  6.5 7.5 %collective-permute-start.1 = (f32[34,8,128]{2,1,0:T(8,128)S(1)}, f32[34,8,128]{2,1,0:T(8,128)S(1)}, u32[]{:S(2)}, u32[]{:S(2)}) collective-permute-start(f32[34,8,128]{2,1,0:T(8,128)S(1)} %lat_pack.1), channel_id=1, source_target_pairs={{1,2},{2,1},{3,255},{5,6},{6,5},{7,251},{9,10},{10,9},{11,247},{13... | collective-permute-start | bytes 417800 | tf_op jit(solution)/shard_map/ppermute | solution.py:440
  11.2 2.7 %collective-permute-start = (f32[34,8,128]{2,1,0:T(8,128)S(1)}, f32[34,8,128]{2,1,0:T(8,128)S(1)}, u32[]{:S(2)}, u32[]{:S(2)}) collective-permute-start(f32[34,8,128]{2,1,0:T(8,128)S(1)} %lat_pack.1), channel_id=1, source_target_pairs={{0,1},{1,0},{2,3},{3,2},{4,5},{5,4},{6,7},{7,6},{8,9},{9,8},{10,11... | collective-permute-start | bytes 417800 | tf_op jit(solution)/shard_map/ppermute | solution.py:440
  11.3 2.6 %copy-start.13 = (f32[8,128]{1,0:T(8,128)S(1)}, f32[8,128]{1,0:T(8,128)}, u32[]{:S(2)}) copy-start(f32[8,128]{1,0:T(8,128)} %z_ref.5) | copy-start | bytes 12292
  11.4 2.6 %copy-start.11 = (s32[8,128]{1,0:T(8,128)S(1)}, s32[8,128]{1,0:T(8,128)}, u32[]{:S(2)}) copy-start(s32[8,128]{1,0:T(8,128)} %m_ref.9) | copy-start | bytes 12292
  11.4 2.6 %copy-start.9 = (s32[8,128]{1,0:T(8,128)S(1)}, s32[8,128]{1,0:T(8,128)}, u32[]{:S(2)}) copy-start(s32[8,128]{1,0:T(8,128)} %d_ref.9) | copy-start | bytes 12292
  14.7 20.9 %copy-start.14 = (f32[8,128]{1,0:T(8,128)S(1)}, f32[8,128]{1,0:T(8,128)}, u32[]{:S(2)}) copy-start(f32[8,128]{1,0:T(8,128)} %f_ref.1) | copy-start | bytes 12292
  14.7 13.0 %collective-permute-start.2 = (f32[34,8,128]{2,1,0:T(8,128)S(1)}, f32[34,8,128]{2,1,0:T(8,128)S(1)}, u32[]{:S(2)}, u32[]{:S(2)}) collective-permute-start(f32[34,8,128]{2,1,0:T(8,128)S(1)} %get-tuple-element.21), channel_id=1, source_target_pairs={{4,0},{8,4},{12,8},{16,12},{20,16},{24,20},{28,24},{32,28},{36,32}... | collective-permute-start | bytes 417800 | tf_op jit(solution)/shard_map/ppermute | solution.py:453
  25.0 10.6 %copy-start.15 = (f32[32]{0:T(128)S(1)}, f32[32]{0:T(128)}, u32[]{:S(2)}) copy-start(f32[32]{0:T(128)} %th_ref.3) | copy-start | bytes 388
  25.0 10.5 %collective-permute-start.3 = (f32[34,8,128]{2,1,0:T(8,128)S(1)}, f32[34,8,128]{2,1,0:T(8,128)S(1)}, u32[]{:S(2)}, u32[]{:S(2)}) collective-permute-start(f32[34,8,128]{2,1,0:T(8,128)S(1)} %get-tuple-element.22), channel_id=1, source_target_pairs={{0,4},{4,8},{8,12},{12,16},{16,20},{20,24},{24,28},{28,32},{32,36}... | collective-permute-start | bytes 417800 | tf_op jit(solution)/shard_map/ppermute | solution.py:454
  43.3 5.1 %collective-permute-start.5 = (f32[4,8,128]{2,1,0:T(8,128)S(1)}, f32[4,8,128]{2,1,0:T(8,128)S(1)}, u32[]{:S(2)}, u32[]{:S(2)}) collective-permute-start(f32[4,8,128]{2,1,0:T(8,128)S(1)} %get-tuple-element.27.flat_ref), channel_id=1, source_target_pairs={{1,2},{2,1},{3,255},{5,6},{6,5},{7,251},{9,10},{10,9},{11,247},{13... | collective-permute-start | bytes 49160 | tf_op jit(solution)/shard_map/ppermute | solution.py:440
  46.7 1.7 %collective-permute-start.4 = (f32[4,8,128]{2,1,0:T(8,128)S(1)}, f32[4,8,128]{2,1,0:T(8,128)S(1)}, u32[]{:S(2)}, u32[]{:S(2)}) collective-permute-start(f32[4,8,128]{2,1,0:T(8,128)S(1)} %get-tuple-element.27.flat_ref), channel_id=1, source_target_pairs={{0,1},{1,0},{2,3},{3,2},{4,5},{5,4},{6,7},{7,6},{8,9},{9,8},{10,11... | collective-permute-start | bytes 49160 | tf_op jit(solution)/shard_map/ppermute | solution.py:440
  80.1 2.2 %collective-permute-start.6 = (f32[1,128]{1,0:T(1,128)S(1)}, f32[1,128]{1,0:T(1,128)S(1)}, u32[]{:S(2)}, u32[]{:S(2)}) collective-permute-start(f32[1,128]{1,0:T(1,128)S(1)} %get-tuple-element.33), channel_id=1, source_target_pairs={{0,1},{1,0},{2,3},{3,2},{4,5},{5,4},{6,7},{7,6},{8,9},{9,8},{10,11... | collective-permute-start | bytes 1544 | tf_op jit(solution)/shard_map/ppermute | solution.py:472
  82.4 17.7 %collective-permute-start.7 = (f32[1,128]{1,0:T(1,128)S(1)}, f32[1,128]{1,0:T(1,128)S(1)}, u32[]{:S(2)}, u32[]{:S(2)}) collective-permute-start(f32[1,128]{1,0:T(1,128)S(1)} %add.15), channel_id=1, source_target_pairs={{0,2},{1,3},{2,0},{3,1},{4,6},{5,7},{6,4},{7,5},{8,10},{9,11},{10,... | collective-permute-start | bytes 1544 | tf_op jit(solution)/shard_map/ppermute | solution.py:475

commit v2 on v1

v2 whole, which is shorter than its diff:
```python
import functools

import jax
import jax.numpy as jnp
from jax import lax
from jax.experimental import pallas as pl
from jax.experimental.pallas import tpu as pltpu
from jax.sharding import PartitionSpec as P

DIFFUSION = 0.15
MIXING = 0.1
EXPANSION = 0.2
CONTRACTION = 0.15
PRESSURE_SCALE = 0.02
CORIOLIS = 0.5
FRICTION = 0.01
DIVERGENCE = 0.3
STORAGE = 0.1
SPECTRUM_LOW = 0.1
SPECTRUM_HIGH = 1.9
GRAVITY = 0.3
EPSILON = 1e-06
ITERS = 4
TILES_PER_STEP = 2
F32 = jnp.float32

VMEM = pl.BlockSpec(memory_space=pltpu.VMEM)
SMEM = pl.BlockSpec(memory_space=pltpu.SMEM)


def lanes(shape=(8, 128)):
    return lax.broadcasted_iota(jnp.int32, shape, 1)


def subs(shape=(8, 128)):
    return lax.broadcasted_iota(jnp.int32, shape, 0)


def roll_lane(x, shift):
    return pltpu.roll(x, shift % x.shape[1], 1)


def roll_sub(x, shift):
    return pltpu.roll(x, shift % x.shape[0], 0)


def north(x, ghost):
    return roll_lane(jnp.where(lanes() == 0, ghost, x), -1)


def south(x, ghost):
    return roll_lane(jnp.where(lanes() == 127, ghost, x), 1)


def east(x, ghost):
    return roll_sub(jnp.where(subs() == 0, ghost, x), -1)


def west(x, ghost):
    return roll_sub(jnp.where(subs() == 7, ghost, x), 1)


def around(x, lat_ghost, lon_ghost):
    return (east(x, lon_ghost), west(x, lon_ghost), north(x, lat_ghost), south(x, lat_ghost))


def one_of(index, values):
    found = index == values[0]
    for value in values[1:]:
        found = found | (index == value)
    return found


def lat_field(x, f, odd):
    return roll_lane(x, 16 * f + 8 + 64 * odd)


def from_lat_group(x, f, odd):
    return roll_lane(x, -(16 * f + 8 + 64 * odd))


def group_of(lane):
    return lane // 16


def lat_pack_kernel(t_hbm, s_hbm, u_hbm, v_hbm, d_hbm, m_hbm, z_hbm, f_hbm, out_ref, t_ref, s_ref, u_ref, v_ref, d_ref, m_ref, z_ref, f_ref, sem):
    levels = t_ref.shape[0]
    pairs = (
        (t_hbm, t_ref), (s_hbm, s_ref), (u_hbm, u_ref), (v_hbm, v_ref), (d_hbm, d_ref), (m_hbm, m_ref), (z_hbm, z_ref), (f_hbm, f_ref),
    )
    copies = [pltpu.make_async_copy(src, dst, sem.at[i]) for i, (src, dst) in enumerate(pairs)]
    for copy in copies:
        copy.start()
    for copy in copies:
        copy.wait()
    group = group_of(lanes())

    def put(out, fields, odd):
        for f, x in enumerate(fields):
            out = jnp.where(group == f + 4 * odd, lat_field(x, f, odd), out)
        return out

    zero = jnp.zeros((8, 128), F32)
    for j in range(levels // 2):
        out = zero
        for odd in range(2):
            k = 2 * j + odd
            out = put(out, (u_ref[k], v_ref[k], t_ref[k], s_ref[k]), odd)
        out_ref[j] = out
    sea = m_ref[...].astype(F32)
    depth = (d_ref[...] * m_ref[...]).astype(F32)
    out_ref[levels // 2] = put(zero, (depth, sea * z_ref[...], sea * f_ref[...]), 0)


def lon_pack_kernel(info_ref, t_ref, s_ref, u_ref, v_ref, d_ref, m_ref, z_ref, f_ref, a_ref, b_ref, g_ref, q_ref, r_ref):
    levels = t_ref.shape[0]
    count = levels // 2 + 1
    lane, sub = lanes(), subs()
    is_even, is_top = info_ref[0], info_ref[1]
    from_north = lane % 16 >= 8
    flow_sign = jnp.where(group_of(lane) % 4 < 2, -1.0, 1.0).astype(F32)
    odd_lon = jnp.full((8, 128), info_ref[3] % 2, jnp.int32) == 1

    @pl.when(is_even == 1)
    def _():
        for j in range(count):
            g_ref[j] = jnp.where(from_north, a_ref[j], b_ref[j])

    @pl.when((is_even == 0) & (is_top == 0))
    def _():
        for j in range(count):
            g_ref[j] = jnp.where(from_north, b_ref[j], a_ref[j])

    @pl.when(is_top == 1)
    def _():
        for j in range(count):
            rows = jnp.concatenate([b_ref[j, 7 - i : 8 - i, :] for i in range(8)], axis=0)
            turned = roll_lane(rows, 1)
            for i in range(1, 7):
                turned = jnp.where(lane % 16 == 8 + i, roll_lane(rows, 1 + 2 * i), turned)
            if j < levels // 2:
                turned = turned * flow_sign
            g_ref[j] = jnp.where(from_north, turned, a_ref[j])

    def put(k, u, v, t, s):
        g = g_ref[k // 2]
        odd = k % 2
        v4, t2, s6 = roll_sub(v, 4), roll_sub(t, 2), roll_sub(s, 6)
        x = jnp.where((sub >= 4) & (sub <= 5), v4, u)
        x = jnp.where(sub == 2, t2, x)
        x = jnp.where(sub == 6, s6, x)
        to_west = jnp.where(sub == 3, roll_sub(g, 3 - odd), x)
        x = jnp.where((sub >= 2) & (sub <= 3), v4, u)
        x = jnp.where(sub == 1, t2, x)
        x = jnp.where(sub == 5, s6, x)
        to_east = jnp.where(sub == 0, roll_sub(g, 1 + odd), x)
        q_ref[k] = jnp.where(odd_lon, to_west, to_east)
        r_ref[k] = jnp.where(odd_lon, to_east, to_west)

    for k in range(levels):
        put(k, u_ref[k], v_ref[k], t_ref[k], s_ref[k])
    sea = m_ref[...].astype(F32)
    depth, start = (d_ref[...] * m_ref[...]).astype(F32), sea * z_ref[...]
    put(levels, depth, start, sea * f_ref[...], start)
    put(levels + 1, depth, start, start, start)


def lon_masks(info_ref):
    sub = subs()
    odd_lon = jnp.full((8, 128), info_ref[3] % 2, jnp.int32) == 1
    return [x != odd_lon for x in (one_of(sub, (0, 1, 4, 5)), sub == 2, sub == 6, sub == 3)]


def lon_ghost(q, r, masks):
    return jnp.where(masks[0], q, r)


def lon_tracers(q, r, masks):
    return roll_sub(jnp.where(masks[1], q, r), -2), roll_sub(jnp.where(masks[2], q, r), -6)


def corner_group(q_ref, r_ref, j, masks):
    sub = subs()
    x = jnp.where(masks[3], q_ref[2 * j], r_ref[2 * j])
    y = jnp.where(masks[3], q_ref[2 * j + 1], r_ref[2 * j + 1])
    return jnp.where(sub == 0, roll_sub(x, -3), jnp.where(sub == 7, roll_sub(x, -1), roll_sub(y, -2)))


LAT_PARTNER = (1, 0, 3, 2)
LON_PARTNER = (2, 3, 0, 1)


def ext_east(x):
    return [east(x[i], x[LON_PARTNER[i]]) for i in range(len(x))]


def ext_north(x):
    return [north(x[i], x[LAT_PARTNER[i]]) for i in range(len(x))]


def lap(x, mask_e, mask_n, tiles):
    f_e = [jnp.where(m, y - c, 0.0) for m, y, c in zip(mask_e, ext_east(x), x)]
    f_n = [jnp.where(m, y - c, 0.0) for m, y, c in zip(mask_n, ext_north(x), x)]
    out = []
    for i in tiles:
        out.append(f_e[i] - west(f_e[i], f_e[LON_PARTNER[i]]) + (f_n[i] - south(f_n[i], f_n[LAT_PARTNER[i]])))
    return out


def floats(i):
    return i.astype(F32)


def momentum_kernel(
    info_ref, th_ref, t_ref, s_ref, u_ref, v_ref, d_ref, m_ref, z_ref, f_ref, g_ref, q_ref, r_ref, us_ref, vs_ref, chunk_ref, st_ref
):
    levels = t_ref.shape[0]
    lane, sub = lanes(), subs()
    edges = lon_masks(info_ref)
    last = levels // 2
    sea = m_ref[...].astype(F32)
    corner = corner_group(q_ref, r_ref, last, edges)
    edge = lon_ghost(q_ref[levels], r_ref[levels], edges)
    depth = [(d_ref[...] * m_ref[...]).astype(F32), from_lat_group(g_ref[last], 0, 0), edge, from_lat_group(corner, 0, 0)]
    low_e = [jnp.minimum(x, y) for x, y in zip(depth, ext_east(depth))]
    low_n = [jnp.minimum(x, y) for x, y in zip(depth, ext_north(depth))]
    lat_index = (lane + info_ref[2] * 128).astype(F32)
    ghost_index = lat_index + jnp.where(lane < 64, 128.0, -128.0)
    lats = 128.0 * info_ref[4].astype(F32)
    ghost_index = jnp.where(ghost_index >= lats, 2.0 * lats - 1.0 - ghost_index, ghost_index)
    coriolis = [CORIOLIS * (2.0 * (x + 0.5) / lats - 1.0) for x in (lat_index, ghost_index)]
    zero = jnp.zeros((8, 128), F32)
    both = (0, 1)

    def level(k, odd, j, corners, carry):
        p, h, tu, tv = carry
        th = th_ref[k]
        kf = floats(k) + 0.5
        g, q_in, r_in = g_ref[j], q_ref[k], r_ref[k]
        u_h = lon_ghost(q_in, r_in, edges)
        t_h, s_h = lon_tracers(q_in, r_in, edges)
        u = [u_ref[k], from_lat_group(g, 0, odd), u_h, from_lat_group(corners, 0, odd)]
        v = [v_ref[k], from_lat_group(g, 1, odd), roll_sub(u_h, 4), from_lat_group(corners, 1, odd)]
        t = [t_ref[k], from_lat_group(g, 2, odd), t_h, from_lat_group(corners, 2, odd)]
        s = [s_ref[k], from_lat_group(g, 3, odd), s_h, from_lat_group(corners, 3, odd)]
        mask_e, mask_n, wet = [[x > kf for x in xs] for xs in (low_e, low_n, depth)]
        drag_u = lap(lap(u, mask_e, mask_n, range(4)), mask_e, mask_n, both)
        drag_v = lap(lap(v, mask_e, mask_n, range(4)), mask_e, mask_n, both)
        p = [c + jnp.where(m, (CONTRACTION * b - EXPANSION * a) * th, 0.0) for c, m, a, b in zip(p, wet, t, s)]
        h = [c + jnp.where(m, th, 0.0) for c, m in zip(h, wet)]
        f_e = [jnp.where(m, y - c, 0.0) for m, y, c in zip(mask_e, ext_east(p), p)]
        f_n = [jnp.where(m, y - c, 0.0) for m, y, c in zip(mask_n, ext_north(p), p)]
        us, vs = [], []
        for i in both:
            grad_x = f_e[i] + west(f_e[i], f_e[LON_PARTNER[i]])
            grad_y = f_n[i] + south(f_n[i], f_n[LAT_PARTNER[i]])
            x = u[i] + coriolis[i] * v[i] - (0.5 * PRESSURE_SCALE) * grad_x - FRICTION * drag_u[i]
            y = v[i] - coriolis[i] * u[i] - (0.5 * PRESSURE_SCALE) * grad_y - FRICTION * drag_v[i]
            us.append(jnp.where(wet[i], x, 0.0))
            vs.append(jnp.where(wet[i], y, 0.0))
        us_ref[k] = us[0]
        vs_ref[k] = vs[0]
        return (p, h, [a + th * b for a, b in zip(tu, us)], [a + th * b for a, b in zip(tv, vs)])

    def step(i, carry):
        for j in range(TILES_PER_STEP):
            at = i * TILES_PER_STEP + j
            corners = corner_group(q_ref, r_ref, at, edges)
            for odd in range(2):
                carry = level(2 * at + odd, odd, at, corners, carry)
        return carry

    _, h, tu, tv = lax.fori_loop(0, last // TILES_PER_STEP, step, ([zero] * 4, [zero] * 4, [zero] * 2, [zero] * 2))
    start = [sea * z_ref[...], from_lat_group(g_ref[last], 1, 0), roll_sub(edge, 4), from_lat_group(corner, 1, 0)]
    drive = [sea * f_ref[...], from_lat_group(g_ref[last], 2, 0)]
    weight_e = [jnp.minimum(x, y) * (1.0 / levels) for x, y in zip(h, ext_east(h))]
    weight_n = [jnp.minimum(x, y) * (1.0 / levels) for x, y in zip(h, ext_north(h))]
    flux_e = [x * (y - c) for x, y, c in zip(weight_e, ext_east(start), start)]
    flux_n = [x * (y - c) for x, y, c in zip(weight_n, ext_north(start), start)]
    rights = []
    for i in both:
        spread = flux_e[i] - west(flux_e[i], flux_e[LON_PARTNER[i]]) + (flux_n[i] - south(flux_n[i], flux_n[LAT_PARTNER[i]]))
        base = drive[i] - (STORAGE * start[i] - spread)
        tu_e = jnp.where(sub == 7, 0.0, roll_sub(tu[i], -1))
        tu_w = jnp.where(sub == 0, 0.0, roll_sub(tu[i], 1))
        tv_n, tv_s = north(tv[i], tv[1 - i]), south(tv[i], tv[1 - i])
        rights.append(base - jnp.where(h[i] > 0.0, (0.5 * DIVERGENCE) * ((tu_e - tu_w) + (tv_n - tv_s)), 0.0))
    halo = jnp.where(lane < 16, roll_lane(h[1], 8), jnp.where(lane < 32, roll_lane(rights[1], 24), roll_lane(tu[1], 40)))
    halo = jnp.where(lane < 64, halo, roll_lane(roll_sub(halo, 4), 64))
    halo = jnp.where(sub < 4, halo, jnp.where(sub == 4, roll_sub(tu[0], 4), roll_sub(tu[0], -2)))
    chunk_ref[0] = h[0]
    chunk_ref[1] = rights[0]
    chunk_ref[2] = halo
    for i in range(3):
        st_ref[i] = start[i]


def tracer_kernel(info_ref, th_ref, t_ref, s_ref, u_ref, v_ref, d_ref, m_ref, g_ref, q_ref, r_ref, after_ref, nt_ref, ns_ref):
    del after_ref
    levels = t_ref.shape[0]
    edges = lon_masks(info_ref)
    depth = (d_ref[...] * m_ref[...]).astype(F32)
    depth_g = from_lat_group(g_ref[levels // 2], 0, 0)
    depth_h = lon_ghost(q_ref[levels], r_ref[levels], edges)
    low = [jnp.minimum(depth, n) for n in around(depth, depth_g, depth_h)]
    zero = jnp.zeros((8, 128), F32)

    def level(k, odd, j, carry):
        above_t, above_s = carry
        kf = floats(k) + 0.5
        below = jnp.minimum(k + 1, levels - 1)
        th, th_below = th_ref[k], th_ref[below]
        u, v, t, s = u_ref[k], v_ref[k], t_ref[k], s_ref[k]
        g, q_in, r_in = g_ref[j], q_ref[k], r_ref[k]
        u_h = lon_ghost(q_in, r_in, edges)
        t_h, s_h = lon_tracers(q_in, r_in, edges)
        v_g = from_lat_group(g, 1, odd)
        wet = depth > kf
        wet_below = (depth > kf + 1.0) & (k + 1 < levels)
        inv_space = 1.0 / jnp.full((8, 128), 0.5 * (th + th_below), F32)
        inv_th = MIXING / jnp.full((8, 128), th, F32)
        flow = [0.25 * x for x in (u + east(u, u_h), west(u, u_h) + u, v + north(v, v_g), south(v, v_g) + v)]
        masks = [x > kf for x in low]
        fluxes = []
        for q, q_g, q_h, full_ref, above, out_ref in (
            (t, from_lat_group(g, 2, odd), t_h, t_ref, above_t, nt_ref),
            (s, from_lat_group(g, 3, odd), s_h, s_ref, above_s, ns_ref),
        ):
            q_e, q_w, q_n, q_s = around(q, q_g, q_h)
            f_e = jnp.where(masks[0], flow[0] * (q + q_e) - DIFFUSION * (q_e - q), 0.0)
            f_w = jnp.where(masks[1], flow[1] * (q_w + q) - DIFFUSION * (q - q_w), 0.0)
            f_n = jnp.where(masks[2], flow[2] * (q + q_n) - DIFFUSION * (q_n - q), 0.0)
            f_s = jnp.where(masks[3], flow[3] * (q_s + q) - DIFFUSION * (q - q_s), 0.0)
            vflux = jnp.where(wet_below, (full_ref[below] - q) * inv_space, 0.0)
            vertical = (vflux - above) * inv_th
            out_ref[k] = jnp.where(wet, q + (f_w - f_e + f_s - f_n) + vertical, 0.0)
            fluxes.append(vflux)
        return tuple(fluxes)

    def step(i, carry):
        for j in range(TILES_PER_STEP):
            at = i * TILES_PER_STEP + j
            for odd in range(2):
                carry = level(2 * at + odd, odd, at, carry)
        return carry

    lax.fori_loop(0, levels // 2 // TILES_PER_STEP, step, (zero, zero))


def slab_kernel(info_ref, in_ref, st_ref, sum_ref, surf_ref, slope_ref, h_s, we_s, wn_s, ws_s, dg_s, fac_s, inv_s, r_s, d_s, z_s):
    blocks = in_ref.shape[0] // 24
    inv_levels = info_ref[5].astype(F32)
    inv_levels = 1.0 / jnp.full((8, 128), inv_levels, F32)[0:1, 0:1]

    def rows(i):
        return in_ref[pl.ds(i, blocks, stride=24), :]

    tu = [None] * 8
    for p in range(8):
        packed = rows(16 + p % 4)
        at = 64 * (p // 4)
        h_s[p, :, 0:128] = rows(p)
        h_s[p, :, 128:256] = roll_lane(packed, -8 - at)
        r_s[p, :, 0:128] = rows(8 + p)
        r_s[p, :, 128:256] = roll_lane(packed, -24 - at)
        if p in (0, 7):
            tu[p] = jnp.concatenate([rows(20 if p == 0 else 21), roll_lane(packed, -40 - at)], axis=1)
    r_s[0] = r_s[0] + jnp.where(h_s[0] > 0.0, (0.5 * DIVERGENCE) * roll_sub(tu[7], 1), 0.0)
    r_s[7] = r_s[7] - jnp.where(h_s[7] > 0.0, (0.5 * DIVERGENCE) * roll_sub(tu[0], -1), 0.0)
    for p in range(8):
        h = h_s[p]
        h_e = h_s[p + 1] if p < 7 else roll_sub(h_s[0], -1)
        we_s[p] = jnp.minimum(h, h_e) * inv_levels
        wn = jnp.minimum(h, roll_lane(h, -1)) * inv_levels
        wn_s[p] = wn
        ws_s[p] = roll_lane(wn, 1)
    for p in range(8):
        w_w = we_s[p - 1] if p > 0 else roll_sub(we_s[7], 1)
        diag = STORAGE + we_s[p] + w_w + wn_s[p] + ws_s[p]
        dg_s[p] = diag
        if p > 0:
            diag = diag + we_s[p - 1] * fac_s[p - 1]
        inv = 1.0 / diag
        inv_s[p] = inv
        fac_s[p] = -we_s[p] * inv

    mid = 0.5 * (SPECTRUM_HIGH + SPECTRUM_LOW)
    half = 0.5 * (SPECTRUM_HIGH - SPECTRUM_LOW)
    ratio = mid / half

    def solve(scale_old, scale_new, first):
        y = [None] * 8
        y[0] = r_s[0] * inv_s[0]
        for p in range(1, 8):
            y[p] = (r_s[p] + we_s[p - 1] * y[p - 1]) * inv_s[p]
        x = None
        for p in range(7, -1, -1):
            x = y[p] if x is None else y[p] - fac_s[p] * x
            if first:
                d = x * scale_new
                z_s[p] = d
            else:
                d = scale_old * d_s[p] + scale_new * x
                z_s[p] = z_s[p] + d
            d_s[p] = d

    def subtract():
        for p in range(8):
            d = d_s[p]
            d_e = d_s[p + 1] if p < 7 else roll_sub(d_s[0], -1)
            d_w = d_s[p - 1] if p > 0 else roll_sub(d_s[7], 1)
            w_w = we_s[p - 1] if p > 0 else roll_sub(we_s[7], 1)
            coupled = we_s[p] * d_e + w_w * d_w + wn_s[p] * roll_lane(d, -1) + ws_s[p] * roll_lane(d, 1)
            r_s[p] = r_s[p] - (dg_s[p] * d - coupled)

    solve(0.0, 1.0 / mid, True)
    rho = 1.0 / ratio
    for _ in range(ITERS - 1):
        subtract()
        rho_next = 1.0 / (2.0 * ratio - rho)
        solve(rho_next * rho, 2.0 * rho_next / half, False)
        rho = rho_next
    subtract()
    total = jnp.zeros((blocks, 128), F32)
    for p in range(8):
        x = r_s[p, :, 0:128]
        total = total + x * x
    sum_ref[...] = jnp.sum(jnp.sum(total, axis=0, keepdims=True), axis=1, keepdims=True) + jnp.zeros((1, 128), F32)

    here = info_ref[3]
    right = jnp.where(here + 1 == blocks, 0, here + 1)
    left = jnp.where(here == 0, blocks - 1, here - 1)
    both = jnp.concatenate([z_s[p, pl.ds(here, 1), :] for p in range(8)], axis=0)
    x, x_g = both[:, 0:128], both[:, 128:256]
    sub = subs()
    x_e = jnp.broadcast_to(z_s[0, pl.ds(right, 1), :][:, 0:128], (8, 128))
    x_w = jnp.broadcast_to(z_s[7, pl.ds(left, 1), :][:, 0:128], (8, 128))
    x_h = jnp.where(sub < 4, x_e, x_w)
    x, x_g, x_h = x + st_ref[0], x_g + st_ref[1], x_h + st_ref[2]
    e, w, n, s = around(x, x_g, x_h)
    surf_ref[...] = x
    slope_ref[0] = (0.5 * GRAVITY) * (e - w)
    slope_ref[1] = (0.5 * GRAVITY) * (n - s)


def velocity_kernel(us_ref, vs_ref, d_ref, m_ref, slope_ref, nu_ref, nv_ref):
    depth = (d_ref[...] * m_ref[...]).astype(F32)
    slope_x, slope_y = slope_ref[0], slope_ref[1]
    for k in range(us_ref.shape[0]):
        wet = depth > k + 0.5
        nu_ref[k] = jnp.where(wet, us_ref[k] - slope_x, 0.0)
        nv_ref[k] = jnp.where(wet, vs_ref[k] - slope_y, 0.0)


def call(kernel, name, outs, in_specs, scratch=()):
    return pl.pallas_call(
        kernel,
        name=name,
        out_shape=outs,
        in_specs=in_specs,
        out_specs=jax.tree.map(lambda _: VMEM, outs),
        scratch_shapes=list(scratch),
        compiler_params=pltpu.CompilerParams(vmem_limit_bytes=48 << 20),
    )


def everywhere(tiles, size):
    copies = jnp.broadcast_to(tiles[None], (size, *tiles.shape))
    return lax.all_to_all(copies, "lon", 0, 0, tiled=True).reshape(-1, 128)


def per_device(lon_size, lat_size, temp, salt, u, v, strata, sea, thickness, elevation, drive):
    levels = temp.shape[0]
    lon, lat = lax.axis_index("lon"), lax.axis_index("lat")
    top = lat_size - 1
    info = jnp.stack(
        [1 - lat % 2, (lat == top).astype(jnp.int32), lat, lon, jnp.int32(lat_size), jnp.int32(levels)]
    ).astype(jnp.int32)
    pairs_a = [(i, i ^ 1) for i in range(lat_size)]
    pairs_b = []
    for a in range(lon_size):
        for i in range(1, top, 2):
            pairs_b += [(a * lat_size + i, a * lat_size + i + 1), (a * lat_size + i + 1, a * lat_size + i)]
        pairs_b.append((a * lat_size + top, (lon_size - 1 - a) * lat_size + top))

    def lat_swap(x):
        return lax.ppermute(x, "lat", pairs_a), lax.ppermute(x, ("lon", "lat"), pairs_b)

    def tiles(n, kind=F32):
        return jax.ShapeDtypeStruct((n, 8, 128), kind)

    field, flat = tiles(levels), (8, 128)
    message, packed = tiles(levels + 2), tiles(levels // 2 + 1)
    own = (temp, salt, u, v, strata, sea, elevation, drive)

    edges = call(
        lat_pack_kernel,
        "lat_pack",
        packed,
        [pl.BlockSpec(memory_space=pltpu.HBM)] * 8,
        [pltpu.VMEM(field.shape, F32)] * 4
        + [pltpu.VMEM(flat, jnp.int32)] * 2
        + [pltpu.VMEM(flat, F32)] * 2
        + [pltpu.SemaphoreType.DMA((8,))],
    )(*[pltpu.with_memory_space_constraint(x, pltpu.HBM) for x in own])
    got_a, got_b = lat_swap(edges)
    ghost, pair_q, pair_r = call(lon_pack_kernel, "lon_pack", (packed, message, message), [SMEM] + [VMEM] * 10)(
        info, *own, got_a, got_b
    )
    pair_q = lax.ppermute(pair_q, "lon", [(i, i ^ 1) for i in range(lon_size)])
    pair_r = lax.ppermute(pair_r, "lon", [(i, (i + 1 if i % 2 else i - 1) % lon_size) for i in range(lon_size)])
    u_star, v_star, chunk, start = call(
        momentum_kernel, "momentum", (field, field, tiles(3), tiles(3)), [SMEM, SMEM] + [VMEM] * 11
    )(info, thickness, *own, ghost, pair_q, pair_r)
    ring = everywhere(chunk, lon_size)
    new_temp, new_salt = call(tracer_kernel, "tracers", (field, field), [SMEM] * 2 + [VMEM] * 10)(
        info, thickness, temp, salt, u, v, strata, sea, ghost, pair_q, pair_r, chunk
    )
    ring, new_temp, new_salt = lax.optimization_barrier((ring, new_temp, new_salt))
    total, surface, slope = call(
        slab_kernel,
        "slab",
        (jax.ShapeDtypeStruct((1, 128), F32), jax.ShapeDtypeStruct((8, 128), F32), tiles(2)),
        [SMEM, VMEM, VMEM],
        [pltpu.VMEM((8, lon_size, 256), F32)] * 10,
    )(info, ring, start)
    total = total + lax.ppermute(total, "lat", pairs_a)
    gap = 2
    while gap < lat_size:
        total = total + lax.ppermute(total, "lat", [(i, i ^ gap) for i in range(lat_size)])
        gap *= 2
    cells = lon_size * 8 * lat_size * 128
    rms = jnp.sqrt(total[0, 0] / cells + EPSILON)
    new_u, new_v = call(velocity_kernel, "velocity", (field, field), [VMEM] * 5)(u_star, v_star, strata, sea, slope)
    return (new_temp, new_salt, new_u, new_v, surface, rms)


def solution(mesh):
    cube, flat = P(None, "lon", "lat"), P("lon", "lat")
    return jax.shard_map(
        functools.partial(per_device, mesh.shape["lon"], mesh.shape["lat"]),
        mesh=mesh,
        in_specs=(cube, cube, cube, cube, flat, flat, P(), flat, flat),
        out_specs=(cube, cube, cube, cube, flat, P()),
        check_vma=False,
    )
```

time: 102 us -> 72.7 us (0.71)
  blocking collectives: 26.9 us -> 0 us
  waiting for transfers between devices: 15.4 us -> 25.4 us
  Pallas kernels: 20.1 us -> 13.6 us
  local copies, waits for them, and re-layouts: 5.85 us -> 1.07 us
    all_to_all x1 -> x0, blocking collectives: 26.9 us -> none  [per_device(): lax.all_to_all(copies, 'lon', 0, 0, tiled=True).reshape(lon_size * 24, 128)]
    all_to_all x0 -> x1, waiting for transfers between devices: none -> 18.5 us  [everywhere(): return lax.all_to_all(copies, 'lon', 0, 0, tiled=True).reshape(-1, 128)]
    all_to_all x0 -> x1, starting transfers between devices: none -> 9.93 us  [everywhere(): return lax.all_to_all(copies, 'lon', 0, 0, tiled=True).reshape(-1, 128)]
    ppermute x1, starting transfers between devices: 10.9 us -> 1.16 us  [per_device(): lax.ppermute(total, 'lat', [(i, i ^ gap) for i in range(lat_size)])]
    ppermute x2, waiting for transfers between devices: 10.5 us -> 3.81 us  [the longest x1 3.81 us: per_device(): lax.ppermute(pair_r, 'lon', [(i, (i + 1 if i % 2 else i - 1) % lon_size)...]
    pallas_call x5 -> x4, Pallas kernels: 15.4 us -> 8.88 us  [the longest x1 4.04 us: per_device(): call(momentum_kernel, 'momentum', (field, field, tiles(3), tiles(3)), [SM...]
    unnamed x32 -> x18, local copies, waits for them, and re-layouts: 5.71 us -> 0.05 us
    ppermute x2 -> x1, starting transfers between devices: 8.1 us -> 4.59 us  [lat_swap(): lax.ppermute(x, ('lon', 'lat'), pairs_b)]
  transfers between devices with their start and end apart: 8 -> 7, of which waited for: 5 -> 5; matrix products, arithmetic and copies ran while one was open for 0% -> 0% of each run, Pallas kernels for 7% -> 5%
where the time goes in v2:
time: 72.7 us; the launch traced here: 72.5 us
  starting transfers between devices  30.4 us (42%)
  waiting for transfers between devices  25.4 us (35%)
  Pallas kernels  13.6 us (19%)
  between operations  2.02 us (3%)
  local copies, waits for them, and re-layouts  1.07 us (1%)
    all_to_all x1, waiting for transfers between devices, everywhere(): return lax.all_to_all(copies, 'lon', 0, 0, tiled=True).reshape(-1, 128)  18.5 us
    all_to_all x1, starting transfers between devices, everywhere(): return lax.all_to_all(copies, 'lon', 0, 0, tiled=True).reshape(-1, 128)  9.93 us
    ppermute x1, starting transfers between devices, per_device(): lax.ppermute(pair_r, 'lon', [(i, (i + 1 if i % 2 else i - 1) % lon_size)...  9.62 us
    ppermute x1, starting transfers between devices, lat_swap(): lax.ppermute(x, ('lon', 'lat'), pairs_b)  4.59 us
    pallas_call x1, Pallas kernels, per_device(): call(momentum_kernel, 'momentum', (field, field, tiles(3), tiles(3)), [SM...  4.04 us
    pallas_call x1, Pallas kernels, per_device(): call(slab_kernel, 'slab', (jax.ShapeDtypeStruct((1, 128), F32), jax.Shape...  4.01 us
    ppermute x1, waiting for transfers between devices, per_device(): lax.ppermute(pair_r, 'lon', [(i, (i + 1 if i % 2 else i - 1) % lon_size)...  3.81 us
    ppermute x1, starting transfers between devices, per_device(): total = total + lax.ppermute(total, 'lat', pairs_a)  3.68 us
  transfers between devices with their start and end apart: 7, of which 5 were waited for; matrix products, arithmetic and copies ran while one was open for 0% of the time, Pallas kernels for 5%

profile of v2, /device:TPU:1, one launch (start us, length us, event | category | flops | bytes accessed | tf_op | source)
XLA Modules:
  0.0 72.5 jit_solution(9487494973580838597)
XLA Ops:
  0.6 0.0 copy-start
  0.6 0.0 copy-start.1
  0.7 0.0 copy-start.2
  0.7 0.0 copy-start.3
  0.7 1.4 %lat_pack.1 = f32[17,8,128]{2,1,0:T(8,128)S(1)} custom-call(f32[32,8,128]{2,1,0:T(8,128)} %t_ref.5, f32[32,8,128]{2,1,0:T(8,128)} %s_ref.5, f32[32,8,128]{2,1,0:T(8,128)} %u_ref.5, f32[32,8,128]{2,1,0:T(8,128)} %v_ref.5, s32[8,128]{1,0:T(8,128)} %d_ref.7, s32[8,128]{1,0:T(8,128)} %m_ref.7, f32[8,128]{1,0:T(8,128)} %z_ref.3, f32[8,128]{1,0:T(8,128)} %f_ref.3), custom_call_target="tpu_custom_call" | custom-call | tf_op jit(solution)/shard_map/lat_pack/pallas_call | solution.py:496
  2.1 4.6 %collective-permute-start.1 = (f32[17,8,128]{2,1,0:T(8,128)S(1)}, f32[17,8,128]{2,1,0:T(8,128)S(1)}, u32[]{:S(2)}, u32[]{:S(2)}) collective-permute-start(f32[17,8,128]{2,1,0:T(8,128)S(1)} %lat_pack.1), channel_id=1, source_target_pairs={{1,2},{2,1},{3,255},{5,6},{6,5},{7,251},{9,10},{10,9},{11,247},{13... | collective-permute-start | bytes 208904 | tf_op jit(solution)/shard_map/ppermute | solution.py:487
  6.7 0.1 collective-permute-start
  6.8 0.0 copy-start.6
  6.8 0.0 copy-start.7
  6.9 0.0 copy-start.5
  6.9 0.0 copy-start.4
  6.9 0.1 stack.23.info_ref
  7.0 1.7 %collective-permute-done.1.b_ref = f32[17,8,128]{2,1,0:T(8,128)S(1)} collective-permute-done((f32[17,8,128]{2,1,0:T(8,128)S(1)}, f32[17,8,128]{2,1,0:T(8,128)S(1)}, u32[]{:S(2)}, u32[]{:S(2)}) %collective-permute-start.1) | collective-permute-done | bytes 69664 | tf_op jit(solution)/shard_map/ppermute | solution.py:487
  8.7 0.0 collective-permute-done.a_ref
  8.7 0.0 copy-done
  8.7 0.0 copy-done.1
  8.7 0.0 copy-done.2
  8.7 0.0 copy-done.3
  8.7 0.0 copy-done.6
  8.7 0.0 copy-done.7
  8.7 0.0 copy-done.5
  8.8 0.0 copy-done.4
  8.8 0.6 lon_pack.1
  9.4 1.3 %collective-permute-start.2 = (f32[34,8,128]{2,1,0:T(8,128)S(1)}, f32[34,8,128]{2,1,0:T(8,128)S(1)}, u32[]{:S(2)}, u32[]{:S(2)}) collective-permute-start(f32[34,8,128]{2,1,0:T(8,128)S(1)} %get-tuple-element.24), channel_id=1, source_target_pairs={{0,4},{4,0},{8,12},{12,8},{16,20},{20,16},{24,28},{28,24},{32,36},... | collective-permute-start | bytes 417800 | tf_op jit(solution)/shard_map/ppermute | solution.py:510
  10.7 0.0 copy-start.8
  10.7 9.6 %collective-permute-start.3 = (f32[34,8,128]{2,1,0:T(8,128)S(1)}, f32[34,8,128]{2,1,0:T(8,128)S(1)}, u32[]{:S(2)}, u32[]{:S(2)}) collective-permute-start(f32[34,8,128]{2,1,0:T(8,128)S(1)} %get-tuple-element.25), channel_id=1, source_target_pairs={{0,252},{4,8},{8,4},{12,16},{16,12},{20,24},{24,20},{28,32},{32,28... | collective-permute-start | bytes 417800 | tf_op jit(solution)/shard_map/ppermute | solution.py:511
  20.3 0.0 collective-permute-done.2.q_ref
  20.3 3.8 %collective-permute-done.3.r_ref = f32[34,8,128]{2,1,0:T(8,128)S(1)} collective-permute-done((f32[34,8,128]{2,1,0:T(8,128)S(1)}, f32[34,8,128]{2,1,0:T(8,128)S(1)}, u32[]{:S(2)}, u32[]{:S(2)}) %collective-permute-start.3) | collective-permute-done | bytes 139296 | tf_op jit(solution)/shard_map/ppermute | solution.py:511
  24.1 0.0 copy-done.8
  24.1 4.0 %momentum.1 = (f32[32,8,128]{2,1,0:T(8,128)S(1)}, f32[32,8,128]{2,1,0:T(8,128)S(1)}, f32[3,8,128]{2,1,0:T(8,128)S(1)}, f32[3,8,128]{2,1,0:T(8,128)S(1)}) custom-call(s32[6]{0:T(128)S(1)} %stack.23.info_ref, f32[32]{0:T(128)S(1)} %copy-done.8, f32[32,8,128]{2,1,0:T(8,128)S(1)} %copy-done, f32[32,8,128]{2,1,0:T(8,128)S(1)} %copy-done.1, ...), custom_call_target="tpu_custom_call" | custom-call | tf_op jit(solution)/shard_map/momentum/pallas_call | solution.py:512
  28.2 0.9 %broadcast_in_dim.2 = f32[64,3,8,128]{3,2,1,0:T(8,128)} broadcast(f32[3,8,128]{2,1,0:T(8,128)S(1)} %get-tuple-element.26.after_ref), dimensions={1,2,3} | broadcast | bytes 798720 | tf_op jit(solution)/shard_map/broadcast_in_dim | solution.py:468
  29.1 9.9 %all-to-all-start = ((f32[64,3,8,128]{3,2,1,0:T(8,128)}), f32[64,3,8,128]{3,2,1,0:T(8,128)S(1)}, u32[]{:S(2)}, u32[]{:S(2)}) async-start(f32[64,3,8,128]{3,2,1,0:T(8,128)} %broadcast_in_dim.2), calls=%async_computation | async-start | bytes 1572864 | tf_op jit(solution)/shard_map/all_to_all | solution.py:469
  39.1 2.8 %tracers.1 = (f32[32,8,128]{2,1,0:T(8,128)}, f32[32,8,128]{2,1,0:T(8,128)}) custom-call(s32[6]{0:T(128)S(1)} %stack.23.info_ref, f32[32]{0:T(128)S(1)} %copy-done.8, f32[32,8,128]{2,1,0:T(8,128)S(1)} %copy-done, f32[32,8,128]{2,1,0:T(8,128)S(1)} %copy-done.1, f32[32,8,128]{2,1,0:T(8,128)S(1)} %copy-done.2, f32[32,8,128]{2,1,0:T(8,128)S(1)} %copy-done.3, ...), custom_call_target="tpu_custom_call" | custom-call | tf_op jit(solution)/shard_map/tracers/pallas_call | solution.py:516
  41.8 18.5 %all-to-all-done = f32[64,3,8,128]{3,2,1,0:T(8,128)S(1)} async-done(((f32[64,3,8,128]{3,2,1,0:T(8,128)}), f32[64,3,8,128]{3,2,1,0:T(8,128)S(1)}, u32[]{:S(2)}, u32[]{:S(2)}) %all-to-all-start) | async-done | bytes 786464 | tf_op jit(solution)/shard_map/all_to_all | solution.py:469
  60.4 4.0 %slab.1 = (f32[1,128]{1,0:T(1,128)S(1)}, f32[8,128]{1,0:T(8,128)}, f32[2,8,128]{2,1,0:T(8,128)S(1)}) custom-call(s32[6]{0:T(128)S(1)} %stack.23.info_ref, f32[1536,128]{1,0:T(8,128)S(1)} %bitcast.7, f32[3,8,128]{2,1,0:T(8,128)S(1)} %get-tuple-element.34.st_ref), custom_call_target="tpu_custom_call" | custom-call | tf_op jit(solution)/shard_map/slab/pallas_call | solution.py:520
  64.4 3.7 %collective-permute-start.4 = (f32[1,128]{1,0:T(1,128)S(1)}, f32[1,128]{1,0:T(1,128)S(1)}, u32[]{:S(2)}, u32[]{:S(2)}) collective-permute-start(f32[1,128]{1,0:T(1,128)S(1)} %get-tuple-element.39), channel_id=1, source_target_pairs={{0,1},{1,0},{2,3},{3,2},{4,5},{5,4},{6,7},{7,6},{8,9},{9,8},{10,11... | collective-permute-start | bytes 1544 | tf_op jit(solution)/shard_map/ppermute | solution.py:527
  68.0 0.8 %collective-permute-done.4 = f32[1,128]{1,0:T(1,128)S(1)} collective-permute-done((f32[1,128]{1,0:T(1,128)S(1)}, f32[1,128]{1,0:T(1,128)S(1)}, u32[]{:S(2)}, u32[]{:S(2)}) %collective-permute-start.4) | collective-permute-done | bytes 544 | tf_op jit(solution)/shard_map/ppermute | solution.py:527
  68.9 1.2 %collective-permute-start.5 = (f32[1,128]{1,0:T(1,128)S(1)}, f32[1,128]{1,0:T(1,128)S(1)}, u32[]{:S(2)}, u32[]{:S(2)}) collective-permute-start(f32[1,128]{1,0:T(1,128)S(1)} %add.15), channel_id=1, source_target_pairs={{0,2},{1,3},{2,0},{3,1},{4,6},{5,7},{6,4},{7,5},{8,10},{9,11},{10,... | collective-permute-start | bytes 1544 | tf_op jit(solution)/shard_map/ppermute | solution.py:530
  70.0 0.7 velocity.1
  70.8 0.5 collective-permute-done.5
  (2 shorter events, 0.0 us)
Async XLA Ops:
  0.6 8.1 %copy-start = (f32[32,8,128]{2,1,0:T(8,128)S(1)}, f32[32,8,128]{2,1,0:T(8,128)}, u32[]{:S(2)}) copy-start(f32[32,8,128]{2,1,0:T(8,128)} %t_ref.5) | copy-start | bytes 393220
  0.6 8.1 %copy-start.1 = (f32[32,8,128]{2,1,0:T(8,128)S(1)}, f32[32,8,128]{2,1,0:T(8,128)}, u32[]{:S(2)}) copy-start(f32[32,8,128]{2,1,0:T(8,128)} %s_ref.5) | copy-start | bytes 393220
  0.7 8.1 %copy-start.2 = (f32[32,8,128]{2,1,0:T(8,128)S(1)}, f32[32,8,128]{2,1,0:T(8,128)}, u32[]{:S(2)}) copy-start(f32[32,8,128]{2,1,0:T(8,128)} %u_ref.5) | copy-start | bytes 393220
  0.7 8.1 %copy-start.3 = (f32[32,8,128]{2,1,0:T(8,128)S(1)}, f32[32,8,128]{2,1,0:T(8,128)}, u32[]{:S(2)}) copy-start(f32[32,8,128]{2,1,0:T(8,128)} %v_ref.5) | copy-start | bytes 393220
  2.1 6.6 %collective-permute-start.1 = (f32[17,8,128]{2,1,0:T(8,128)S(1)}, f32[17,8,128]{2,1,0:T(8,128)S(1)}, u32[]{:S(2)}, u32[]{:S(2)}) collective-permute-start(f32[17,8,128]{2,1,0:T(8,128)S(1)} %lat_pack.1), channel_id=1, source_target_pairs={{1,2},{2,1},{3,255},{5,6},{6,5},{7,251},{9,10},{10,9},{11,247},{13... | collective-permute-start | bytes 208904 | tf_op jit(solution)/shard_map/ppermute | solution.py:487
  6.7 2.0 %collective-permute-start = (f32[17,8,128]{2,1,0:T(8,128)S(1)}, f32[17,8,128]{2,1,0:T(8,128)S(1)}, u32[]{:S(2)}, u32[]{:S(2)}) collective-permute-start(f32[17,8,128]{2,1,0:T(8,128)S(1)} %lat_pack.1), channel_id=1, source_target_pairs={{0,1},{1,0},{2,3},{3,2},{4,5},{5,4},{6,7},{7,6},{8,9},{9,8},{10,11... | collective-permute-start | bytes 208904 | tf_op jit(solution)/shard_map/ppermute | solution.py:487
  6.8 1.9 %copy-start.6 = (f32[8,128]{1,0:T(8,128)S(1)}, f32[8,128]{1,0:T(8,128)}, u32[]{:S(2)}) copy-start(f32[8,128]{1,0:T(8,128)} %z_ref.3) | copy-start | bytes 12292
  6.8 1.9 %copy-start.7 = (f32[8,128]{1,0:T(8,128)S(1)}, f32[8,128]{1,0:T(8,128)}, u32[]{:S(2)}) copy-start(f32[8,128]{1,0:T(8,128)} %f_ref.3) | copy-start | bytes 12292
  6.9 1.9 %copy-start.5 = (s32[8,128]{1,0:T(8,128)S(1)}, s32[8,128]{1,0:T(8,128)}, u32[]{:S(2)}) copy-start(s32[8,128]{1,0:T(8,128)} %m_ref.7) | copy-start | bytes 12292
  6.9 1.9 %copy-start.4 = (s32[8,128]{1,0:T(8,128)S(1)}, s32[8,128]{1,0:T(8,128)}, u32[]{:S(2)}) copy-start(s32[8,128]{1,0:T(8,128)} %d_ref.7) | copy-start | bytes 12292
  9.4 10.9 %collective-permute-start.2 = (f32[34,8,128]{2,1,0:T(8,128)S(1)}, f32[34,8,128]{2,1,0:T(8,128)S(1)}, u32[]{:S(2)}, u32[]{:S(2)}) collective-permute-start(f32[34,8,128]{2,1,0:T(8,128)S(1)} %get-tuple-element.24), channel_id=1, source_target_pairs={{0,4},{4,0},{8,12},{12,8},{16,20},{20,16},{24,28},{28,24},{32,36},... | collective-permute-start | bytes 417800 | tf_op jit(solution)/shard_map/ppermute | solution.py:510
  10.7 13.4 %copy-start.8 = (f32[32]{0:T(128)S(1)}, f32[32]{0:T(128)}, u32[]{:S(2)}) copy-start(f32[32]{0:T(128)} %th_ref.3) | copy-start | bytes 388
  10.7 13.4 %collective-permute-start.3 = (f32[34,8,128]{2,1,0:T(8,128)S(1)}, f32[34,8,128]{2,1,0:T(8,128)S(1)}, u32[]{:S(2)}, u32[]{:S(2)}) collective-permute-start(f32[34,8,128]{2,1,0:T(8,128)S(1)} %get-tuple-element.25), channel_id=1, source_target_pairs={{0,252},{4,8},{8,4},{12,16},{16,12},{20,24},{24,20},{28,32},{32,28... | collective-permute-start | bytes 417800 | tf_op jit(solution)/shard_map/ppermute | solution.py:511
  29.1 31.2 %all-to-all-start = ((f32[64,3,8,128]{3,2,1,0:T(8,128)}), f32[64,3,8,128]{3,2,1,0:T(8,128)S(1)}, u32[]{:S(2)}, u32[]{:S(2)}) async-start(f32[64,3,8,128]{3,2,1,0:T(8,128)} %broadcast_in_dim.2), calls=%async_computation | async-start | bytes 1572864 | tf_op jit(solution)/shard_map/all_to_all | solution.py:469
  64.4 4.5 %collective-permute-start.4 = (f32[1,128]{1,0:T(1,128)S(1)}, f32[1,128]{1,0:T(1,128)S(1)}, u32[]{:S(2)}, u32[]{:S(2)}) collective-permute-start(f32[1,128]{1,0:T(1,128)S(1)} %get-tuple-element.39), channel_id=1, source_target_pairs={{0,1},{1,0},{2,3},{3,2},{4,5},{5,4},{6,7},{7,6},{8,9},{9,8},{10,11... | collective-permute-start | bytes 1544 | tf_op jit(solution)/shard_map/ppermute | solution.py:527
  68.9 2.4 %collective-permute-start.5 = (f32[1,128]{1,0:T(1,128)S(1)}, f32[1,128]{1,0:T(1,128)S(1)}, u32[]{:S(2)}, u32[]{:S(2)}) collective-permute-start(f32[1,128]{1,0:T(1,128)S(1)} %add.15), channel_id=1, source_target_pairs={{0,2},{1,3},{2,0},{3,1},{4,6},{5,7},{6,4},{7,5},{8,10},{9,11},{10,... | collective-permute-start | bytes 1544 | tf_op jit(solution)/shard_map/ppermute | solution.py:530

commit v3 on v2

--- a/solution.py
+++ b/solution.py
@@ -5,6 +5,7 @@
 from jax import lax
 from jax.experimental import pallas as pl
 from jax.experimental.pallas import tpu as pltpu
+from jax.sharding import Mesh
 from jax.sharding import PartitionSpec as P
 
 DIFFUSION = 0.15
@@ -22,6 +23,8 @@
 EPSILON = 1e-06
 ITERS = 4
 TILES_PER_STEP = 2
+GROUP = 8
+LON = ("lon_hi", "lon_lo")
 F32 = jnp.float32
 
 VMEM = pl.BlockSpec(memory_space=pltpu.VMEM)
@@ -347,39 +350,36 @@
     lax.fori_loop(0, levels // 2 // TILES_PER_STEP, step, (zero, zero))
 
 
-def slab_kernel(info_ref, in_ref, st_ref, sum_ref, surf_ref, slope_ref, h_s, we_s, wn_s, ws_s, dg_s, fac_s, inv_s, r_s, d_s, z_s):
-    blocks = in_ref.shape[0] // 24
-    inv_levels = info_ref[5].astype(F32)
-    inv_levels = 1.0 / jnp.full((8, 128), inv_levels, F32)[0:1, 0:1]
+def slab_kernel(levels, info_ref, own_ref, q_ref, r_ref, st_ref, sum_ref, surf_ref, slope_ref, we_s, wn_s, fac_s, inv_s, r_s, d_s):
+    odd_group = jnp.full((GROUP, 128), info_ref[3] // GROUP % 2, jnp.int32) == 1
 
     def rows(i):
-        return in_ref[pl.ds(i, blocks, stride=24), :]
-
-    tu = [None] * 8
+        own, q, r = (ref[pl.ds(i, GROUP, stride=24), :] for ref in (own_ref, q_ref, r_ref))
+        return jnp.concatenate([jnp.where(odd_group, q, r), own, jnp.where(odd_group, r, q)], axis=0)
+
+    here = GROUP + info_ref[3] % GROUP
+    right, left = here + 1, here - 1
+    heights, tu = [], [None] * 8
     for p in range(8):
         packed = rows(16 + p % 4)
         at = 64 * (p // 4)
-        h_s[p, :, 0:128] = rows(p)
-        h_s[p, :, 128:256] = roll_lane(packed, -8 - at)
-        r_s[p, :, 0:128] = rows(8 + p)
-        r_s[p, :, 128:256] = roll_lane(packed, -24 - at)
+        heights.append(jnp.concatenate([rows(p), roll_lane(packed, -8 - at)], axis=1))
+        r_s[p] = jnp.concatenate([rows(8 + p), roll_lane(packed, -24 - at)], axis=1)
         if p in (0, 7):
             tu[p] = jnp.concatenate([rows(20 if p == 0 else 21), roll_lane(packed, -40 - at)], axis=1)
-    r_s[0] = r_s[0] + jnp.where(h_s[0] > 0.0, (0.5 * DIVERGENCE) * roll_sub(tu[7], 1), 0.0)
-    r_s[7] = r_s[7] - jnp.where(h_s[7] > 0.0, (0.5 * DIVERGENCE) * roll_sub(tu[0], -1), 0.0)
+    r_s[0] = r_s[0] + jnp.where(heights[0] > 0.0, (0.5 * DIVERGENCE) * roll_sub(tu[7], 1), 0.0)
+    r_s[7] = r_s[7] - jnp.where(heights[7] > 0.0, (0.5 * DIVERGENCE) * roll_sub(tu[0], -1), 0.0)
     for p in range(8):
-        h = h_s[p]
-        h_e = h_s[p + 1] if p < 7 else roll_sub(h_s[0], -1)
-        we_s[p] = jnp.minimum(h, h_e) * inv_levels
-        wn = jnp.minimum(h, roll_lane(h, -1)) * inv_levels
-        wn_s[p] = wn
-        ws_s[p] = roll_lane(wn, 1)
+        h = heights[p]
+        h_e = heights[p + 1] if p < 7 else roll_sub(heights[0], -1)
+        we_s[p] = jnp.minimum(h, h_e) * (1.0 / levels)
+        wn_s[p] = jnp.minimum(h, roll_lane(h, -1)) * (1.0 / levels)
     for p in range(8):
         w_w = we_s[p - 1] if p > 0 else roll_sub(we_s[7], 1)
-        diag = STORAGE + we_s[p] + w_w + wn_s[p] + ws_s[p]
-        dg_s[p] = diag
+        wn = wn_s[p]
+        diag = STORAGE + we_s[p] + w_w + wn + roll_lane(wn, 1)
         if p > 0:
-            diag = diag + we_s[p - 1] * fac_s[p - 1]
+            diag = diag + w_w * fac_s[p - 1]
         inv = 1.0 / diag
         inv_s[p] = inv
         fac_s[p] = -we_s[p] * inv
@@ -388,53 +388,47 @@
     half = 0.5 * (SPECTRUM_HIGH - SPECTRUM_LOW)
     ratio = mid / half
 
-    def solve(scale_old, scale_new, first):
-        y = [None] * 8
-        y[0] = r_s[0] * inv_s[0]
-        for p in range(1, 8):
-            y[p] = (r_s[p] + we_s[p - 1] * y[p - 1]) * inv_s[p]
+    def residuals():
+        d, last = d_s[0], d_s[7]
+        edge = we_s[7] * (roll_sub(d, -1) - last)
+        f_w = roll_sub(edge, 1)
+        for p in range(8):
+            d_e = d_s[p + 1] if p < 7 else None
+            f_e = we_s[p] * (d_e - d) if p < 7 else edge
+            f_n = wn_s[p] * (roll_lane(d, -1) - d)
+            yield r_s[p] - STORAGE * d + ((f_e - f_w) + (f_n - roll_lane(f_n, 1)))
+            f_w, d = f_e, d_e
+
+    def step(scale_old, scale_new, first):
+        y = []
+        for p, r in enumerate((r_s[p] for p in range(8)) if first else residuals()):
+            if not first:
+                r_s[p] = r
+            y.append((r + we_s[p - 1] * y[p - 1] if p > 0 else r) * inv_s[p])
         x = None
         for p in range(7, -1, -1):
             x = y[p] if x is None else y[p] - fac_s[p] * x
-            if first:
-                d = x * scale_new
-                z_s[p] = d
-            else:
-                d = scale_old * d_s[p] + scale_new * x
-                z_s[p] = z_s[p] + d
-            d_s[p] = d
-
-    def subtract():
-        for p in range(8):
-            d = d_s[p]
-            d_e = d_s[p + 1] if p < 7 else roll_sub(d_s[0], -1)
-            d_w = d_s[p - 1] if p > 0 else roll_sub(d_s[7], 1)
-            w_w = we_s[p - 1] if p > 0 else roll_sub(we_s[7], 1)
-            coupled = we_s[p] * d_e + w_w * d_w + wn_s[p] * roll_lane(d, -1) + ws_s[p] * roll_lane(d, 1)
-            r_s[p] = r_s[p] - (dg_s[p] * d - coupled)
-
-    solve(0.0, 1.0 / mid, True)
+            d_s[p] = x * scale_new if first else scale_old * d_s[p] + scale_new * x
+        own = jnp.concatenate([d_s[p, pl.ds(here, 1), :] for p in range(8)], axis=0)
+        return own, d_s[0, pl.ds(right, 1), :], d_s[7, pl.ds(left, 1), :]
+
+    found = step(0.0, 1.0 / mid, True)
     rho = 1.0 / ratio
     for _ in range(ITERS - 1):
-        subtract()
         rho_next = 1.0 / (2.0 * ratio - rho)
-        solve(rho_next * rho, 2.0 * rho_next / half, False)
+        found = [a + b for a, b in zip(found, step(rho_next * rho, 2.0 * rho_next / half, False))]
         rho = rho_next
-    subtract()
-    total = jnp.zeros((blocks, 128), F32)
-    for p in range(8):
-        x = r_s[p, :, 0:128]
-        total = total + x * x
+    total = jnp.zeros((GROUP, 128), F32)
+    for r in residuals():
+        r = r[GROUP : 2 * GROUP, 0:128]
+        total = total + r * r
     sum_ref[...] = jnp.sum(jnp.sum(total, axis=0, keepdims=True), axis=1, keepdims=True) + jnp.zeros((1, 128), F32)
 
-    here = info_ref[3]
-    right = jnp.where(here + 1 == blocks, 0, here + 1)
-    left = jnp.where(here == 0, blocks - 1, here - 1)
-    both = jnp.concatenate([z_s[p, pl.ds(here, 1), :] for p in range(8)], axis=0)
+    both, x_e, x_w = found
     x, x_g = both[:, 0:128], both[:, 128:256]
     sub = subs()
-    x_e = jnp.broadcast_to(z_s[0, pl.ds(right, 1), :][:, 0:128], (8, 128))
-    x_w = jnp.broadcast_to(z_s[7, pl.ds(left, 1), :][:, 0:128], (8, 128))
+    x_e = jnp.broadcast_to(x_e[:, 0:128], (8, 128))
+    x_w = jnp.broadcast_to(x_w[:, 0:128], (8, 128))
     x_h = jnp.where(sub < 4, x_e, x_w)
     x, x_g, x_h = x + st_ref[0], x_g + st_ref[1], x_h + st_ref[2]
     e, w, n, s = around(x, x_g, x_h)
@@ -464,14 +458,17 @@
     )
 
 
-def everywhere(tiles, size):
-    copies = jnp.broadcast_to(tiles[None], (size, *tiles.shape))
-    return lax.all_to_all(copies, "lon", 0, 0, tiled=True).reshape(-1, 128)
+def from_all(x, axes):
+    size = 1
+    for axis in axes:
+        size *= lax.axis_size(axis)
+    copies = jnp.broadcast_to(x[None], (size, *x.shape))
+    return lax.all_to_all(copies, axes, 0, 0, tiled=True)
 
 
 def per_device(lon_size, lat_size, temp, salt, u, v, strata, sea, thickness, elevation, drive):
     levels = temp.shape[0]
-    lon, lat = lax.axis_index("lon"), lax.axis_index("lat")
+    lon, lat = lax.axis_index(LON), lax.axis_index("lat")
     top = lat_size - 1
     info = jnp.stack(
         [1 - lat % 2, (lat == top).astype(jnp.int32), lat, lon, jnp.int32(lat_size), jnp.int32(levels)]
@@ -484,7 +481,7 @@
         pairs_b.append((a * lat_size + top, (lon_size - 1 - a) * lat_size + top))
 
     def lat_swap(x):
-        return lax.ppermute(x, "lat", pairs_a), lax.ppermute(x, ("lon", "lat"), pairs_b)
+        return lax.ppermute(x, "lat", pairs_a), lax.ppermute(x, (*LON, "lat"), pairs_b)
 
     def tiles(n, kind=F32):
         return jax.ShapeDtypeStruct((n, 8, 128), kind)
@@ -507,28 +504,28 @@
     ghost, pair_q, pair_r = call(lon_pack_kernel, "lon_pack", (packed, message, message), [SMEM] + [VMEM] * 10)(
         info, *own, got_a, got_b
     )
-    pair_q = lax.ppermute(pair_q, "lon", [(i, i ^ 1) for i in range(lon_size)])
-    pair_r = lax.ppermute(pair_r, "lon", [(i, (i + 1 if i % 2 else i - 1) % lon_size) for i in range(lon_size)])
+    pair_q = lax.ppermute(pair_q, LON, [(i, i ^ 1) for i in range(lon_size)])
+    pair_r = lax.ppermute(pair_r, LON, [(i, (i + 1 if i % 2 else i - 1) % lon_size) for i in range(lon_size)])
     u_star, v_star, chunk, start = call(
         momentum_kernel, "momentum", (field, field, tiles(3), tiles(3)), [SMEM, SMEM] + [VMEM] * 11
     )(info, thickness, *own, ghost, pair_q, pair_r)
-    ring = everywhere(chunk, lon_size)
+    group = from_all(chunk, ("lon_lo",)).reshape(GROUP * 24, 128)
+    group, after = lax.optimization_barrier((group, chunk))
+    groups = lon_size // GROUP
+    group_q = lax.ppermute(group, "lon_hi", [(i, i ^ 1) for i in range(groups)])
+    group_r = lax.ppermute(group, "lon_hi", [(i, (i + 1 if i % 2 else i - 1) % groups) for i in range(groups)])
     new_temp, new_salt = call(tracer_kernel, "tracers", (field, field), [SMEM] * 2 + [VMEM] * 10)(
-        info, thickness, temp, salt, u, v, strata, sea, ghost, pair_q, pair_r, chunk
+        info, thickness, temp, salt, u, v, strata, sea, ghost, pair_q, pair_r, after
     )
-    ring, new_temp, new_salt = lax.optimization_barrier((ring, new_temp, new_salt))
+    group_q, group_r, new_temp, new_salt = lax.optimization_barrier((group_q, group_r, new_temp, new_salt))
     total, surface, slope = call(
-        slab_kernel,
+        functools.partial(slab_kernel, levels),
         "slab",
         (jax.ShapeDtypeStruct((1, 128), F32), jax.ShapeDtypeStruct((8, 128), F32), tiles(2)),
-        [SMEM, VMEM, VMEM],
-        [pltpu.VMEM((8, lon_size, 256), F32)] * 10,
-    )(info, ring, start)
-    total = total + lax.ppermute(total, "lat", pairs_a)
-    gap = 2
-    while gap < lat_size:
-        total = total + lax.ppermute(total, "lat", [(i, i ^ gap) for i in range(lat_size)])
-        gap *= 2
+        [SMEM] + [VMEM] * 4,
+        [pltpu.VMEM((8, 3 * GROUP, 256), F32)] * 6,
+    )(info, group, group_q, group_r, start)
+    total = jnp.sum(from_all(total, ("lon_hi", "lat")), axis=0)
     cells = lon_size * 8 * lat_size * 128
     rms = jnp.sqrt(total[0, 0] / cells + EPSILON)
     new_u, new_v = call(velocity_kernel, "velocity", (field, field), [VMEM] * 5)(u_star, v_star, strata, sea, slope)
@@ -536,10 +533,12 @@
 
 
 def solution(mesh):
-    cube, flat = P(None, "lon", "lat"), P("lon", "lat")
+    lon_size, lat_size = mesh.shape["lon"], mesh.shape["lat"]
+    finer = Mesh(mesh.devices.reshape(lon_size // GROUP, GROUP, lat_size), (*LON, "lat"))
+    cube, flat = P(None, LON, "lat"), P(LON, "lat")
     return jax.shard_map(
-        functools.partial(per_device, mesh.shape["lon"], mesh.shape["lat"]),
-        mesh=mesh,
+        functools.partial(per_device, lon_size, lat_size),
+        mesh=finer,
         in_specs=(cube, cube, cube, cube, flat, flat, P(), flat, flat),
         out_specs=(cube, cube, cube, cube, flat, P()),
         check_vma=False,

time: 72.7 us -> 67.4 us (0.927)
  waiting for transfers between devices: 25.4 us -> 13.6 us
  blocking collectives: 0 us -> 9.18 us
  Pallas kernels: 13.6 us -> 11.9 us
  starting transfers between devices: 30.4 us -> 29.6 us
    all_to_all x1, waiting for transfers between devices: 18.5 us -> 7.09 us  [from_all(): return lax.all_to_all(copies, axes, 0, 0, tiled=True)]
    all_to_all x0 -> x1, blocking collectives: none -> 9.18 us  [from_all(): return lax.all_to_all(copies, axes, 0, 0, tiled=True)]
    all_to_all x1, starting transfers between devices: 9.93 us -> 7.53 us  [from_all(): return lax.all_to_all(copies, axes, 0, 0, tiled=True)]
    pallas_call x1, Pallas kernels: 4.01 us -> 2.34 us  [per_device(): call(functools.partial(slab_kernel, levels), 'slab', (jax.ShapeDtypeStruc...]
    ppermute x5, starting transfers between devices: 20.3 us -> 22 us  [the longest x1 9.62 us: per_device(): lax.ppermute(pair_r, LON, [(i, (i + 1 if i % 2 else i - 1) % lon_size) fo...]
  transfers between devices with their start and end apart: 7 -> 7, of which waited for: 5 -> 4; matrix products, arithmetic and copies ran while one was open for 0% -> 0% of each run, Pallas kernels for 5% -> 5%
where the time goes in v3:
time: 67.4 us; the launch traced here: 67.2 us
  starting transfers between devices  29.6 us (44%)
  waiting for transfers between devices  13.6 us (20%)
  Pallas kernels  11.9 us (18%)
  blocking collectives  9.18 us (14%)
  between operations  2.03 us (3%)
  local copies, waits for them, and re-layouts  0.75 us (1%)
    ppermute x1, starting transfers between devices, per_device(): lax.ppermute(pair_r, LON, [(i, (i + 1 if i % 2 else i - 1) % lon_size) fo...  9.62 us
    all_to_all x1, blocking collectives, from_all(): return lax.all_to_all(copies, axes, 0, 0, tiled=True)  9.18 us
    all_to_all x1, starting transfers between devices, from_all(): return lax.all_to_all(copies, axes, 0, 0, tiled=True)  7.53 us
    all_to_all x1, waiting for transfers between devices, from_all(): return lax.all_to_all(copies, axes, 0, 0, tiled=True)  7.09 us
    ppermute x1, starting transfers between devices, per_device(): lax.ppermute(group, 'lon_hi', [(i, (i + 1 if i % 2 else i - 1) % groups)...  6.5 us
    ppermute x1, starting transfers between devices, lat_swap(): lax.ppermute(x, (*LON, 'lat'), pairs_b)  4.59 us
    pallas_call x1, Pallas kernels, per_device(): call(momentum_kernel, 'momentum', (field, field, tiles(3), tiles(3)), [SM...  4.04 us
    ppermute x1, waiting for transfers between devices, per_device(): lax.ppermute(pair_r, LON, [(i, (i + 1 if i % 2 else i - 1) % lon_size) fo...  3.81 us
  transfers between devices with their start and end apart: 7, of which 4 were waited for; matrix products, arithmetic and copies ran while one was open for 0% of the time, Pallas kernels for 5%

profile of v3, /device:TPU:1, one launch (start us, length us, event | category | flops | bytes accessed | tf_op | source)
XLA Modules:
  0.0 67.2 jit_solution(397820657362455312)
XLA Ops:
  0.6 0.0 copy-start
  0.6 0.0 copy-start.1
  0.7 0.0 copy-start.2
  0.7 0.0 copy-start.3
  0.7 1.4 %lat_pack.1 = f32[17,8,128]{2,1,0:T(8,128)S(1)} custom-call(f32[32,8,128]{2,1,0:T(8,128)} %t_ref.5, f32[32,8,128]{2,1,0:T(8,128)} %s_ref.5, f32[32,8,128]{2,1,0:T(8,128)} %u_ref.5, f32[32,8,128]{2,1,0:T(8,128)} %v_ref.5, s32[8,128]{1,0:T(8,128)} %d_ref.7, s32[8,128]{1,0:T(8,128)} %m_ref.7, f32[8,128]{1,0:T(8,128)} %z_ref.3, f32[8,128]{1,0:T(8,128)} %f_ref.3), custom_call_target="tpu_custom_call" | custom-call | tf_op jit(solution)/shard_map/lat_pack/pallas_call | solution.py:493
  2.1 4.6 %collective-permute-start.1 = (f32[17,8,128]{2,1,0:T(8,128)S(1)}, f32[17,8,128]{2,1,0:T(8,128)S(1)}, u32[]{:S(2)}, u32[]{:S(2)}) collective-permute-start(f32[17,8,128]{2,1,0:T(8,128)S(1)} %lat_pack.1), channel_id=1, source_target_pairs={{1,2},{2,1},{3,255},{5,6},{6,5},{7,251},{9,10},{10,9},{11,247},{13... | collective-permute-start | bytes 208904 | tf_op jit(solution)/shard_map/ppermute | solution.py:484
  6.7 0.1 collective-permute-start
  6.8 0.0 copy-start.6
  6.8 0.0 copy-start.7
  6.9 0.0 copy-start.5
  6.9 0.0 copy-start.4
  6.9 0.1 stack.23.info_ref
  7.0 1.7 %collective-permute-done.1.b_ref = f32[17,8,128]{2,1,0:T(8,128)S(1)} collective-permute-done((f32[17,8,128]{2,1,0:T(8,128)S(1)}, f32[17,8,128]{2,1,0:T(8,128)S(1)}, u32[]{:S(2)}, u32[]{:S(2)}) %collective-permute-start.1) | collective-permute-done | bytes 69664 | tf_op jit(solution)/shard_map/ppermute | solution.py:484
  8.7 0.0 collective-permute-done.a_ref
  8.7 0.0 copy-done
  8.7 0.0 copy-done.1
  8.7 0.0 copy-done.2
  8.7 0.0 copy-done.3
  8.7 0.0 copy-done.6
  8.7 0.0 copy-done.7
  8.7 0.0 copy-done.5
  8.8 0.0 copy-done.4
  8.8 0.6 lon_pack.1
  9.4 1.3 %collective-permute-start.2 = (f32[34,8,128]{2,1,0:T(8,128)S(1)}, f32[34,8,128]{2,1,0:T(8,128)S(1)}, u32[]{:S(2)}, u32[]{:S(2)}) collective-permute-start(f32[34,8,128]{2,1,0:T(8,128)S(1)} %get-tuple-element.27), channel_id=1, source_target_pairs={{0,4},{4,0},{8,12},{12,8},{16,20},{20,16},{24,28},{28,24},{32,36},... | collective-permute-start | bytes 417800 | tf_op jit(solution)/shard_map/ppermute | solution.py:507
  10.7 0.0 copy-start.8
  10.7 9.6 %collective-permute-start.3 = (f32[34,8,128]{2,1,0:T(8,128)S(1)}, f32[34,8,128]{2,1,0:T(8,128)S(1)}, u32[]{:S(2)}, u32[]{:S(2)}) collective-permute-start(f32[34,8,128]{2,1,0:T(8,128)S(1)} %get-tuple-element.28), channel_id=1, source_target_pairs={{0,252},{4,8},{8,4},{12,16},{16,12},{20,24},{24,20},{28,32},{32,28... | collective-permute-start | bytes 417800 | tf_op jit(solution)/shard_map/ppermute | solution.py:508
  20.3 0.0 collective-permute-done.2.q_ref
  20.3 3.8 %collective-permute-done.3.r_ref = f32[34,8,128]{2,1,0:T(8,128)S(1)} collective-permute-done((f32[34,8,128]{2,1,0:T(8,128)S(1)}, f32[34,8,128]{2,1,0:T(8,128)S(1)}, u32[]{:S(2)}, u32[]{:S(2)}) %collective-permute-start.3) | collective-permute-done | bytes 139296 | tf_op jit(solution)/shard_map/ppermute | solution.py:508
  24.1 0.0 copy-done.8
  24.1 4.0 %momentum.1 = (f32[32,8,128]{2,1,0:T(8,128)S(1)}, f32[32,8,128]{2,1,0:T(8,128)S(1)}, f32[3,8,128]{2,1,0:T(8,128)S(1)}, f32[3,8,128]{2,1,0:T(8,128)S(1)}) custom-call(s32[6]{0:T(128)S(1)} %stack.23.info_ref, f32[32]{0:T(128)S(1)} %copy-done.8, f32[32,8,128]{2,1,0:T(8,128)S(1)} %copy-done, f32[32,8,128]{2,1,0:T(8,128)S(1)} %copy-done.1, ...), custom_call_target="tpu_custom_call" | custom-call | tf_op jit(solution)/shard_map/momentum/pallas_call | solution.py:509
  28.2 9.2 %all_to_all.10 = f32[8,3,8,128]{3,2,1,0:T(8,128)S(1)} all-to-all(f32[8,3,8,128]{3,2,1,0:T(8,128)S(1)} %broadcast_in_dim.6), channel_id=1, replica_groups=mesh['lon_hi'=8,'lon_lo'=8,'lat'=4] {'lon_lo'}, dimensions={0} | all-to-all | bytes 196608 | tf_op jit(solution)/shard_map/all_to_all | solution.py:466
  37.4 6.5 %collective-permute-start.5 = (f32[192,128]{1,0:T(8,128)S(1)}, f32[192,128]{1,0:T(8,128)S(1)}, u32[]{:S(2)}, u32[]{:S(2)}) collective-permute-start(f32[192,128]{1,0:T(8,128)S(1)} %bitcast.10), channel_id=1, source_target_pairs={{0,224},{32,64},{64,32},{96,128},{128,96},{160,192},{192,160},{224... | collective-permute-start | bytes 294920 | tf_op jit(solution)/shard_map/ppermute | solution.py:516
  43.9 0.0 collective-permute-start.4
  43.9 2.8 %tracers.1 = (f32[32,8,128]{2,1,0:T(8,128)}, f32[32,8,128]{2,1,0:T(8,128)}) custom-call(s32[6]{0:T(128)S(1)} %stack.23.info_ref, f32[32]{0:T(128)S(1)} %copy-done.8, f32[32,8,128]{2,1,0:T(8,128)S(1)} %copy-done, f32[32,8,128]{2,1,0:T(8,128)S(1)} %copy-done.1, f32[32,8,128]{2,1,0:T(8,128)S(1)} %copy-done.2, f32[32,8,128]{2,1,0:T(8,128)S(1)} %copy-done.3, ...), custom_call_target="tpu_custom_call" | custom-call | tf_op jit(solution)/shard_map/tracers/pallas_call | solution.py:517
  46.6 0.0 collective-permute-done.5.r_ref
  46.6 1.0 %collective-permute-done.4.q_ref = f32[192,128]{1,0:T(8,128)S(1)} collective-permute-done((f32[192,128]{1,0:T(8,128)S(1)}, f32[192,128]{1,0:T(8,128)S(1)}, u32[]{:S(2)}, u32[]{:S(2)}) %collective-permute-start.4) | collective-permute-done | bytes 98336 | tf_op jit(solution)/shard_map/ppermute | solution.py:515
  47.7 2.3 %slab.1 = (f32[1,128]{1,0:T(1,128)S(1)}, f32[8,128]{1,0:T(8,128)}, f32[2,8,128]{2,1,0:T(8,128)S(1)}) custom-call(s32[6]{0:T(128)S(1)} %stack.23.info_ref, f32[192,128]{1,0:T(8,128)S(1)} %bitcast.12, f32[192,128]{1,0:T(8,128)S(1)} %collective-permute-done.4.q_ref, f32[192,128]{1,0:T(8,128)S(1)} %collective-permute-done.5.r_ref, ...), custom_call_target="tpu_custom_call" | custom-call | tf_op jit(solution)/shard_map/slab/pallas_call | solution.py:521
  50.0 0.6 broadcast_in_dim.16
  50.6 7.5 %all-to-all-start.1 = ((f32[32,1,128]{2,1,0:T(1,128)}), f32[32,1,128]{2,1,0:T(1,128)S(1)}, u32[]{:S(2)}, u32[]{:S(2)}) async-start(f32[32,1,128]{2,1,0:T(1,128)} %broadcast_in_dim.16), calls=%async_computation.1 | async-start | bytes 32768 | tf_op jit(solution)/shard_map/all_to_all | solution.py:466
  58.1 0.7 %velocity.1 = (f32[32,8,128]{2,1,0:T(8,128)}, f32[32,8,128]{2,1,0:T(8,128)}) custom-call(f32[32,8,128]{2,1,0:T(8,128)S(1)} %get-tuple-element.36.us_ref, f32[32,8,128]{2,1,0:T(8,128)S(1)} %get-tuple-element.37.vs_ref, s32[8,128]{1,0:T(8,128)S(1)} %copy-done.4, s32[8,128]{1,0:T(8,128)S(1)} %copy-done.5, f32[2,8,128]{2,1,0:T(8,128)S(1)} %get-tuple-element.41.slope_ref), custom_call_target="tpu_custom_call" | custom-call | tf_op jit(solution)/shard_map/velocity/pallas_call | solution.py:531
  58.9 7.1 %all-to-all-done.1 = f32[32,1,128]{2,1,0:T(1,128)S(1)} async-done(((f32[32,1,128]{2,1,0:T(1,128)}), f32[32,1,128]{2,1,0:T(1,128)S(1)}, u32[]{:S(2)}, u32[]{:S(2)}) %all-to-all-start.1) | async-done | bytes 16416 | tf_op jit(solution)/shard_map/all_to_all | solution.py:466
  (2 shorter events, 0.0 us)
Async XLA Ops:
  0.6 8.1 %copy-start = (f32[32,8,128]{2,1,0:T(8,128)S(1)}, f32[32,8,128]{2,1,0:T(8,128)}, u32[]{:S(2)}) copy-start(f32[32,8,128]{2,1,0:T(8,128)} %t_ref.5) | copy-start | bytes 393220
  0.6 8.1 %copy-start.1 = (f32[32,8,128]{2,1,0:T(8,128)S(1)}, f32[32,8,128]{2,1,0:T(8,128)}, u32[]{:S(2)}) copy-start(f32[32,8,128]{2,1,0:T(8,128)} %s_ref.5) | copy-start | bytes 393220
  0.7 8.1 %copy-start.2 = (f32[32,8,128]{2,1,0:T(8,128)S(1)}, f32[32,8,128]{2,1,0:T(8,128)}, u32[]{:S(2)}) copy-start(f32[32,8,128]{2,1,0:T(8,128)} %u_ref.5) | copy-start | bytes 393220
  0.7 8.1 %copy-start.3 = (f32[32,8,128]{2,1,0:T(8,128)S(1)}, f32[32,8,128]{2,1,0:T(8,128)}, u32[]{:S(2)}) copy-start(f32[32,8,128]{2,1,0:T(8,128)} %v_ref.5) | copy-start | bytes 393220
  2.1 6.6 %collective-permute-start.1 = (f32[17,8,128]{2,1,0:T(8,128)S(1)}, f32[17,8,128]{2,1,0:T(8,128)S(1)}, u32[]{:S(2)}, u32[]{:S(2)}) collective-permute-start(f32[17,8,128]{2,1,0:T(8,128)S(1)} %lat_pack.1), channel_id=1, source_target_pairs={{1,2},{2,1},{3,255},{5,6},{6,5},{7,251},{9,10},{10,9},{11,247},{13... | collective-permute-start | bytes 208904 | tf_op jit(solution)/shard_map/ppermute | solution.py:484
  6.7 2.0 %collective-permute-start = (f32[17,8,128]{2,1,0:T(8,128)S(1)}, f32[17,8,128]{2,1,0:T(8,128)S(1)}, u32[]{:S(2)}, u32[]{:S(2)}) collective-permute-start(f32[17,8,128]{2,1,0:T(8,128)S(1)} %lat_pack.1), channel_id=1, source_target_pairs={{0,1},{1,0},{2,3},{3,2},{4,5},{5,4},{6,7},{7,6},{8,9},{9,8},{10,11... | collective-permute-start | bytes 208904 | tf_op jit(solution)/shard_map/ppermute | solution.py:484
  6.8 1.9 %copy-start.6 = (f32[8,128]{1,0:T(8,128)S(1)}, f32[8,128]{1,0:T(8,128)}, u32[]{:S(2)}) copy-start(f32[8,128]{1,0:T(8,128)} %z_ref.3) | copy-start | bytes 12292
  6.8 1.9 %copy-start.7 = (f32[8,128]{1,0:T(8,128)S(1)}, f32[8,128]{1,0:T(8,128)}, u32[]{:S(2)}) copy-start(f32[8,128]{1,0:T(8,128)} %f_ref.3) | copy-start | bytes 12292
  6.9 1.9 %copy-start.5 = (s32[8,128]{1,0:T(8,128)S(1)}, s32[8,128]{1,0:T(8,128)}, u32[]{:S(2)}) copy-start(s32[8,128]{1,0:T(8,128)} %m_ref.7) | copy-start | bytes 12292
  6.9 1.9 %copy-start.4 = (s32[8,128]{1,0:T(8,128)S(1)}, s32[8,128]{1,0:T(8,128)}, u32[]{:S(2)}) copy-start(s32[8,128]{1,0:T(8,128)} %d_ref.7) | copy-start | bytes 12292
  9.4 10.9 %collective-permute-start.2 = (f32[34,8,128]{2,1,0:T(8,128)S(1)}, f32[34,8,128]{2,1,0:T(8,128)S(1)}, u32[]{:S(2)}, u32[]{:S(2)}) collective-permute-start(f32[34,8,128]{2,1,0:T(8,128)S(1)} %get-tuple-element.27), channel_id=1, source_target_pairs={{0,4},{4,0},{8,12},{12,8},{16,20},{20,16},{24,28},{28,24},{32,36},... | collective-permute-start | bytes 417800 | tf_op jit(solution)/shard_map/ppermute | solution.py:507
  10.7 13.4 %copy-start.8 = (f32[32]{0:T(128)S(1)}, f32[32]{0:T(128)}, u32[]{:S(2)}) copy-start(f32[32]{0:T(128)} %th_ref.3) | copy-start | bytes 388
  10.7 13.4 %collective-permute-start.3 = (f32[34,8,128]{2,1,0:T(8,128)S(1)}, f32[34,8,128]{2,1,0:T(8,128)S(1)}, u32[]{:S(2)}, u32[]{:S(2)}) collective-permute-start(f32[34,8,128]{2,1,0:T(8,128)S(1)} %get-tuple-element.28), channel_id=1, source_target_pairs={{0,252},{4,8},{8,4},{12,16},{16,12},{20,24},{24,20},{28,32},{32,28... | collective-permute-start | bytes 417800 | tf_op jit(solution)/shard_map/ppermute | solution.py:508
  37.4 9.3 %collective-permute-start.5 = (f32[192,128]{1,0:T(8,128)S(1)}, f32[192,128]{1,0:T(8,128)S(1)}, u32[]{:S(2)}, u32[]{:S(2)}) collective-permute-start(f32[192,128]{1,0:T(8,128)S(1)} %bitcast.10), channel_id=1, source_target_pairs={{0,224},{32,64},{64,32},{96,128},{128,96},{160,192},{192,160},{224... | collective-permute-start | bytes 294920 | tf_op jit(solution)/shard_map/ppermute | solution.py:516
  43.9 3.8 %collective-permute-start.4 = (f32[192,128]{1,0:T(8,128)S(1)}, f32[192,128]{1,0:T(8,128)S(1)}, u32[]{:S(2)}, u32[]{:S(2)}) collective-permute-start(f32[192,128]{1,0:T(8,128)S(1)} %bitcast.11), channel_id=1, source_target_pairs={{0,32},{32,0},{64,96},{96,64},{128,160},{160,128},{192,224},{224,1... | collective-permute-start | bytes 294920 | tf_op jit(solution)/shard_map/ppermute | solution.py:515
  50.6 15.4 %all-to-all-start.1 = ((f32[32,1,128]{2,1,0:T(1,128)}), f32[32,1,128]{2,1,0:T(1,128)S(1)}, u32[]{:S(2)}, u32[]{:S(2)}) async-start(f32[32,1,128]{2,1,0:T(1,128)} %broadcast_in_dim.16), calls=%async_computation.1 | async-start | bytes 32768 | tf_op jit(solution)/shard_map/all_to_all | solution.py:466

commit v4 on v3

--- a/solution.py
+++ b/solution.py
@@ -22,7 +22,7 @@
 GRAVITY = 0.3
 EPSILON = 1e-06
 ITERS = 4
-TILES_PER_STEP = 2
+TILES_PER_STEP = 4
 GROUP = 8
 LON = ("lon_hi", "lon_lo")
 F32 = jnp.float32
@@ -115,14 +115,37 @@
     out_ref[levels // 2] = put(zero, (depth, sea * z_ref[...], sea * f_ref[...]), 0)
 
 
-def lon_pack_kernel(info_ref, t_ref, s_ref, u_ref, v_ref, d_ref, m_ref, z_ref, f_ref, a_ref, b_ref, g_ref, q_ref, r_ref):
+def lon_rows_kernel(info_ref, t_ref, s_ref, u_ref, v_ref, d_ref, m_ref, z_ref, f_ref, q_ref, r_ref):
     levels = t_ref.shape[0]
-    count = levels // 2 + 1
-    lane, sub = lanes(), subs()
-    is_even, is_top = info_ref[0], info_ref[1]
+    sub = subs()
+    odd_lon = jnp.full((8, 128), info_ref[3] % 2, jnp.int32) == 1
+
+    def put(k, u, v, t, s):
+        v4, t2, s6 = roll_sub(v, 4), roll_sub(t, 2), roll_sub(s, 6)
+        x = jnp.where((sub >= 4) & (sub <= 5), v4, u)
+        x = jnp.where(sub == 2, t2, x)
+        to_west = jnp.where(sub == 6, s6, x)
+        x = jnp.where((sub >= 2) & (sub <= 3), v4, u)
+        x = jnp.where(sub == 1, t2, x)
+        to_east = jnp.where(sub == 5, s6, x)
+        q_ref[k] = jnp.where(odd_lon, to_west, to_east)
+        r_ref[k] = jnp.where(odd_lon, to_east, to_west)
+
+    for k in range(levels):
+        put(k, u_ref[k], v_ref[k], t_ref[k], s_ref[k])
+    sea = m_ref[...].astype(F32)
+    depth, start = (d_ref[...] * m_ref[...]).astype(F32), sea * z_ref[...]
+    put(levels, depth, start, sea * f_ref[...], start)
+    put(levels + 1, depth, start, start, start)
+
+
+def corners_kernel(info_ref, a_ref, b_ref, q_in, r_in, g_ref, q_ref, r_ref):
+    del q_in, r_in
+    count = a_ref.shape[0]
+    lane = lanes()
+    is_even, is_top, odd_lon = info_ref[0], info_ref[1], info_ref[3] % 2
     from_north = lane % 16 >= 8
     flow_sign = jnp.where(group_of(lane) % 4 < 2, -1.0, 1.0).astype(F32)
-    odd_lon = jnp.full((8, 128), info_ref[3] % 2, jnp.int32) == 1
 
     @pl.when(is_even == 1)
     def _():
@@ -141,31 +164,23 @@
             turned = roll_lane(rows, 1)
             for i in range(1, 7):
                 turned = jnp.where(lane % 16 == 8 + i, roll_lane(rows, 1 + 2 * i), turned)
-            if j < levels // 2:
+            if j < count - 1:
                 turned = turned * flow_sign
             g_ref[j] = jnp.where(from_north, turned, a_ref[j])
 
-    def put(k, u, v, t, s):
-        g = g_ref[k // 2]
-        odd = k % 2
-        v4, t2, s6 = roll_sub(v, 4), roll_sub(t, 2), roll_sub(s, 6)
-        x = jnp.where((sub >= 4) & (sub <= 5), v4, u)
-        x = jnp.where(sub == 2, t2, x)
-        x = jnp.where(sub == 6, s6, x)
-        to_west = jnp.where(sub == 3, roll_sub(g, 3 - odd), x)
-        x = jnp.where((sub >= 2) & (sub <= 3), v4, u)
-        x = jnp.where(sub == 1, t2, x)
-        x = jnp.where(sub == 5, s6, x)
-        to_east = jnp.where(sub == 0, roll_sub(g, 1 + odd), x)
-        q_ref[k] = jnp.where(odd_lon, to_west, to_east)
-        r_ref[k] = jnp.where(odd_lon, to_east, to_west)
-
-    for k in range(levels):
-        put(k, u_ref[k], v_ref[k], t_ref[k], s_ref[k])
-    sea = m_ref[...].astype(F32)
-    depth, start = (d_ref[...] * m_ref[...]).astype(F32), sea * z_ref[...]
-    put(levels, depth, start, sea * f_ref[...], start)
-    put(levels + 1, depth, start, start, start)
+    def put(west_ref, east_ref):
+        for k in range(2 * count):
+            odd = k % 2
+            west_ref[k, 3:4, :] = g_ref[k // 2, odd : odd + 1, :]
+            east_ref[k, 0:1, :] = g_ref[k // 2, 7 - odd : 8 - odd, :]
+
+    @pl.when(odd_lon == 1)
+    def _():
+        put(q_ref, r_ref)
+
+    @pl.when(odd_lon == 0)
+    def _():
+        put(r_ref, q_ref)
 
 
 def lon_masks(info_ref):
@@ -422,7 +437,9 @@
     for r in residuals():
         r = r[GROUP : 2 * GROUP, 0:128]
         total = total + r * r
-    sum_ref[...] = jnp.sum(jnp.sum(total, axis=0, keepdims=True), axis=1, keepdims=True) + jnp.zeros((1, 128), F32)
+    total = jnp.sum(jnp.sum(total, axis=0, keepdims=True), axis=1, keepdims=True) + jnp.zeros((1, 128), F32)
+    for i in range(sum_ref.shape[0]):
+        sum_ref[i] = total
 
     both, x_e, x_w = found
     x, x_g = both[:, 0:128], both[:, 128:256]
@@ -446,7 +463,7 @@
         nv_ref[k] = jnp.where(wet, vs_ref[k] - slope_y, 0.0)
 
 
-def call(kernel, name, outs, in_specs, scratch=()):
+def call(kernel, name, outs, in_specs, scratch=(), aliases=None):
     return pl.pallas_call(
         kernel,
         name=name,
@@ -454,6 +471,7 @@
         in_specs=in_specs,
         out_specs=jax.tree.map(lambda _: VMEM, outs),
         scratch_shapes=list(scratch),
+        input_output_aliases=aliases or {},
         compiler_params=pltpu.CompilerParams(vmem_limit_bytes=48 << 20),
     )
 
@@ -501,9 +519,10 @@
         + [pltpu.SemaphoreType.DMA((8,))],
     )(*[pltpu.with_memory_space_constraint(x, pltpu.HBM) for x in own])
     got_a, got_b = lat_swap(edges)
-    ghost, pair_q, pair_r = call(lon_pack_kernel, "lon_pack", (packed, message, message), [SMEM] + [VMEM] * 10)(
-        info, *own, got_a, got_b
-    )
+    rows_q, rows_r = call(lon_rows_kernel, "lon_rows", (message, message), [SMEM] + [VMEM] * 8)(info, *own)
+    ghost, pair_q, pair_r = call(
+        corners_kernel, "corners", (packed, message, message), [SMEM] + [VMEM] * 4, aliases={3: 1, 4: 2}
+    )(info, got_a, got_b, rows_q, rows_r)
     pair_q = lax.ppermute(pair_q, LON, [(i, i ^ 1) for i in range(lon_size)])
     pair_r = lax.ppermute(pair_r, LON, [(i, (i + 1 if i % 2 else i - 1) % lon_size) for i in range(lon_size)])
     u_star, v_star, chunk, start = call(
@@ -518,14 +537,15 @@
         info, thickness, temp, salt, u, v, strata, sea, ghost, pair_q, pair_r, after
     )
     group_q, group_r, new_temp, new_salt = lax.optimization_barrier((group_q, group_r, new_temp, new_salt))
-    total, surface, slope = call(
+    sums, surface, slope = call(
         functools.partial(slab_kernel, levels),
         "slab",
-        (jax.ShapeDtypeStruct((1, 128), F32), jax.ShapeDtypeStruct((8, 128), F32), tiles(2)),
+        (jax.ShapeDtypeStruct((groups * lat_size, 1, 128), F32), jax.ShapeDtypeStruct((8, 128), F32), tiles(2)),
         [SMEM] + [VMEM] * 4,
         [pltpu.VMEM((8, 3 * GROUP, 256), F32)] * 6,
     )(info, group, group_q, group_r, start)
-    total = jnp.sum(from_all(total, ("lon_hi", "lat")), axis=0)
+    sums = lax.all_to_all(sums, ("lon_hi", "lat"), 0, 0, tiled=True)
+    total = jnp.sum(sums, axis=0)
     cells = lon_size * 8 * lat_size * 128
     rms = jnp.sqrt(total[0, 0] / cells + EPSILON)
     new_u, new_v = call(velocity_kernel, "velocity", (field, field), [VMEM] * 5)(u_star, v_star, strata, sea, slope)

time: 67.4 us -> 66.4 us (0.985)
    ppermute x1, waiting for transfers between devices: 1.73 us -> 0.53 us  [lat_swap(): lax.ppermute(x, (*LON, 'lat'), pairs_b)]
    pallas_call x1, Pallas kernels: 4.04 us -> 3.29 us  [per_device(): call(momentum_kernel, 'momentum', (field, field, tiles(3), tiles(3)), [SM...]
where the time goes in v4:
time: 66.4 us; the launch traced here: 66.1 us
  starting transfers between devices  29.7 us (45%)
  waiting for transfers between devices  13.2 us (20%)
  Pallas kernels  11.4 us (17%)
  blocking collectives  9.18 us (14%)
  between operations  2.01 us (3%)
  local copies, waits for them, and re-layouts  0.71 us (1%)
    ppermute x1, starting transfers between devices, per_device(): lax.ppermute(pair_r, LON, [(i, (i + 1 if i % 2 else i - 1) % lon_size) fo...  9.63 us
    all_to_all x1, blocking collectives, from_all(): return lax.all_to_all(copies, axes, 0, 0, tiled=True)  9.18 us
    all_to_all x1, starting transfers between devices, per_device(): sums = lax.all_to_all(sums, ('lon_hi', 'lat'), 0, 0, tiled=True)  8.02 us
    all_to_all x1, waiting for transfers between devices, per_device(): sums = lax.all_to_all(sums, ('lon_hi', 'lat'), 0, 0, tiled=True)  7.13 us
    ppermute x1, starting transfers between devices, per_device(): lax.ppermute(group, 'lon_hi', [(i, (i + 1 if i % 2 else i - 1) % groups)...  6.02 us
    ppermute x1, starting transfers between devices, lat_swap(): lax.ppermute(x, (*LON, 'lat'), pairs_b)  4.59 us
    ppermute x1, waiting for transfers between devices, per_device(): lax.ppermute(pair_r, LON, [(i, (i + 1 if i % 2 else i - 1) % lon_size) fo...  3.95 us
    pallas_call x1, Pallas kernels, per_device(): call(momentum_kernel, 'momentum', (field, field, tiles(3), tiles(3)), [SM...  3.29 us
  transfers between devices with their start and end apart: 7, of which 4 were waited for; matrix products, arithmetic and copies ran while one was open for 0% of the time, Pallas kernels for 5%

profile of v4, /device:TPU:1, one launch (start us, length us, event | category | flops | bytes accessed | tf_op | source)
XLA Modules:
  0.0 66.1 jit_solution(6932123793244705527)
XLA Ops:
  0.6 0.0 copy-start
  0.6 0.0 copy-start.1
  0.7 0.0 copy-start.2
  0.7 0.0 copy-start.3
  0.7 1.4 %lat_pack.1 = f32[17,8,128]{2,1,0:T(8,128)S(1)} custom-call(f32[32,8,128]{2,1,0:T(8,128)} %t_ref.5, f32[32,8,128]{2,1,0:T(8,128)} %s_ref.5, f32[32,8,128]{2,1,0:T(8,128)} %u_ref.5, f32[32,8,128]{2,1,0:T(8,128)} %v_ref.5, s32[8,128]{1,0:T(8,128)} %d_ref.7, s32[8,128]{1,0:T(8,128)} %m_ref.7, f32[8,128]{1,0:T(8,128)} %z_ref.3, f32[8,128]{1,0:T(8,128)} %f_ref.3), custom_call_target="tpu_custom_call" | custom-call | tf_op jit(solution)/shard_map/lat_pack/pallas_call | solution.py:511
  2.1 4.6 %collective-permute-start.1 = (f32[17,8,128]{2,1,0:T(8,128)S(1)}, f32[17,8,128]{2,1,0:T(8,128)S(1)}, u32[]{:S(2)}, u32[]{:S(2)}) collective-permute-start(f32[17,8,128]{2,1,0:T(8,128)S(1)} %lat_pack.1), channel_id=1, source_target_pairs={{1,2},{2,1},{3,255},{5,6},{6,5},{7,251},{9,10},{10,9},{11,247},{13... | collective-permute-start | bytes 208904 | tf_op jit(solution)/shard_map/ppermute | solution.py:502
  6.7 0.1 collective-permute-start
  6.8 0.0 copy-start.6
  6.8 0.0 copy-start.7
  6.9 0.0 copy-start.5
  6.9 0.0 copy-start.4
  6.9 0.1 stack.23.info_ref
  7.0 0.0 copy-done
  7.0 0.0 copy-done.1
  7.0 0.0 copy-done.2
  7.0 0.0 copy-done.3
  7.0 0.5 copy-done.6
  7.5 0.0 copy-done.7
  7.5 0.0 copy-done.5
  7.6 0.0 copy-done.4
  7.6 0.6 lon_rows.1
  8.2 0.5 collective-permute-done.1.b_ref
  8.7 0.0 collective-permute-done.a_ref
  8.7 0.6 corners.1
  9.3 1.3 %collective-permute-start.2 = (f32[34,8,128]{2,1,0:T(8,128)S(1)}, f32[34,8,128]{2,1,0:T(8,128)S(1)}, u32[]{:S(2)}, u32[]{:S(2)}) collective-permute-start(f32[34,8,128]{2,1,0:T(8,128)S(1)} %get-tuple-element.31), channel_id=1, source_target_pairs={{0,4},{4,0},{8,12},{12,8},{16,20},{20,16},{24,28},{28,24},{32,36},... | collective-permute-start | bytes 417800 | tf_op jit(solution)/shard_map/ppermute | solution.py:526
  10.6 0.0 copy-start.8
  10.6 9.6 %collective-permute-start.3 = (f32[34,8,128]{2,1,0:T(8,128)S(1)}, f32[34,8,128]{2,1,0:T(8,128)S(1)}, u32[]{:S(2)}, u32[]{:S(2)}) collective-permute-start(f32[34,8,128]{2,1,0:T(8,128)S(1)} %get-tuple-element.32), channel_id=1, source_target_pairs={{0,252},{4,8},{8,4},{12,16},{16,12},{20,24},{24,20},{28,32},{32,28... | collective-permute-start | bytes 417800 | tf_op jit(solution)/shard_map/ppermute | solution.py:527
  20.2 0.0 collective-permute-done.2.q_ref
  20.2 3.9 %collective-permute-done.3.r_ref = f32[34,8,128]{2,1,0:T(8,128)S(1)} collective-permute-done((f32[34,8,128]{2,1,0:T(8,128)S(1)}, f32[34,8,128]{2,1,0:T(8,128)S(1)}, u32[]{:S(2)}, u32[]{:S(2)}) %collective-permute-start.3) | collective-permute-done | bytes 139296 | tf_op jit(solution)/shard_map/ppermute | solution.py:527
  24.2 0.0 copy-done.8
  24.2 3.3 %momentum.1 = (f32[32,8,128]{2,1,0:T(8,128)S(1)}, f32[32,8,128]{2,1,0:T(8,128)S(1)}, f32[3,8,128]{2,1,0:T(8,128)S(1)}, f32[3,8,128]{2,1,0:T(8,128)S(1)}) custom-call(s32[6]{0:T(128)S(1)} %stack.23.info_ref, f32[32]{0:T(128)S(1)} %copy-done.8, f32[32,8,128]{2,1,0:T(8,128)S(1)} %copy-done, f32[32,8,128]{2,1,0:T(8,128)S(1)} %copy-done.1, ...), custom_call_target="tpu_custom_call" | custom-call | tf_op jit(solution)/shard_map/momentum/pallas_call | solution.py:528
  27.5 9.2 %all_to_all.10 = f32[8,3,8,128]{3,2,1,0:T(8,128)S(1)} all-to-all(f32[8,3,8,128]{3,2,1,0:T(8,128)S(1)} %broadcast_in_dim.2), channel_id=1, replica_groups=mesh['lon_hi'=8,'lon_lo'=8,'lat'=4] {'lon_lo'}, dimensions={0} | all-to-all | bytes 196608 | tf_op jit(solution)/shard_map/all_to_all | solution.py:484
  36.7 6.0 %collective-permute-start.5 = (f32[192,128]{1,0:T(8,128)S(1)}, f32[192,128]{1,0:T(8,128)S(1)}, u32[]{:S(2)}, u32[]{:S(2)}) collective-permute-start(f32[192,128]{1,0:T(8,128)S(1)} %bitcast.8), channel_id=1, source_target_pairs={{0,224},{32,64},{64,32},{96,128},{128,96},{160,192},{192,160},{224... | collective-permute-start | bytes 294920 | tf_op jit(solution)/shard_map/ppermute | solution.py:535
  42.7 0.0 collective-permute-start.4
  42.7 2.2 %tracers.1 = (f32[32,8,128]{2,1,0:T(8,128)}, f32[32,8,128]{2,1,0:T(8,128)}) custom-call(s32[6]{0:T(128)S(1)} %stack.23.info_ref, f32[32]{0:T(128)S(1)} %copy-done.8, f32[32,8,128]{2,1,0:T(8,128)S(1)} %copy-done, f32[32,8,128]{2,1,0:T(8,128)S(1)} %copy-done.1, f32[32,8,128]{2,1,0:T(8,128)S(1)} %copy-done.2, f32[32,8,128]{2,1,0:T(8,128)S(1)} %copy-done.3, ...), custom_call_target="tpu_custom_call" | custom-call | tf_op jit(solution)/shard_map/tracers/pallas_call | solution.py:536
  44.9 0.0 collective-permute-done.5.r_ref
  44.9 1.5 %collective-permute-done.4.q_ref = f32[192,128]{1,0:T(8,128)S(1)} collective-permute-done((f32[192,128]{1,0:T(8,128)S(1)}, f32[192,128]{1,0:T(8,128)S(1)}, u32[]{:S(2)}, u32[]{:S(2)}) %collective-permute-start.4) | collective-permute-done | bytes 98336 | tf_op jit(solution)/shard_map/ppermute | solution.py:534
  46.5 2.5 %slab.1 = (f32[32,1,128]{2,1,0:T(1,128)}, f32[8,128]{1,0:T(8,128)}, f32[2,8,128]{2,1,0:T(8,128)S(1)}) custom-call(s32[6]{0:T(128)S(1)} %stack.23.info_ref, f32[192,128]{1,0:T(8,128)S(1)} %bitcast.10, f32[192,128]{1,0:T(8,128)S(1)} %collective-permute-done.4.q_ref, f32[192,128]{1,0:T(8,128)S(1)} %collective-permute-done.5.r_ref, ...), custom_call_target="tpu_custom_call" | custom-call | tf_op jit(solution)/shard_map/slab/pallas_call | solution.py:540
  49.0 8.0 %all-to-all-start.1 = ((f32[32,1,128]{2,1,0:T(1,128)}), f32[32,1,128]{2,1,0:T(1,128)S(1)}, u32[]{:S(2)}, u32[]{:S(2)}) async-start(f32[32,1,128]{2,1,0:T(1,128)} %get-tuple-element.49), calls=%async_computation.1 | async-start | bytes 32768 | tf_op jit(solution)/shard_map/all_to_all | solution.py:547
  57.0 0.7 %velocity.1 = (f32[32,8,128]{2,1,0:T(8,128)}, f32[32,8,128]{2,1,0:T(8,128)}) custom-call(f32[32,8,128]{2,1,0:T(8,128)S(1)} %get-tuple-element.40.us_ref, f32[32,8,128]{2,1,0:T(8,128)S(1)} %get-tuple-element.41.vs_ref, s32[8,128]{1,0:T(8,128)S(1)} %copy-done.4, s32[8,128]{1,0:T(8,128)S(1)} %copy-done.5, f32[2,8,128]{2,1,0:T(8,128)S(1)} %get-tuple-element.45.slope_ref), custom_call_target="tpu_custom_call" | custom-call | tf_op jit(solution)/shard_map/velocity/pallas_call | solution.py:551
  57.7 7.1 %all-to-all-done.1 = f32[32,1,128]{2,1,0:T(1,128)S(1)} async-done(((f32[32,1,128]{2,1,0:T(1,128)}), f32[32,1,128]{2,1,0:T(1,128)S(1)}, u32[]{:S(2)}, u32[]{:S(2)}) %all-to-all-start.1) | async-done | bytes 16416 | tf_op jit(solution)/shard_map/all_to_all | solution.py:547
  64.8 0.1 reduce_sum.11
  (1 shorter events, 0.0 us)
Async XLA Ops:
  0.6 6.3 %copy-start = (f32[32,8,128]{2,1,0:T(8,128)S(1)}, f32[32,8,128]{2,1,0:T(8,128)}, u32[]{:S(2)}) copy-start(f32[32,8,128]{2,1,0:T(8,128)} %t_ref.5) | copy-start | bytes 393220
  0.6 6.3 %copy-start.1 = (f32[32,8,128]{2,1,0:T(8,128)S(1)}, f32[32,8,128]{2,1,0:T(8,128)}, u32[]{:S(2)}) copy-start(f32[32,8,128]{2,1,0:T(8,128)} %s_ref.5) | copy-start | bytes 393220
  0.7 6.3 %copy-start.2 = (f32[32,8,128]{2,1,0:T(8,128)S(1)}, f32[32,8,128]{2,1,0:T(8,128)}, u32[]{:S(2)}) copy-start(f32[32,8,128]{2,1,0:T(8,128)} %u_ref.5) | copy-start | bytes 393220
  0.7 6.3 %copy-start.3 = (f32[32,8,128]{2,1,0:T(8,128)S(1)}, f32[32,8,128]{2,1,0:T(8,128)}, u32[]{:S(2)}) copy-start(f32[32,8,128]{2,1,0:T(8,128)} %v_ref.5) | copy-start | bytes 393220
  2.1 6.6 %collective-permute-start.1 = (f32[17,8,128]{2,1,0:T(8,128)S(1)}, f32[17,8,128]{2,1,0:T(8,128)S(1)}, u32[]{:S(2)}, u32[]{:S(2)}) collective-permute-start(f32[17,8,128]{2,1,0:T(8,128)S(1)} %lat_pack.1), channel_id=1, source_target_pairs={{1,2},{2,1},{3,255},{5,6},{6,5},{7,251},{9,10},{10,9},{11,247},{13... | collective-permute-start | bytes 208904 | tf_op jit(solution)/shard_map/ppermute | solution.py:502
  6.7 2.0 %collective-permute-start = (f32[17,8,128]{2,1,0:T(8,128)S(1)}, f32[17,8,128]{2,1,0:T(8,128)S(1)}, u32[]{:S(2)}, u32[]{:S(2)}) collective-permute-start(f32[17,8,128]{2,1,0:T(8,128)S(1)} %lat_pack.1), channel_id=1, source_target_pairs={{0,1},{1,0},{2,3},{3,2},{4,5},{5,4},{6,7},{7,6},{8,9},{9,8},{10,11... | collective-permute-start | bytes 208904 | tf_op jit(solution)/shard_map/ppermute | solution.py:502
  6.8 0.7 %copy-start.6 = (f32[8,128]{1,0:T(8,128)S(1)}, f32[8,128]{1,0:T(8,128)}, u32[]{:S(2)}) copy-start(f32[8,128]{1,0:T(8,128)} %z_ref.3) | copy-start | bytes 12292
  6.8 0.7 %copy-start.7 = (f32[8,128]{1,0:T(8,128)S(1)}, f32[8,128]{1,0:T(8,128)}, u32[]{:S(2)}) copy-start(f32[8,128]{1,0:T(8,128)} %f_ref.3) | copy-start | bytes 12292
  6.9 0.7 %copy-start.5 = (s32[8,128]{1,0:T(8,128)S(1)}, s32[8,128]{1,0:T(8,128)}, u32[]{:S(2)}) copy-start(s32[8,128]{1,0:T(8,128)} %m_ref.7) | copy-start | bytes 12292
  6.9 0.7 %copy-start.4 = (s32[8,128]{1,0:T(8,128)S(1)}, s32[8,128]{1,0:T(8,128)}, u32[]{:S(2)}) copy-start(s32[8,128]{1,0:T(8,128)} %d_ref.7) | copy-start | bytes 12292
  9.3 10.9 %collective-permute-start.2 = (f32[34,8,128]{2,1,0:T(8,128)S(1)}, f32[34,8,128]{2,1,0:T(8,128)S(1)}, u32[]{:S(2)}, u32[]{:S(2)}) collective-permute-start(f32[34,8,128]{2,1,0:T(8,128)S(1)} %get-tuple-element.31), channel_id=1, source_target_pairs={{0,4},{4,0},{8,12},{12,8},{16,20},{20,16},{24,28},{28,24},{32,36},... | collective-permute-start | bytes 417800 | tf_op jit(solution)/shard_map/ppermute | solution.py:526
  10.6 13.6 %copy-start.8 = (f32[32]{0:T(128)S(1)}, f32[32]{0:T(128)}, u32[]{:S(2)}) copy-start(f32[32]{0:T(128)} %th_ref.3) | copy-start | bytes 388
  10.6 13.6 %collective-permute-start.3 = (f32[34,8,128]{2,1,0:T(8,128)S(1)}, f32[34,8,128]{2,1,0:T(8,128)S(1)}, u32[]{:S(2)}, u32[]{:S(2)}) collective-permute-start(f32[34,8,128]{2,1,0:T(8,128)S(1)} %get-tuple-element.32), channel_id=1, source_target_pairs={{0,252},{4,8},{8,4},{12,16},{16,12},{20,24},{24,20},{28,32},{32,28... | collective-permute-start | bytes 417800 | tf_op jit(solution)/shard_map/ppermute | solution.py:527
  36.7 8.2 %collective-permute-start.5 = (f32[192,128]{1,0:T(8,128)S(1)}, f32[192,128]{1,0:T(8,128)S(1)}, u32[]{:S(2)}, u32[]{:S(2)}) collective-permute-start(f32[192,128]{1,0:T(8,128)S(1)} %bitcast.8), channel_id=1, source_target_pairs={{0,224},{32,64},{64,32},{96,128},{128,96},{160,192},{192,160},{224... | collective-permute-start | bytes 294920 | tf_op jit(solution)/shard_map/ppermute | solution.py:535
  42.7 3.8 %collective-permute-start.4 = (f32[192,128]{1,0:T(8,128)S(1)}, f32[192,128]{1,0:T(8,128)S(1)}, u32[]{:S(2)}, u32[]{:S(2)}) collective-permute-start(f32[192,128]{1,0:T(8,128)S(1)} %bitcast.9), channel_id=1, source_target_pairs={{0,32},{32,0},{64,96},{96,64},{128,160},{160,128},{192,224},{224,1... | collective-permute-start | bytes 294920 | tf_op jit(solution)/shard_map/ppermute | solution.py:534
  49.0 15.9 %all-to-all-start.1 = ((f32[32,1,128]{2,1,0:T(1,128)}), f32[32,1,128]{2,1,0:T(1,128)S(1)}, u32[]{:S(2)}, u32[]{:S(2)}) async-start(f32[32,1,128]{2,1,0:T(1,128)} %get-tuple-element.49), calls=%async_computation.1 | async-start | bytes 32768 | tf_op jit(solution)/shard_map/all_to_all | solution.py:547

commit v5 on v4

--- a/solution.py
+++ b/solution.py
@@ -88,14 +88,14 @@
 
 def lat_pack_kernel(t_hbm, s_hbm, u_hbm, v_hbm, d_hbm, m_hbm, z_hbm, f_hbm, out_ref, t_ref, s_ref, u_ref, v_ref, d_ref, m_ref, z_ref, f_ref, sem):
     levels = t_ref.shape[0]
-    pairs = (
-        (t_hbm, t_ref), (s_hbm, s_ref), (u_hbm, u_ref), (v_hbm, v_ref), (d_hbm, d_ref), (m_hbm, m_ref), (z_hbm, z_ref), (f_hbm, f_ref),
-    )
-    copies = [pltpu.make_async_copy(src, dst, sem.at[i]) for i, (src, dst) in enumerate(pairs)]
-    for copy in copies:
-        copy.start()
-    for copy in copies:
-        copy.wait()
+    half = levels // 2
+    fields = ((t_hbm, t_ref), (s_hbm, s_ref), (u_hbm, u_ref), (v_hbm, v_ref))
+    parts = [[(src.at[i : i + half], dst.at[i : i + half]) for src, dst in fields] for i in (0, half)]
+    parts.append([(d_hbm, d_ref), (m_hbm, m_ref), (z_hbm, z_ref), (f_hbm, f_ref)])
+    copies = [[pltpu.make_async_copy(*p, sem.at[i, j]) for j, p in enumerate(part)] for i, part in enumerate(parts)]
+    for part in copies:
+        for copy in part:
+            copy.start()
     group = group_of(lanes())
 
     def put(out, fields, odd):
@@ -105,11 +105,16 @@
 
     zero = jnp.zeros((8, 128), F32)
     for j in range(levels // 2):
+        if j % (half // 2) == 0:
+            for copy in copies[j // (half // 2)]:
+                copy.wait()
         out = zero
         for odd in range(2):
             k = 2 * j + odd
             out = put(out, (u_ref[k], v_ref[k], t_ref[k], s_ref[k]), odd)
         out_ref[j] = out
+    for copy in copies[2]:
+        copy.wait()
     sea = m_ref[...].astype(F32)
     depth = (d_ref[...] * m_ref[...]).astype(F32)
     out_ref[levels // 2] = put(zero, (depth, sea * z_ref[...], sea * f_ref[...]), 0)
@@ -139,7 +144,14 @@
     put(levels + 1, depth, start, start, start)
 
 
-def corners_kernel(info_ref, a_ref, b_ref, q_in, r_in, g_ref, q_ref, r_ref):
+def turn_rows(x):
+    sub = subs()
+    x = roll_sub(x, 4)
+    x = jnp.where(sub // 2 % 2 == 0, roll_sub(x, -2), roll_sub(x, 2))
+    return jnp.where(sub % 2 == 0, roll_sub(x, -1), roll_sub(x, 1))
+
+
+def corners_kernel(info_ref, a_ref, b_ref, r_in, q_in, g_ref, r_ref, q_ref):
     del q_in, r_in
     count = a_ref.shape[0]
     lane = lanes()
@@ -160,7 +172,7 @@
     @pl.when(is_top == 1)
     def _():
         for j in range(count):
-            rows = jnp.concatenate([b_ref[j, 7 - i : 8 - i, :] for i in range(8)], axis=0)
+            rows = turn_rows(b_ref[j])
             turned = roll_lane(rows, 1)
             for i in range(1, 7):
                 turned = jnp.where(lane % 16 == 8 + i, roll_lane(rows, 1 + 2 * i), turned)
@@ -230,7 +242,7 @@
 
 
 def momentum_kernel(
-    info_ref, th_ref, t_ref, s_ref, u_ref, v_ref, d_ref, m_ref, z_ref, f_ref, g_ref, q_ref, r_ref, us_ref, vs_ref, chunk_ref, st_ref
+    info_ref, th_ref, t_ref, s_ref, u_ref, v_ref, d_ref, m_ref, z_ref, f_ref, g_ref, r_ref, q_ref, us_ref, vs_ref, chunk_ref, st_ref
 ):
     levels = t_ref.shape[0]
     lane, sub = lanes(), subs()
@@ -365,7 +377,7 @@
     lax.fori_loop(0, levels // 2 // TILES_PER_STEP, step, (zero, zero))
 
 
-def slab_kernel(levels, info_ref, own_ref, q_ref, r_ref, st_ref, sum_ref, surf_ref, slope_ref, we_s, wn_s, fac_s, inv_s, r_s, d_s):
+def slab_kernel(levels, info_ref, own_ref, q_ref, r_ref, st_ref, sum_ref, surf_ref, slope_ref, we_s, wn_s, fac_s, inv_s, r_s, d_s, z_s):
     odd_group = jnp.full((GROUP, 128), info_ref[3] // GROUP % 2, jnp.int32) == 1
 
     def rows(i):
@@ -423,15 +435,15 @@
         x = None
         for p in range(7, -1, -1):
             x = y[p] if x is None else y[p] - fac_s[p] * x
-            d_s[p] = x * scale_new if first else scale_old * d_s[p] + scale_new * x
-        own = jnp.concatenate([d_s[p, pl.ds(here, 1), :] for p in range(8)], axis=0)
-        return own, d_s[0, pl.ds(right, 1), :], d_s[7, pl.ds(left, 1), :]
-
-    found = step(0.0, 1.0 / mid, True)
+            d = x * scale_new if first else scale_old * d_s[p] + scale_new * x
+            d_s[p] = d
+            z_s[p] = d if first else z_s[p] + d
+
+    step(0.0, 1.0 / mid, True)
     rho = 1.0 / ratio
     for _ in range(ITERS - 1):
         rho_next = 1.0 / (2.0 * ratio - rho)
-        found = [a + b for a, b in zip(found, step(rho_next * rho, 2.0 * rho_next / half, False))]
+        step(rho_next * rho, 2.0 * rho_next / half, False)
         rho = rho_next
     total = jnp.zeros((GROUP, 128), F32)
     for r in residuals():
@@ -441,7 +453,8 @@
     for i in range(sum_ref.shape[0]):
         sum_ref[i] = total
 
-    both, x_e, x_w = found
+    both = jnp.concatenate([z_s[p, pl.ds(here, 1), :] for p in range(8)], axis=0)
+    x_e, x_w = z_s[0, pl.ds(right, 1), :], z_s[7, pl.ds(left, 1), :]
     x, x_g = both[:, 0:128], both[:, 128:256]
     sub = subs()
     x_e = jnp.broadcast_to(x_e[:, 0:128], (8, 128))
@@ -516,18 +529,18 @@
         [pltpu.VMEM(field.shape, F32)] * 4
         + [pltpu.VMEM(flat, jnp.int32)] * 2
         + [pltpu.VMEM(flat, F32)] * 2
-        + [pltpu.SemaphoreType.DMA((8,))],
+        + [pltpu.SemaphoreType.DMA((3, 4))],
     )(*[pltpu.with_memory_space_constraint(x, pltpu.HBM) for x in own])
     got_a, got_b = lat_swap(edges)
     rows_q, rows_r = call(lon_rows_kernel, "lon_rows", (message, message), [SMEM] + [VMEM] * 8)(info, *own)
-    ghost, pair_q, pair_r = call(
+    ghost, pair_r, pair_q = call(
         corners_kernel, "corners", (packed, message, message), [SMEM] + [VMEM] * 4, aliases={3: 1, 4: 2}
-    )(info, got_a, got_b, rows_q, rows_r)
+    )(info, got_a, got_b, rows_r, rows_q)
+    pair_r = lax.ppermute(pair_r, LON, [(i, (i + 1 if i % 2 else i - 1) % lon_size) for i in range(lon_size)])
     pair_q = lax.ppermute(pair_q, LON, [(i, i ^ 1) for i in range(lon_size)])
-    pair_r = lax.ppermute(pair_r, LON, [(i, (i + 1 if i % 2 else i - 1) % lon_size) for i in range(lon_size)])
     u_star, v_star, chunk, start = call(
         momentum_kernel, "momentum", (field, field, tiles(3), tiles(3)), [SMEM, SMEM] + [VMEM] * 11
-    )(info, thickness, *own, ghost, pair_q, pair_r)
+    )(info, thickness, *own, ghost, pair_r, pair_q)
     group = from_all(chunk, ("lon_lo",)).reshape(GROUP * 24, 128)
     group, after = lax.optimization_barrier((group, chunk))
     groups = lon_size // GROUP
@@ -542,7 +555,7 @@
         "slab",
         (jax.ShapeDtypeStruct((groups * lat_size, 1, 128), F32), jax.ShapeDtypeStruct((8, 128), F32), tiles(2)),
         [SMEM] + [VMEM] * 4,
-        [pltpu.VMEM((8, 3 * GROUP, 256), F32)] * 6,
+        [pltpu.VMEM((8, 3 * GROUP, 256), F32)] * 7,
     )(info, group, group_q, group_r, start)
     sums = lax.all_to_all(sums, ("lon_hi", "lat"), 0, 0, tiled=True)
     total = jnp.sum(sums, axis=0)

time: 66.4 us -> 65.5 us (0.986)
  starting transfers between devices: 29.7 us -> 27.6 us
  waiting for transfers between devices: 13.2 us -> 14.4 us
    ppermute x1, starting transfers between devices: 1.3 us -> 0.01 us  [per_device(): pair_q = lax.ppermute(pair_q, LON, [(i, i ^ 1) for i in range(lon_size)])]
    ppermute x1, starting transfers between devices: 6.02 us -> 4.9 us  [per_device(): lax.ppermute(group, 'lon_hi', [(i, (i + 1 if i % 2 else i - 1) % groups)...]
    ppermute x1, waiting for transfers between devices: 0.01 us -> 1.06 us  [per_device(): pair_q = lax.ppermute(pair_q, LON, [(i, i ^ 1) for i in range(lon_size)])]
    ppermute x1, starting transfers between devices: 9.63 us -> 10.4 us  [per_device(): lax.ppermute(pair_r, LON, [(i, (i + 1 if i % 2 else i - 1) % lon_size) fo...]
  transfers between devices with their start and end apart: 7 -> 7, of which waited for: 4 -> 5; matrix products, arithmetic and copies ran while one was open for 0% -> 0% of each run, Pallas kernels for 5% -> 5%
where the time goes in v5:
time: 65.5 us; the launch traced here: 65.3 us
  starting transfers between devices  27.6 us (42%)
  waiting for transfers between devices  14.4 us (22%)
  Pallas kernels  11.3 us (17%)
  blocking collectives  9.18 us (14%)
  between operations  2.01 us (3%)
  local copies, waits for them, and re-layouts  0.71 us (1%)
    ppermute x1, starting transfers between devices, per_device(): lax.ppermute(pair_r, LON, [(i, (i + 1 if i % 2 else i - 1) % lon_size) fo...  10.4 us
    all_to_all x1, blocking collectives, from_all(): return lax.all_to_all(copies, axes, 0, 0, tiled=True)  9.18 us
    all_to_all x1, starting transfers between devices, per_device(): sums = lax.all_to_all(sums, ('lon_hi', 'lat'), 0, 0, tiled=True)  7.66 us
    all_to_all x1, waiting for transfers between devices, per_device(): sums = lax.all_to_all(sums, ('lon_hi', 'lat'), 0, 0, tiled=True)  7.13 us
    ppermute x1, starting transfers between devices, per_device(): lax.ppermute(group, 'lon_hi', [(i, (i + 1 if i % 2 else i - 1) % groups)...  4.9 us
    ppermute x1, starting transfers between devices, lat_swap(): lax.ppermute(x, (*LON, 'lat'), pairs_b)  4.59 us
    ppermute x1, waiting for transfers between devices, per_device(): lax.ppermute(pair_r, LON, [(i, (i + 1 if i % 2 else i - 1) % lon_size) fo...  4.18 us
    pallas_call x1, Pallas kernels, per_device(): call(momentum_kernel, 'momentum', (field, field, tiles(3), tiles(3)), [SM...  3.29 us
  transfers between devices with their start and end apart: 7, of which 5 were waited for; matrix products, arithmetic and copies ran while one was open for 0% of the time, Pallas kernels for 5%

profile of v5, /device:TPU:1, one launch (start us, length us, event | category | flops | bytes accessed | tf_op | source)
XLA Modules:
  0.0 65.3 jit_solution(16212129294210656644)
XLA Ops:
  0.6 0.0 copy-start
  0.6 0.0 copy-start.1
  0.7 0.0 copy-start.2
  0.7 0.0 copy-start.3
  0.7 1.5 %lat_pack.1 = f32[17,8,128]{2,1,0:T(8,128)S(1)} custom-call(f32[32,8,128]{2,1,0:T(8,128)} %t_ref.5, f32[32,8,128]{2,1,0:T(8,128)} %s_ref.5, f32[32,8,128]{2,1,0:T(8,128)} %u_ref.5, f32[32,8,128]{2,1,0:T(8,128)} %v_ref.5, s32[8,128]{1,0:T(8,128)} %d_ref.7, s32[8,128]{1,0:T(8,128)} %m_ref.7, f32[8,128]{1,0:T(8,128)} %z_ref.3, f32[8,128]{1,0:T(8,128)} %f_ref.3), custom_call_target="tpu_custom_call" | custom-call | tf_op jit(solution)/shard_map/lat_pack/pallas_call | solution.py:524
  2.1 4.6 %collective-permute-start.1 = (f32[17,8,128]{2,1,0:T(8,128)S(1)}, f32[17,8,128]{2,1,0:T(8,128)S(1)}, u32[]{:S(2)}, u32[]{:S(2)}) collective-permute-start(f32[17,8,128]{2,1,0:T(8,128)S(1)} %lat_pack.1), channel_id=1, source_target_pairs={{1,2},{2,1},{3,255},{5,6},{6,5},{7,251},{9,10},{10,9},{11,247},{13... | collective-permute-start | bytes 208904 | tf_op jit(solution)/shard_map/ppermute | solution.py:515
  6.7 0.1 collective-permute-start
  6.8 0.0 copy-start.6
  6.9 0.0 copy-start.7
  6.9 0.0 copy-start.5
  6.9 0.0 copy-start.4
  6.9 0.1 stack.23.info_ref
  7.0 0.0 copy-done
  7.0 0.0 copy-done.1
  7.0 0.0 copy-done.2
  7.0 0.0 copy-done.3
  7.0 0.5 copy-done.6
  7.5 0.0 copy-done.7
  7.6 0.0 copy-done.5
  7.6 0.0 copy-done.4
  7.6 0.6 lon_rows.1
  8.2 0.5 collective-permute-done.1.b_ref
  8.7 0.0 collective-permute-done.a_ref
  8.7 0.6 corners.1
  9.3 10.4 %collective-permute-start.2 = (f32[34,8,128]{2,1,0:T(8,128)S(1)}, f32[34,8,128]{2,1,0:T(8,128)S(1)}, u32[]{:S(2)}, u32[]{:S(2)}) collective-permute-start(f32[34,8,128]{2,1,0:T(8,128)S(1)} %get-tuple-element.31), channel_id=1, source_target_pairs={{0,252},{4,8},{8,4},{12,16},{16,12},{20,24},{24,20},{28,32},{32,28... | collective-permute-start | bytes 417800 | tf_op jit(solution)/shard_map/ppermute | solution.py:539
  19.7 0.0 copy-start.8
  19.7 0.0 collective-permute-start.3
  19.7 4.2 %collective-permute-done.2.r_ref = f32[34,8,128]{2,1,0:T(8,128)S(1)} collective-permute-done((f32[34,8,128]{2,1,0:T(8,128)S(1)}, f32[34,8,128]{2,1,0:T(8,128)S(1)}, u32[]{:S(2)}, u32[]{:S(2)}) %collective-permute-start.2) | collective-permute-done | bytes 139296 | tf_op jit(solution)/shard_map/ppermute | solution.py:539
  23.9 1.1 %collective-permute-done.3.q_ref = f32[34,8,128]{2,1,0:T(8,128)S(1)} collective-permute-done((f32[34,8,128]{2,1,0:T(8,128)S(1)}, f32[34,8,128]{2,1,0:T(8,128)S(1)}, u32[]{:S(2)}, u32[]{:S(2)}) %collective-permute-start.3) | collective-permute-done | bytes 139296 | tf_op jit(solution)/shard_map/ppermute | solution.py:540
  24.9 0.0 copy-done.8
  24.9 3.3 %momentum.1 = (f32[32,8,128]{2,1,0:T(8,128)S(1)}, f32[32,8,128]{2,1,0:T(8,128)S(1)}, f32[3,8,128]{2,1,0:T(8,128)S(1)}, f32[3,8,128]{2,1,0:T(8,128)S(1)}) custom-call(s32[6]{0:T(128)S(1)} %stack.23.info_ref, f32[32]{0:T(128)S(1)} %copy-done.8, f32[32,8,128]{2,1,0:T(8,128)S(1)} %copy-done, f32[32,8,128]{2,1,0:T(8,128)S(1)} %copy-done.1, ...), custom_call_target="tpu_custom_call" | custom-call | tf_op jit(solution)/shard_map/momentum/pallas_call | solution.py:541
  28.3 9.2 %all_to_all.10 = f32[8,3,8,128]{3,2,1,0:T(8,128)S(1)} all-to-all(f32[8,3,8,128]{3,2,1,0:T(8,128)S(1)} %broadcast_in_dim.2), channel_id=1, replica_groups=mesh['lon_hi'=8,'lon_lo'=8,'lat'=4] {'lon_lo'}, dimensions={0} | all-to-all | bytes 196608 | tf_op jit(solution)/shard_map/all_to_all | solution.py:497
  37.4 4.9 %collective-permute-start.5 = (f32[192,128]{1,0:T(8,128)S(1)}, f32[192,128]{1,0:T(8,128)S(1)}, u32[]{:S(2)}, u32[]{:S(2)}) collective-permute-start(f32[192,128]{1,0:T(8,128)S(1)} %bitcast.8), channel_id=1, source_target_pairs={{0,224},{32,64},{64,32},{96,128},{128,96},{160,192},{192,160},{224... | collective-permute-start | bytes 294920 | tf_op jit(solution)/shard_map/ppermute | solution.py:548
  42.3 0.0 collective-permute-start.4
  42.3 2.2 %tracers.1 = (f32[32,8,128]{2,1,0:T(8,128)}, f32[32,8,128]{2,1,0:T(8,128)}) custom-call(s32[6]{0:T(128)S(1)} %stack.23.info_ref, f32[32]{0:T(128)S(1)} %copy-done.8, f32[32,8,128]{2,1,0:T(8,128)S(1)} %copy-done, f32[32,8,128]{2,1,0:T(8,128)S(1)} %copy-done.1, f32[32,8,128]{2,1,0:T(8,128)S(1)} %copy-done.2, f32[32,8,128]{2,1,0:T(8,128)S(1)} %copy-done.3, ...), custom_call_target="tpu_custom_call" | custom-call | tf_op jit(solution)/shard_map/tracers/pallas_call | solution.py:549
  44.6 0.0 collective-permute-done.5.r_ref
  44.6 1.5 %collective-permute-done.4.q_ref = f32[192,128]{1,0:T(8,128)S(1)} collective-permute-done((f32[192,128]{1,0:T(8,128)S(1)}, f32[192,128]{1,0:T(8,128)S(1)}, u32[]{:S(2)}, u32[]{:S(2)}) %collective-permute-start.4) | collective-permute-done | bytes 98336 | tf_op jit(solution)/shard_map/ppermute | solution.py:547
  46.1 2.4 %slab.1 = (f32[32,1,128]{2,1,0:T(1,128)}, f32[8,128]{1,0:T(8,128)}, f32[2,8,128]{2,1,0:T(8,128)S(1)}) custom-call(s32[6]{0:T(128)S(1)} %stack.23.info_ref, f32[192,128]{1,0:T(8,128)S(1)} %bitcast.10, f32[192,128]{1,0:T(8,128)S(1)} %collective-permute-done.4.q_ref, f32[192,128]{1,0:T(8,128)S(1)} %collective-permute-done.5.r_ref, ...), custom_call_target="tpu_custom_call" | custom-call | tf_op jit(solution)/shard_map/slab/pallas_call | solution.py:553
  48.5 7.7 %all-to-all-start.1 = ((f32[32,1,128]{2,1,0:T(1,128)}), f32[32,1,128]{2,1,0:T(1,128)S(1)}, u32[]{:S(2)}, u32[]{:S(2)}) async-start(f32[32,1,128]{2,1,0:T(1,128)} %get-tuple-element.49), calls=%async_computation.1 | async-start | bytes 32768 | tf_op jit(solution)/shard_map/all_to_all | solution.py:560
  56.2 0.7 %velocity.1 = (f32[32,8,128]{2,1,0:T(8,128)}, f32[32,8,128]{2,1,0:T(8,128)}) custom-call(f32[32,8,128]{2,1,0:T(8,128)S(1)} %get-tuple-element.40.us_ref, f32[32,8,128]{2,1,0:T(8,128)S(1)} %get-tuple-element.41.vs_ref, s32[8,128]{1,0:T(8,128)S(1)} %copy-done.4, s32[8,128]{1,0:T(8,128)S(1)} %copy-done.5, f32[2,8,128]{2,1,0:T(8,128)S(1)} %get-tuple-element.45.slope_ref), custom_call_target="tpu_custom_call" | custom-call | tf_op jit(solution)/shard_map/velocity/pallas_call | solution.py:564
  56.9 7.1 %all-to-all-done.1 = f32[32,1,128]{2,1,0:T(1,128)S(1)} async-done(((f32[32,1,128]{2,1,0:T(1,128)}), f32[32,1,128]{2,1,0:T(1,128)S(1)}, u32[]{:S(2)}, u32[]{:S(2)}) %all-to-all-start.1) | async-done | bytes 16416 | tf_op jit(solution)/shard_map/all_to_all | solution.py:560
  64.0 0.1 reduce_sum.11
  (1 shorter events, 0.0 us)
Async XLA Ops:
  0.6 6.4 %copy-start = (f32[32,8,128]{2,1,0:T(8,128)S(1)}, f32[32,8,128]{2,1,0:T(8,128)}, u32[]{:S(2)}) copy-start(f32[32,8,128]{2,1,0:T(8,128)} %t_ref.5) | copy-start | bytes 393220
  0.6 6.3 %copy-start.1 = (f32[32,8,128]{2,1,0:T(8,128)S(1)}, f32[32,8,128]{2,1,0:T(8,128)}, u32[]{:S(2)}) copy-start(f32[32,8,128]{2,1,0:T(8,128)} %s_ref.5) | copy-start | bytes 393220
  0.7 6.3 %copy-start.2 = (f32[32,8,128]{2,1,0:T(8,128)S(1)}, f32[32,8,128]{2,1,0:T(8,128)}, u32[]{:S(2)}) copy-start(f32[32,8,128]{2,1,0:T(8,128)} %u_ref.5) | copy-start | bytes 393220
  0.7 6.3 %copy-start.3 = (f32[32,8,128]{2,1,0:T(8,128)S(1)}, f32[32,8,128]{2,1,0:T(8,128)}, u32[]{:S(2)}) copy-start(f32[32,8,128]{2,1,0:T(8,128)} %v_ref.5) | copy-start | bytes 393220
  2.1 6.6 %collective-permute-start.1 = (f32[17,8,128]{2,1,0:T(8,128)S(1)}, f32[17,8,128]{2,1,0:T(8,128)S(1)}, u32[]{:S(2)}, u32[]{:S(2)}) collective-permute-start(f32[17,8,128]{2,1,0:T(8,128)S(1)} %lat_pack.1), channel_id=1, source_target_pairs={{1,2},{2,1},{3,255},{5,6},{6,5},{7,251},{9,10},{10,9},{11,247},{13... | collective-permute-start | bytes 208904 | tf_op jit(solution)/shard_map/ppermute | solution.py:515
  6.7 2.0 %collective-permute-start = (f32[17,8,128]{2,1,0:T(8,128)S(1)}, f32[17,8,128]{2,1,0:T(8,128)S(1)}, u32[]{:S(2)}, u32[]{:S(2)}) collective-permute-start(f32[17,8,128]{2,1,0:T(8,128)S(1)} %lat_pack.1), channel_id=1, source_target_pairs={{0,1},{1,0},{2,3},{3,2},{4,5},{5,4},{6,7},{7,6},{8,9},{9,8},{10,11... | collective-permute-start | bytes 208904 | tf_op jit(solution)/shard_map/ppermute | solution.py:515
  6.8 0.7 %copy-start.6 = (f32[8,128]{1,0:T(8,128)S(1)}, f32[8,128]{1,0:T(8,128)}, u32[]{:S(2)}) copy-start(f32[8,128]{1,0:T(8,128)} %z_ref.3) | copy-start | bytes 12292
  6.9 0.7 %copy-start.7 = (f32[8,128]{1,0:T(8,128)S(1)}, f32[8,128]{1,0:T(8,128)}, u32[]{:S(2)}) copy-start(f32[8,128]{1,0:T(8,128)} %f_ref.3) | copy-start | bytes 12292
  6.9 0.7 %copy-start.5 = (s32[8,128]{1,0:T(8,128)S(1)}, s32[8,128]{1,0:T(8,128)}, u32[]{:S(2)}) copy-start(s32[8,128]{1,0:T(8,128)} %m_ref.7) | copy-start | bytes 12292
  6.9 0.7 %copy-start.4 = (s32[8,128]{1,0:T(8,128)S(1)}, s32[8,128]{1,0:T(8,128)}, u32[]{:S(2)}) copy-start(s32[8,128]{1,0:T(8,128)} %d_ref.7) | copy-start | bytes 12292
  9.3 14.6 %collective-permute-start.2 = (f32[34,8,128]{2,1,0:T(8,128)S(1)}, f32[34,8,128]{2,1,0:T(8,128)S(1)}, u32[]{:S(2)}, u32[]{:S(2)}) collective-permute-start(f32[34,8,128]{2,1,0:T(8,128)S(1)} %get-tuple-element.31), channel_id=1, source_target_pairs={{0,252},{4,8},{8,4},{12,16},{16,12},{20,24},{24,20},{28,32},{32,28... | collective-permute-start | bytes 417800 | tf_op jit(solution)/shard_map/ppermute | solution.py:539
  19.7 5.3 %copy-start.8 = (f32[32]{0:T(128)S(1)}, f32[32]{0:T(128)}, u32[]{:S(2)}) copy-start(f32[32]{0:T(128)} %th_ref.3) | copy-start | bytes 388
  19.7 5.3 %collective-permute-start.3 = (f32[34,8,128]{2,1,0:T(8,128)S(1)}, f32[34,8,128]{2,1,0:T(8,128)S(1)}, u32[]{:S(2)}, u32[]{:S(2)}) collective-permute-start(f32[34,8,128]{2,1,0:T(8,128)S(1)} %get-tuple-element.32), channel_id=1, source_target_pairs={{0,4},{4,0},{8,12},{12,8},{16,20},{20,16},{24,28},{28,24},{32,36},... | collective-permute-start | bytes 417800 | tf_op jit(solution)/shard_map/ppermute | solution.py:540
  37.4 7.1 %collective-permute-start.5 = (f32[192,128]{1,0:T(8,128)S(1)}, f32[192,128]{1,0:T(8,128)S(1)}, u32[]{:S(2)}, u32[]{:S(2)}) collective-permute-start(f32[192,128]{1,0:T(8,128)S(1)} %bitcast.8), channel_id=1, source_target_pairs={{0,224},{32,64},{64,32},{96,128},{128,96},{160,192},{192,160},{224... | collective-permute-start | bytes 294920 | tf_op jit(solution)/shard_map/ppermute | solution.py:548
  42.3 3.8 %collective-permute-start.4 = (f32[192,128]{1,0:T(8,128)S(1)}, f32[192,128]{1,0:T(8,128)S(1)}, u32[]{:S(2)}, u32[]{:S(2)}) collective-permute-start(f32[192,128]{1,0:T(8,128)S(1)} %bitcast.9), channel_id=1, source_target_pairs={{0,32},{32,0},{64,96},{96,64},{128,160},{160,128},{192,224},{224,1... | collective-permute-start | bytes 294920 | tf_op jit(solution)/shard_map/ppermute | solution.py:547
  48.5 15.5 %all-to-all-start.1 = ((f32[32,1,128]{2,1,0:T(1,128)}), f32[32,1,128]{2,1,0:T(1,128)S(1)}, u32[]{:S(2)}, u32[]{:S(2)}) async-start(f32[32,1,128]{2,1,0:T(1,128)} %get-tuple-element.49), calls=%async_computation.1 | async-start | bytes 32768 | tf_op jit(solution)/shard_map/all_to_all | solution.py:560

commit v6 on v5

--- a/solution.py
+++ b/solution.py
@@ -28,7 +28,10 @@
 F32 = jnp.float32
 
 VMEM = pl.BlockSpec(memory_space=pltpu.VMEM)
-SMEM = pl.BlockSpec(memory_space=pltpu.SMEM)
+
+
+def place():
+    return lax.axis_index(LON[0]) * GROUP + lax.axis_index(LON[1]), lax.axis_index("lat")
 
 
 def lanes(shape=(8, 128)):
@@ -120,10 +123,10 @@
     out_ref[levels // 2] = put(zero, (depth, sea * z_ref[...], sea * f_ref[...]), 0)
 
 
-def lon_rows_kernel(info_ref, t_ref, s_ref, u_ref, v_ref, d_ref, m_ref, z_ref, f_ref, q_ref, r_ref):
+def lon_rows_kernel(t_ref, s_ref, u_ref, v_ref, d_ref, m_ref, z_ref, f_ref, q_ref, r_ref):
     levels = t_ref.shape[0]
     sub = subs()
-    odd_lon = jnp.full((8, 128), info_ref[3] % 2, jnp.int32) == 1
+    odd_lon = jnp.full((8, 128), place()[0] % 2, jnp.int32) == 1
 
     def put(k, u, v, t, s):
         v4, t2, s6 = roll_sub(v, 4), roll_sub(t, 2), roll_sub(s, 6)
@@ -151,25 +154,36 @@
     return jnp.where(sub % 2 == 0, roll_sub(x, -1), roll_sub(x, 1))
 
 
-def corners_kernel(info_ref, a_ref, b_ref, r_in, q_in, g_ref, r_ref, q_ref):
+def corners_kernel(top, a_ref, b_ref, r_in, q_in, g_ref, r_ref, q_ref):
     del q_in, r_in
     count = a_ref.shape[0]
     lane = lanes()
-    is_even, is_top, odd_lon = info_ref[0], info_ref[1], info_ref[3] % 2
+    lon, lat = place()
+    is_even, odd_lon = 1 - lat % 2, lon % 2
     from_north = lane % 16 >= 8
     flow_sign = jnp.where(group_of(lane) % 4 < 2, -1.0, 1.0).astype(F32)
 
-    @pl.when(is_even == 1)
+    sub = subs()
+    odd_block = jnp.full((8, 128), odd_lon, jnp.int32) == 1
+    west_row, east_row = sub == 3, sub == 0
+    in_q = (west_row & odd_block) | (east_row & ~odd_block)
+    in_r = (east_row & odd_block) | (west_row & ~odd_block)
+
+    def put(j, g):
+        g_ref[j] = g
+        for odd in range(2):
+            rows = jnp.where(west_row, roll_sub(g, 3 - odd), roll_sub(g, 1 + odd))
+            k = 2 * j + odd
+            q_ref[k] = jnp.where(in_q, rows, q_ref[k])
+            r_ref[k] = jnp.where(in_r, rows, r_ref[k])
+
+    @pl.when(lat != top)
     def _():
+        from_a = from_north == (jnp.full((8, 128), is_even, jnp.int32) == 1)
         for j in range(count):
-            g_ref[j] = jnp.where(from_north, a_ref[j], b_ref[j])
-
-    @pl.when((is_even == 0) & (is_top == 0))
-    def _():
-        for j in range(count):
-            g_ref[j] = jnp.where(from_north, b_ref[j], a_ref[j])
-
-    @pl.when(is_top == 1)
+            put(j, jnp.where(from_a, a_ref[j], b_ref[j]))
+
+    @pl.when(lat == top)
     def _():
         for j in range(count):
             rows = turn_rows(b_ref[j])
@@ -178,26 +192,12 @@
                 turned = jnp.where(lane % 16 == 8 + i, roll_lane(rows, 1 + 2 * i), turned)
             if j < count - 1:
                 turned = turned * flow_sign
-            g_ref[j] = jnp.where(from_north, turned, a_ref[j])
-
-    def put(west_ref, east_ref):
-        for k in range(2 * count):
-            odd = k % 2
-            west_ref[k, 3:4, :] = g_ref[k // 2, odd : odd + 1, :]
-            east_ref[k, 0:1, :] = g_ref[k // 2, 7 - odd : 8 - odd, :]
-
-    @pl.when(odd_lon == 1)
-    def _():
-        put(q_ref, r_ref)
-
-    @pl.when(odd_lon == 0)
-    def _():
-        put(r_ref, q_ref)
-
-
-def lon_masks(info_ref):
+            put(j, jnp.where(from_north, turned, a_ref[j]))
+
+
+def lon_masks():
     sub = subs()
-    odd_lon = jnp.full((8, 128), info_ref[3] % 2, jnp.int32) == 1
+    odd_lon = jnp.full((8, 128), place()[0] % 2, jnp.int32) == 1
     return [x != odd_lon for x in (one_of(sub, (0, 1, 4, 5)), sub == 2, sub == 6, sub == 3)]
 
 
@@ -242,11 +242,11 @@
 
 
 def momentum_kernel(
-    info_ref, th_ref, t_ref, s_ref, u_ref, v_ref, d_ref, m_ref, z_ref, f_ref, g_ref, r_ref, q_ref, us_ref, vs_ref, chunk_ref, st_ref
+    lat_size, th_ref, t_ref, s_ref, u_ref, v_ref, d_ref, m_ref, z_ref, f_ref, g_ref, r_ref, q_ref, us_ref, vs_ref, chunk_ref, st_ref
 ):
     levels = t_ref.shape[0]
     lane, sub = lanes(), subs()
-    edges = lon_masks(info_ref)
+    edges = lon_masks()
     last = levels // 2
     sea = m_ref[...].astype(F32)
     corner = corner_group(q_ref, r_ref, last, edges)
@@ -254,9 +254,9 @@
     depth = [(d_ref[...] * m_ref[...]).astype(F32), from_lat_group(g_ref[last], 0, 0), edge, from_lat_group(corner, 0, 0)]
     low_e = [jnp.minimum(x, y) for x, y in zip(depth, ext_east(depth))]
     low_n = [jnp.minimum(x, y) for x, y in zip(depth, ext_north(depth))]
-    lat_index = (lane + info_ref[2] * 128).astype(F32)
+    lat_index = (lane + place()[1] * 128).astype(F32)
     ghost_index = lat_index + jnp.where(lane < 64, 128.0, -128.0)
-    lats = 128.0 * info_ref[4].astype(F32)
+    lats = 128.0 * lat_size
     ghost_index = jnp.where(ghost_index >= lats, 2.0 * lats - 1.0 - ghost_index, ghost_index)
     coriolis = [CORIOLIS * (2.0 * (x + 0.5) / lats - 1.0) for x in (lat_index, ghost_index)]
     zero = jnp.zeros((8, 128), F32)
@@ -325,10 +325,10 @@
         st_ref[i] = start[i]
 
 
-def tracer_kernel(info_ref, th_ref, t_ref, s_ref, u_ref, v_ref, d_ref, m_ref, g_ref, q_ref, r_ref, after_ref, nt_ref, ns_ref):
+def tracer_kernel(th_ref, t_ref, s_ref, u_ref, v_ref, d_ref, m_ref, g_ref, q_ref, r_ref, after_ref, nt_ref, ns_ref):
     del after_ref
     levels = t_ref.shape[0]
-    edges = lon_masks(info_ref)
+    edges = lon_masks()
     depth = (d_ref[...] * m_ref[...]).astype(F32)
     depth_g = from_lat_group(g_ref[levels // 2], 0, 0)
     depth_h = lon_ghost(q_ref[levels], r_ref[levels], edges)
@@ -347,8 +347,8 @@
         v_g = from_lat_group(g, 1, odd)
         wet = depth > kf
         wet_below = (depth > kf + 1.0) & (k + 1 < levels)
-        inv_space = 1.0 / jnp.full((8, 128), 0.5 * (th + th_below), F32)
-        inv_th = MIXING / jnp.full((8, 128), th, F32)
+        inv_space = 1.0 / (0.5 * (th + th_below))
+        inv_th = MIXING / th
         flow = [0.25 * x for x in (u + east(u, u_h), west(u, u_h) + u, v + north(v, v_g), south(v, v_g) + v)]
         masks = [x > kf for x in low]
         fluxes = []
@@ -377,14 +377,14 @@
     lax.fori_loop(0, levels // 2 // TILES_PER_STEP, step, (zero, zero))
 
 
-def slab_kernel(levels, info_ref, own_ref, q_ref, r_ref, st_ref, sum_ref, surf_ref, slope_ref, we_s, wn_s, fac_s, inv_s, r_s, d_s, z_s):
-    odd_group = jnp.full((GROUP, 128), info_ref[3] // GROUP % 2, jnp.int32) == 1
+def slab_kernel(levels, own_ref, q_ref, r_ref, st_ref, sum_ref, surf_ref, slope_ref, we_s, wn_s, fac_s, inv_s, r_s, d_s, z_s):
+    odd_group = jnp.full((GROUP, 128), lax.axis_index(LON[0]) % 2, jnp.int32) == 1
 
     def rows(i):
         own, q, r = (ref[pl.ds(i, GROUP, stride=24), :] for ref in (own_ref, q_ref, r_ref))
         return jnp.concatenate([jnp.where(odd_group, q, r), own, jnp.where(odd_group, r, q)], axis=0)
 
-    here = GROUP + info_ref[3] % GROUP
+    here = GROUP + lax.axis_index(LON[1])
     right, left = here + 1, here - 1
     heights, tu = [], [None] * 8
     for p in range(8):
@@ -499,11 +499,7 @@
 
 def per_device(lon_size, lat_size, temp, salt, u, v, strata, sea, thickness, elevation, drive):
     levels = temp.shape[0]
-    lon, lat = lax.axis_index(LON), lax.axis_index("lat")
     top = lat_size - 1
-    info = jnp.stack(
-        [1 - lat % 2, (lat == top).astype(jnp.int32), lat, lon, jnp.int32(lat_size), jnp.int32(levels)]
-    ).astype(jnp.int32)
     pairs_a = [(i, i ^ 1) for i in range(lat_size)]
     pairs_b = []
     for a in range(lon_size):
@@ -532,31 +528,33 @@
         + [pltpu.SemaphoreType.DMA((3, 4))],
     )(*[pltpu.with_memory_space_constraint(x, pltpu.HBM) for x in own])
     got_a, got_b = lat_swap(edges)
-    rows_q, rows_r = call(lon_rows_kernel, "lon_rows", (message, message), [SMEM] + [VMEM] * 8)(info, *own)
-    ghost, pair_r, pair_q = call(
-        corners_kernel, "corners", (packed, message, message), [SMEM] + [VMEM] * 4, aliases={3: 1, 4: 2}
-    )(info, got_a, got_b, rows_r, rows_q)
+    thick = jnp.broadcast_to(thickness[:, None, None], field.shape)
+    rows_q, rows_r = call(lon_rows_kernel, "lon_rows", (message, message), [VMEM] * 8)(*own)
+    corners = functools.partial(corners_kernel, top)
+    ghost, pair_r, pair_q = call(corners, "corners", (packed, message, message), [VMEM] * 4, aliases={2: 1, 3: 2})(
+        got_a, got_b, rows_r, rows_q
+    )
     pair_r = lax.ppermute(pair_r, LON, [(i, (i + 1 if i % 2 else i - 1) % lon_size) for i in range(lon_size)])
     pair_q = lax.ppermute(pair_q, LON, [(i, i ^ 1) for i in range(lon_size)])
     u_star, v_star, chunk, start = call(
-        momentum_kernel, "momentum", (field, field, tiles(3), tiles(3)), [SMEM, SMEM] + [VMEM] * 11
-    )(info, thickness, *own, ghost, pair_r, pair_q)
+        functools.partial(momentum_kernel, lat_size), "momentum", (field, field, tiles(3), tiles(3)), [VMEM] * 12
+    )(thick, *own, ghost, pair_r, pair_q)
     group = from_all(chunk, ("lon_lo",)).reshape(GROUP * 24, 128)
     group, after = lax.optimization_barrier((group, chunk))
     groups = lon_size // GROUP
     group_q = lax.ppermute(group, "lon_hi", [(i, i ^ 1) for i in range(groups)])
     group_r = lax.ppermute(group, "lon_hi", [(i, (i + 1 if i % 2 else i - 1) % groups) for i in range(groups)])
-    new_temp, new_salt = call(tracer_kernel, "tracers", (field, field), [SMEM] * 2 + [VMEM] * 10)(
-        info, thickness, temp, salt, u, v, strata, sea, ghost, pair_q, pair_r, after
+    new_temp, new_salt = call(tracer_kernel, "tracers", (field, field), [VMEM] * 11)(
+        thick, temp, salt, u, v, strata, sea, ghost, pair_q, pair_r, after
     )
     group_q, group_r, new_temp, new_salt = lax.optimization_barrier((group_q, group_r, new_temp, new_salt))
     sums, surface, slope = call(
         functools.partial(slab_kernel, levels),
         "slab",
         (jax.ShapeDtypeStruct((groups * lat_size, 1, 128), F32), jax.ShapeDtypeStruct((8, 128), F32), tiles(2)),
-        [SMEM] + [VMEM] * 4,
+        [VMEM] * 4,
         [pltpu.VMEM((8, 3 * GROUP, 256), F32)] * 7,
-    )(info, group, group_q, group_r, start)
+    )(group, group_q, group_r, start)
     sums = lax.all_to_all(sums, ("lon_hi", "lat"), 0, 0, tiled=True)
     total = jnp.sum(sums, axis=0)
     cells = lon_size * 8 * lat_size * 128

time: 65.5 us -> 64.1 us (0.979)
  Pallas kernels: 11.3 us -> 8.65 us
  waiting for transfers between devices: 14.4 us -> 16.5 us
    pallas_call x4, Pallas kernels: 6.7 us -> 4.58 us  [the longest x1 2.8 us: per_device(): call(functools.partial(momentum_kernel, lat_size), 'momentum', (field, fi...]
    ppermute x1, waiting for transfers between devices: 0.53 us -> 1.73 us  [lat_swap(): lax.ppermute(x, (*LON, 'lat'), pairs_b)]
    ppermute x1, waiting for transfers between devices: 1.06 us -> 2.13 us  [per_device(): pair_q = lax.ppermute(pair_q, LON, [(i, i ^ 1) for i in range(lon_size)])]
    ppermute x1, waiting for transfers between devices: 4.18 us -> 3.47 us  [per_device(): lax.ppermute(pair_r, LON, [(i, (i + 1 if i % 2 else i - 1) % lon_size) fo...]
  transfers between devices with their start and end apart: 7 -> 7, of which waited for: 5 -> 6; matrix products, arithmetic and copies ran while one was open for 0% -> 0% of each run, Pallas kernels for 5% -> 4%
where the time goes in v6:
time: 64.1 us; the launch traced here: 63.9 us
  starting transfers between devices  27.2 us (42%)
  waiting for transfers between devices  16.5 us (26%)
  blocking collectives  9.18 us (14%)
  Pallas kernels  8.65 us (13%)
  between operations  2.05 us (3%)
    ppermute x1, starting transfers between devices, per_device(): lax.ppermute(pair_r, LON, [(i, (i + 1 if i % 2 else i - 1) % lon_size) fo...  10.4 us
    all_to_all x1, blocking collectives, from_all(): return lax.all_to_all(copies, axes, 0, 0, tiled=True)  9.18 us
    all_to_all x1, starting transfers between devices, per_device(): sums = lax.all_to_all(sums, ('lon_hi', 'lat'), 0, 0, tiled=True)  7.78 us
    all_to_all x1, waiting for transfers between devices, per_device(): sums = lax.all_to_all(sums, ('lon_hi', 'lat'), 0, 0, tiled=True)  7.13 us
    ppermute x1, starting transfers between devices, lat_swap(): lax.ppermute(x, (*LON, 'lat'), pairs_b)  4.59 us
    ppermute x1, starting transfers between devices, per_device(): lax.ppermute(group, 'lon_hi', [(i, (i + 1 if i % 2 else i - 1) % groups)...  4.41 us
    ppermute x1, waiting for transfers between devices, per_device(): lax.ppermute(pair_r, LON, [(i, (i + 1 if i % 2 else i - 1) % lon_size) fo...  3.47 us
    pallas_call x1, Pallas kernels, per_device(): call(functools.partial(momentum_kernel, lat_size), 'momentum', (field, fi...  2.8 us
  transfers between devices with their start and end apart: 7, of which 6 were waited for; matrix products, arithmetic and copies ran while one was open for 0% of the time, Pallas kernels for 4%

profile of v6, /device:TPU:1, one launch (start us, length us, event | category | flops | bytes accessed | tf_op | source)
XLA Modules:
  0.0 63.9 jit_solution(10391697251261912320)
XLA Ops:
  0.6 0.0 copy-start.5
  0.6 0.0 copy-start.4
  0.7 0.0 copy-start.3
  0.7 0.0 copy-start.2
  0.7 0.0 copy-start.1
  0.7 0.0 copy-start
  0.7 0.0 copy-start.7
  0.7 0.0 copy-start.6
  0.7 1.5 %lat_pack.1 = f32[17,8,128]{2,1,0:T(8,128)S(1)} custom-call(f32[32,8,128]{2,1,0:T(8,128)} %t_ref.5, f32[32,8,128]{2,1,0:T(8,128)} %s_ref.5, f32[32,8,128]{2,1,0:T(8,128)} %u_ref.5, f32[32,8,128]{2,1,0:T(8,128)} %v_ref.5, s32[8,128]{1,0:T(8,128)} %d_ref.7, s32[8,128]{1,0:T(8,128)} %m_ref.7, f32[8,128]{1,0:T(8,128)} %z_ref.3, f32[8,128]{1,0:T(8,128)} %f_ref.3), custom_call_target="tpu_custom_call" | custom-call | tf_op jit(solution)/shard_map/lat_pack/pallas_call | solution.py:520
  2.2 4.6 %collective-permute-start.1 = (f32[17,8,128]{2,1,0:T(8,128)S(1)}, f32[17,8,128]{2,1,0:T(8,128)S(1)}, u32[]{:S(2)}, u32[]{:S(2)}) collective-permute-start(f32[17,8,128]{2,1,0:T(8,128)S(1)} %lat_pack.1), channel_id=1, source_target_pairs={{1,2},{2,1},{3,255},{5,6},{6,5},{7,251},{9,10},{10,9},{11,247},{13... | collective-permute-start | bytes 208904 | tf_op jit(solution)/shard_map/ppermute | solution.py:511
  6.8 0.1 collective-permute-start
  6.9 0.0 copy-done.5
  6.9 0.0 copy-done.4
  6.9 0.0 copy-done.3
  6.9 0.0 copy-done.2
  7.0 0.0 copy-done.1
  7.0 0.0 copy-done
  7.0 0.0 copy-done.7
  7.0 0.0 copy-done.6
  7.0 0.1 lon_rows.1
  7.1 1.7 %collective-permute-done.1.b_ref = f32[17,8,128]{2,1,0:T(8,128)S(1)} collective-permute-done((f32[17,8,128]{2,1,0:T(8,128)S(1)}, f32[17,8,128]{2,1,0:T(8,128)S(1)}, u32[]{:S(2)}, u32[]{:S(2)}) %collective-permute-start.1) | collective-permute-done | bytes 69664 | tf_op jit(solution)/shard_map/ppermute | solution.py:511
  8.8 0.0 collective-permute-done.a_ref
  8.9 0.0 copy-start.8
  8.9 10.4 %collective-permute-start.2 = (f32[34,8,128]{2,1,0:T(8,128)S(1)}, f32[34,8,128]{2,1,0:T(8,128)S(1)}, u32[]{:S(2)}, u32[]{:S(2)}) collective-permute-start(f32[34,8,128]{2,1,0:T(8,128)S(1)} %get-tuple-element.31), channel_id=1, source_target_pairs={{0,252},{4,8},{8,4},{12,16},{16,12},{20,24},{24,20},{28,32},{32,28... | collective-permute-start | bytes 417800 | tf_op jit(solution)/shard_map/ppermute | solution.py:537
  19.2 0.0 collective-permute-start.3
  19.2 3.5 %collective-permute-done.2.r_ref = f32[34,8,128]{2,1,0:T(8,128)S(1)} collective-permute-done((f32[34,8,128]{2,1,0:T(8,128)S(1)}, f32[34,8,128]{2,1,0:T(8,128)S(1)}, u32[]{:S(2)}, u32[]{:S(2)}) %collective-permute-start.2) | collective-permute-done | bytes 139296 | tf_op jit(solution)/shard_map/ppermute | solution.py:537
  22.7 2.1 %collective-permute-done.3.q_ref = f32[34,8,128]{2,1,0:T(8,128)S(1)} collective-permute-done((f32[34,8,128]{2,1,0:T(8,128)S(1)}, f32[34,8,128]{2,1,0:T(8,128)S(1)}, u32[]{:S(2)}, u32[]{:S(2)}) %collective-permute-start.3) | collective-permute-done | bytes 139296 | tf_op jit(solution)/shard_map/ppermute | solution.py:538
  24.8 0.0 copy-done.8
  24.8 0.1 broadcast_in_dim.4.th_ref
  24.9 2.8 %momentum.1 = (f32[32,8,128]{2,1,0:T(8,128)S(1)}, f32[32,8,128]{2,1,0:T(8,128)S(1)}, f32[3,8,128]{2,1,0:T(8,128)S(1)}, f32[3,8,128]{2,1,0:T(8,128)S(1)}) custom-call(f32[32,8,128]{2,1,0:T(8,128)S(1)} %broadcast_in_dim.4.th_ref, f32[32,8,128]{2,1,0:T(8,128)S(1)} %copy-done, f32[32,8,128]{2,1,0:T(8,128)S(1)} %copy-done.1, f32[32,8,128]{2,1,0:T(8,128)S(1)} %copy-done.2, ...), custom_call_target="tpu_custom_call" | custom-call | tf_op jit(solution)/shard_map/momentum/pallas_call | solution.py:539
  27.7 9.2 %all_to_all.10 = f32[8,3,8,128]{3,2,1,0:T(8,128)S(1)} all-to-all(f32[8,3,8,128]{3,2,1,0:T(8,128)S(1)} %broadcast_in_dim.5), channel_id=1, replica_groups=mesh['lon_hi'=8,'lon_lo'=8,'lat'=4] {'lon_lo'}, dimensions={0} | all-to-all | bytes 196608 | tf_op jit(solution)/shard_map/all_to_all | solution.py:497
  36.9 4.4 %collective-permute-start.5 = (f32[192,128]{1,0:T(8,128)S(1)}, f32[192,128]{1,0:T(8,128)S(1)}, u32[]{:S(2)}, u32[]{:S(2)}) collective-permute-start(f32[192,128]{1,0:T(8,128)S(1)} %bitcast.4), channel_id=1, source_target_pairs={{0,224},{32,64},{64,32},{96,128},{128,96},{160,192},{192,160},{224... | collective-permute-start | bytes 294920 | tf_op jit(solution)/shard_map/ppermute | solution.py:546
  41.3 0.0 collective-permute-start.4
  41.3 1.7 %tracers.1 = (f32[32,8,128]{2,1,0:T(8,128)}, f32[32,8,128]{2,1,0:T(8,128)}) custom-call(f32[32,8,128]{2,1,0:T(8,128)S(1)} %broadcast_in_dim.4.th_ref, f32[32,8,128]{2,1,0:T(8,128)S(1)} %copy-done, f32[32,8,128]{2,1,0:T(8,128)S(1)} %copy-done.1, f32[32,8,128]{2,1,0:T(8,128)S(1)} %copy-done.2, f32[32,8,128]{2,1,0:T(8,128)S(1)} %copy-done.3, ...), custom_call_target="tpu_custom_call" | custom-call | tf_op jit(solution)/shard_map/tracers/pallas_call | solution.py:547
  43.0 0.3 collective-permute-done.5.r_ref
  43.3 1.8 %collective-permute-done.4.q_ref = f32[192,128]{1,0:T(8,128)S(1)} collective-permute-done((f32[192,128]{1,0:T(8,128)S(1)}, f32[192,128]{1,0:T(8,128)S(1)}, u32[]{:S(2)}, u32[]{:S(2)}) %collective-permute-start.4) | collective-permute-done | bytes 98336 | tf_op jit(solution)/shard_map/ppermute | solution.py:545
  45.1 1.9 %slab.1 = (f32[32,1,128]{2,1,0:T(1,128)}, f32[8,128]{1,0:T(8,128)}, f32[2,8,128]{2,1,0:T(8,128)S(1)}) custom-call(f32[192,128]{1,0:T(8,128)S(1)} %bitcast.6, f32[192,128]{1,0:T(8,128)S(1)} %collective-permute-done.4.q_ref, f32[192,128]{1,0:T(8,128)S(1)} %collective-permute-done.5.r_ref, f32[3,8,128]{2,1,0:T(8,128)S(1)} %get-tuple-element.44.st_ref), custom_call_target="tpu_custom_call" | custom-call | tf_op jit(solution)/shard_map/slab/pallas_call | solution.py:551
  47.0 7.8 %all-to-all-start.1 = ((f32[32,1,128]{2,1,0:T(1,128)}), f32[32,1,128]{2,1,0:T(1,128)S(1)}, u32[]{:S(2)}, u32[]{:S(2)}) async-start(f32[32,1,128]{2,1,0:T(1,128)} %get-tuple-element.49), calls=%async_computation.1 | async-start | bytes 32768 | tf_op jit(solution)/shard_map/all_to_all | solution.py:558
  54.7 0.7 %velocity.1 = (f32[32,8,128]{2,1,0:T(8,128)}, f32[32,8,128]{2,1,0:T(8,128)}) custom-call(f32[32,8,128]{2,1,0:T(8,128)S(1)} %get-tuple-element.40.us_ref, f32[32,8,128]{2,1,0:T(8,128)S(1)} %get-tuple-element.41.vs_ref, s32[8,128]{1,0:T(8,128)S(1)} %copy-done.4, s32[8,128]{1,0:T(8,128)S(1)} %copy-done.5, f32[2,8,128]{2,1,0:T(8,128)S(1)} %get-tuple-element.45.slope_ref), custom_call_target="tpu_custom_call" | custom-call | tf_op jit(solution)/shard_map/velocity/pallas_call | solution.py:562
  55.5 7.1 %all-to-all-done.1 = f32[32,1,128]{2,1,0:T(1,128)S(1)} async-done(((f32[32,1,128]{2,1,0:T(1,128)}), f32[32,1,128]{2,1,0:T(1,128)S(1)}, u32[]{:S(2)}, u32[]{:S(2)}) %all-to-all-start.1) | async-done | bytes 16416 | tf_op jit(solution)/shard_map/all_to_all | solution.py:558
  62.6 0.1 reduce_sum.11
  (2 shorter events, 0.1 us)
Async XLA Ops:
  0.6 6.3 %copy-start.5 = (s32[8,128]{1,0:T(8,128)S(1)}, s32[8,128]{1,0:T(8,128)}, u32[]{:S(2)}) copy-start(s32[8,128]{1,0:T(8,128)} %m_ref.7) | copy-start | bytes 12292
  0.6 6.3 %copy-start.4 = (s32[8,128]{1,0:T(8,128)S(1)}, s32[8,128]{1,0:T(8,128)}, u32[]{:S(2)}) copy-start(s32[8,128]{1,0:T(8,128)} %d_ref.7) | copy-start | bytes 12292
  0.7 6.3 %copy-start.3 = (f32[32,8,128]{2,1,0:T(8,128)S(1)}, f32[32,8,128]{2,1,0:T(8,128)}, u32[]{:S(2)}) copy-start(f32[32,8,128]{2,1,0:T(8,128)} %v_ref.5) | copy-start | bytes 393220
  0.7 6.3 %copy-start.2 = (f32[32,8,128]{2,1,0:T(8,128)S(1)}, f32[32,8,128]{2,1,0:T(8,128)}, u32[]{:S(2)}) copy-start(f32[32,8,128]{2,1,0:T(8,128)} %u_ref.5) | copy-start | bytes 393220
  0.7 6.3 %copy-start.1 = (f32[32,8,128]{2,1,0:T(8,128)S(1)}, f32[32,8,128]{2,1,0:T(8,128)}, u32[]{:S(2)}) copy-start(f32[32,8,128]{2,1,0:T(8,128)} %s_ref.5) | copy-start | bytes 393220
  0.7 6.3 %copy-start = (f32[32,8,128]{2,1,0:T(8,128)S(1)}, f32[32,8,128]{2,1,0:T(8,128)}, u32[]{:S(2)}) copy-start(f32[32,8,128]{2,1,0:T(8,128)} %t_ref.5) | copy-start | bytes 393220
  0.7 6.3 %copy-start.7 = (f32[8,128]{1,0:T(8,128)S(1)}, f32[8,128]{1,0:T(8,128)}, u32[]{:S(2)}) copy-start(f32[8,128]{1,0:T(8,128)} %f_ref.3) | copy-start | bytes 12292
  0.7 6.3 %copy-start.6 = (f32[8,128]{1,0:T(8,128)S(1)}, f32[8,128]{1,0:T(8,128)}, u32[]{:S(2)}) copy-start(f32[8,128]{1,0:T(8,128)} %z_ref.3) | copy-start | bytes 12292
  2.2 6.6 %collective-permute-start.1 = (f32[17,8,128]{2,1,0:T(8,128)S(1)}, f32[17,8,128]{2,1,0:T(8,128)S(1)}, u32[]{:S(2)}, u32[]{:S(2)}) collective-permute-start(f32[17,8,128]{2,1,0:T(8,128)S(1)} %lat_pack.1), channel_id=1, source_target_pairs={{1,2},{2,1},{3,255},{5,6},{6,5},{7,251},{9,10},{10,9},{11,247},{13... | collective-permute-start | bytes 208904 | tf_op jit(solution)/shard_map/ppermute | solution.py:511
  6.8 2.0 %collective-permute-start = (f32[17,8,128]{2,1,0:T(8,128)S(1)}, f32[17,8,128]{2,1,0:T(8,128)S(1)}, u32[]{:S(2)}, u32[]{:S(2)}) collective-permute-start(f32[17,8,128]{2,1,0:T(8,128)S(1)} %lat_pack.1), channel_id=1, source_target_pairs={{0,1},{1,0},{2,3},{3,2},{4,5},{5,4},{6,7},{7,6},{8,9},{9,8},{10,11... | collective-permute-start | bytes 208904 | tf_op jit(solution)/shard_map/ppermute | solution.py:511
  8.9 16.0 %copy-start.8 = (f32[32]{0:T(128)S(1)}, f32[32]{0:T(128)}, u32[]{:S(2)}) copy-start(f32[32]{0:T(128)} %param.15) | copy-start | bytes 388
  8.9 13.8 %collective-permute-start.2 = (f32[34,8,128]{2,1,0:T(8,128)S(1)}, f32[34,8,128]{2,1,0:T(8,128)S(1)}, u32[]{:S(2)}, u32[]{:S(2)}) collective-permute-start(f32[34,8,128]{2,1,0:T(8,128)S(1)} %get-tuple-element.31), channel_id=1, source_target_pairs={{0,252},{4,8},{8,4},{12,16},{16,12},{20,24},{24,20},{28,32},{32,28... | collective-permute-start | bytes 417800 | tf_op jit(solution)/shard_map/ppermute | solution.py:537
  19.2 5.6 %collective-permute-start.3 = (f32[34,8,128]{2,1,0:T(8,128)S(1)}, f32[34,8,128]{2,1,0:T(8,128)S(1)}, u32[]{:S(2)}, u32[]{:S(2)}) collective-permute-start(f32[34,8,128]{2,1,0:T(8,128)S(1)} %get-tuple-element.32), channel_id=1, source_target_pairs={{0,4},{4,0},{8,12},{12,8},{16,20},{20,16},{24,28},{28,24},{32,36},... | collective-permute-start | bytes 417800 | tf_op jit(solution)/shard_map/ppermute | solution.py:538
  36.9 6.4 %collective-permute-start.5 = (f32[192,128]{1,0:T(8,128)S(1)}, f32[192,128]{1,0:T(8,128)S(1)}, u32[]{:S(2)}, u32[]{:S(2)}) collective-permute-start(f32[192,128]{1,0:T(8,128)S(1)} %bitcast.4), channel_id=1, source_target_pairs={{0,224},{32,64},{64,32},{96,128},{128,96},{160,192},{192,160},{224... | collective-permute-start | bytes 294920 | tf_op jit(solution)/shard_map/ppermute | solution.py:546
  41.3 3.8 %collective-permute-start.4 = (f32[192,128]{1,0:T(8,128)S(1)}, f32[192,128]{1,0:T(8,128)S(1)}, u32[]{:S(2)}, u32[]{:S(2)}) collective-permute-start(f32[192,128]{1,0:T(8,128)S(1)} %bitcast.5), channel_id=1, source_target_pairs={{0,32},{32,0},{64,96},{96,64},{128,160},{160,128},{192,224},{224,1... | collective-permute-start | bytes 294920 | tf_op jit(solution)/shard_map/ppermute | solution.py:545
  47.0 15.6 %all-to-all-start.1 = ((f32[32,1,128]{2,1,0:T(1,128)}), f32[32,1,128]{2,1,0:T(1,128)S(1)}, u32[]{:S(2)}, u32[]{:S(2)}) async-start(f32[32,1,128]{2,1,0:T(1,128)} %get-tuple-element.49), calls=%async_computation.1 | async-start | bytes 32768 | tf_op jit(solution)/shard_map/all_to_all | solution.py:558

commit v7 on v6

--- a/solution.py
+++ b/solution.py
@@ -377,7 +377,7 @@
     lax.fori_loop(0, levels // 2 // TILES_PER_STEP, step, (zero, zero))
 
 
-def slab_kernel(levels, own_ref, q_ref, r_ref, st_ref, sum_ref, surf_ref, slope_ref, we_s, wn_s, fac_s, inv_s, r_s, d_s, z_s):
+def slab_kernel(levels, own_ref, q_ref, r_ref, st_ref, sum_ref, flat_ref, we_s, wn_s, fac_s, inv_s, r_s, d_s, z_s):
     odd_group = jnp.full((GROUP, 128), lax.axis_index(LON[0]) % 2, jnp.int32) == 1
 
     def rows(i):
@@ -462,14 +462,15 @@
     x_h = jnp.where(sub < 4, x_e, x_w)
     x, x_g, x_h = x + st_ref[0], x_g + st_ref[1], x_h + st_ref[2]
     e, w, n, s = around(x, x_g, x_h)
-    surf_ref[...] = x
-    slope_ref[0] = (0.5 * GRAVITY) * (e - w)
-    slope_ref[1] = (0.5 * GRAVITY) * (n - s)
-
-
-def velocity_kernel(us_ref, vs_ref, d_ref, m_ref, slope_ref, nu_ref, nv_ref):
+    flat_ref[0] = (0.5 * GRAVITY) * (e - w)
+    flat_ref[1] = (0.5 * GRAVITY) * (n - s)
+    flat_ref[2] = x
+
+
+def velocity_kernel(us_ref, vs_ref, d_ref, m_ref, flat_ref, nu_ref, nv_ref, surf_ref):
     depth = (d_ref[...] * m_ref[...]).astype(F32)
-    slope_x, slope_y = slope_ref[0], slope_ref[1]
+    slope_x, slope_y = flat_ref[0], flat_ref[1]
+    surf_ref[...] = flat_ref[2]
     for k in range(us_ref.shape[0]):
         wet = depth > k + 0.5
         nu_ref[k] = jnp.where(wet, us_ref[k] - slope_x, 0.0)
@@ -517,16 +518,15 @@
     message, packed = tiles(levels + 2), tiles(levels // 2 + 1)
     own = (temp, salt, u, v, strata, sea, elevation, drive)
 
-    edges = call(
+    flat_int, flat_float = jax.ShapeDtypeStruct(flat, jnp.int32), jax.ShapeDtypeStruct(flat, F32)
+    edges, *own = call(
         lat_pack_kernel,
         "lat_pack",
-        packed,
+        (packed, *[field] * 4, flat_int, flat_int, flat_float, flat_float),
         [pl.BlockSpec(memory_space=pltpu.HBM)] * 8,
-        [pltpu.VMEM(field.shape, F32)] * 4
-        + [pltpu.VMEM(flat, jnp.int32)] * 2
-        + [pltpu.VMEM(flat, F32)] * 2
-        + [pltpu.SemaphoreType.DMA((3, 4))],
+        [pltpu.SemaphoreType.DMA((3, 4))],
     )(*[pltpu.with_memory_space_constraint(x, pltpu.HBM) for x in own])
+    temp, salt, u, v, strata, sea = own[:6]
     got_a, got_b = lat_swap(edges)
     thick = jnp.broadcast_to(thickness[:, None, None], field.shape)
     rows_q, rows_r = call(lon_rows_kernel, "lon_rows", (message, message), [VMEM] * 8)(*own)
@@ -548,10 +548,10 @@
         thick, temp, salt, u, v, strata, sea, ghost, pair_q, pair_r, after
     )
     group_q, group_r, new_temp, new_salt = lax.optimization_barrier((group_q, group_r, new_temp, new_salt))
-    sums, surface, slope = call(
+    sums, solved = call(
         functools.partial(slab_kernel, levels),
         "slab",
-        (jax.ShapeDtypeStruct((groups * lat_size, 1, 128), F32), jax.ShapeDtypeStruct((8, 128), F32), tiles(2)),
+        (jax.ShapeDtypeStruct((groups * lat_size, 1, 128), F32), tiles(3)),
         [VMEM] * 4,
         [pltpu.VMEM((8, 3 * GROUP, 256), F32)] * 7,
     )(group, group_q, group_r, start)
@@ -559,7 +559,9 @@
     total = jnp.sum(sums, axis=0)
     cells = lon_size * 8 * lat_size * 128
     rms = jnp.sqrt(total[0, 0] / cells + EPSILON)
-    new_u, new_v = call(velocity_kernel, "velocity", (field, field), [VMEM] * 5)(u_star, v_star, strata, sea, slope)
+    new_u, new_v, surface = call(velocity_kernel, "velocity", (field, field, flat_float), [VMEM] * 5)(
+        u_star, v_star, strata, sea, solved
+    )
     return (new_temp, new_salt, new_u, new_v, surface, rms)
 
 

time: 64.1 us -> 64 us (level)
  no operation moved by 1% of the time
where the time goes in v7:
time: 64 us; the launch traced here: 63.7 us
  starting transfers between devices  27.2 us (42%)
  waiting for transfers between devices  16.6 us (26%)
  blocking collectives  9.18 us (14%)
  Pallas kernels  8.58 us (13%)
  between operations  1.93 us (3%)
    ppermute x1, starting transfers between devices, per_device(): lax.ppermute(pair_r, LON, [(i, (i + 1 if i % 2 else i - 1) % lon_size) fo...  10.4 us
    all_to_all x1, blocking collectives, from_all(): return lax.all_to_all(copies, axes, 0, 0, tiled=True)  9.18 us
    all_to_all x1, starting transfers between devices, per_device(): sums = lax.all_to_all(sums, ('lon_hi', 'lat'), 0, 0, tiled=True)  7.78 us
    all_to_all x1, waiting for transfers between devices, per_device(): sums = lax.all_to_all(sums, ('lon_hi', 'lat'), 0, 0, tiled=True)  7.14 us
    ppermute x1, starting transfers between devices, lat_swap(): lax.ppermute(x, (*LON, 'lat'), pairs_b)  4.59 us
    ppermute x1, starting transfers between devices, per_device(): lax.ppermute(group, 'lon_hi', [(i, (i + 1 if i % 2 else i - 1) % groups)...  4.41 us
    ppermute x1, waiting for transfers between devices, per_device(): lax.ppermute(pair_r, LON, [(i, (i + 1 if i % 2 else i - 1) % lon_size) fo...  3.47 us
    pallas_call x1, Pallas kernels, per_device(): call(functools.partial(momentum_kernel, lat_size), 'momentum', (field, fi...  2.81 us
  transfers between devices with their start and end apart: 7, of which 6 were waited for; matrix products, arithmetic and copies ran while one was open for 0% of the time, Pallas kernels for 4%

profile of v7, /device:TPU:1, one launch (start us, length us, event | category | flops | bytes accessed | tf_op | source)
XLA Modules:
  0.0 63.7 jit_solution(11751085536665302381)
XLA Ops:
  0.6 1.4 %lat_pack.1 = (f32[17,8,128]{2,1,0:T(8,128)S(1)}, f32[32,8,128]{2,1,0:T(8,128)S(1)}, f32[32,8,128]{2,1,0:T(8,128)S(1)}, f32[32,8,128]{2,1,0:T(8,128)S(1)}, f32[3...) custom-call(f32[32,8,128]{2,1,0:T(8,128)} %t_hbm.1, ...), custom_call_target="tpu_custom_call" | custom-call | tf_op jit(solution)/shard_map/lat_pack/pallas_call | solution.py:522
  2.0 4.6 %collective-permute-start.1 = (f32[17,8,128]{2,1,0:T(8,128)S(1)}, f32[17,8,128]{2,1,0:T(8,128)S(1)}, u32[]{:S(2)}, u32[]{:S(2)}) collective-permute-start(f32[17,8,128]{2,1,0:T(8,128)S(1)} %get-tuple-element.45), channel_id=1, source_target_pairs={{1,2},{2,1},{3,255},{5,6},{6,5},{7,251},{9,10},{10,9},{11,247},{13... | collective-permute-start | bytes 208904 | tf_op jit(solution)/shard_map/ppermute | solution.py:512
  6.6 0.1 collective-permute-start
  6.7 0.1 lon_rows.1
  6.8 1.8 %collective-permute-done.1.b_ref = f32[17,8,128]{2,1,0:T(8,128)S(1)} collective-permute-done((f32[17,8,128]{2,1,0:T(8,128)S(1)}, f32[17,8,128]{2,1,0:T(8,128)S(1)}, u32[]{:S(2)}, u32[]{:S(2)}) %collective-permute-start.1) | collective-permute-done | bytes 69664 | tf_op jit(solution)/shard_map/ppermute | solution.py:512
  8.6 0.0 collective-permute-done.a_ref
  8.7 0.0 copy-start
  8.7 10.4 %collective-permute-start.2 = (f32[34,8,128]{2,1,0:T(8,128)S(1)}, f32[34,8,128]{2,1,0:T(8,128)S(1)}, u32[]{:S(2)}, u32[]{:S(2)}) collective-permute-start(f32[34,8,128]{2,1,0:T(8,128)S(1)} %get-tuple-element.49), channel_id=1, source_target_pairs={{0,252},{4,8},{8,4},{12,16},{16,12},{20,24},{24,20},{28,32},{32,28... | collective-permute-start | bytes 417800 | tf_op jit(solution)/shard_map/ppermute | solution.py:537
  19.1 0.0 collective-permute-start.3
  19.1 3.5 %collective-permute-done.2.r_ref = f32[34,8,128]{2,1,0:T(8,128)S(1)} collective-permute-done((f32[34,8,128]{2,1,0:T(8,128)S(1)}, f32[34,8,128]{2,1,0:T(8,128)S(1)}, u32[]{:S(2)}, u32[]{:S(2)}) %collective-permute-start.2) | collective-permute-done | bytes 139296 | tf_op jit(solution)/shard_map/ppermute | solution.py:537
  22.5 2.1 %collective-permute-done.3.q_ref = f32[34,8,128]{2,1,0:T(8,128)S(1)} collective-permute-done((f32[34,8,128]{2,1,0:T(8,128)S(1)}, f32[34,8,128]{2,1,0:T(8,128)S(1)}, u32[]{:S(2)}, u32[]{:S(2)}) %collective-permute-start.3) | collective-permute-done | bytes 139296 | tf_op jit(solution)/shard_map/ppermute | solution.py:538
  24.7 0.0 copy-done
  24.7 0.1 broadcast_in_dim.4.th_ref
  24.8 2.8 %momentum.1 = (f32[32,8,128]{2,1,0:T(8,128)S(1)}, f32[32,8,128]{2,1,0:T(8,128)S(1)}, f32[3,8,128]{2,1,0:T(8,128)S(1)}, f32[3,8,128]{2,1,0:T(8,128)S(1)}) custom-call(f32[32,8,128]{2,1,0:T(8,128)S(1)} %broadcast_in_dim.4.th_ref, f32[32,8,128]{2,1,0:T(8,128)S(1)} %get-tuple-element.37.t_ref, f32[32,8,128]{2,1,0:T(8,128)S(1)} %get-tuple-element.38.s_ref, ...), custom_call_target="tpu_custom_call" | custom-call | tf_op jit(solution)/shard_map/momentum/pallas_call | solution.py:539
  27.6 9.2 %all_to_all.10 = f32[8,3,8,128]{3,2,1,0:T(8,128)S(1)} all-to-all(f32[8,3,8,128]{3,2,1,0:T(8,128)S(1)} %broadcast_in_dim.5), channel_id=1, replica_groups=mesh['lon_hi'=8,'lon_lo'=8,'lat'=4] {'lon_lo'}, dimensions={0} | all-to-all | bytes 196608 | tf_op jit(solution)/shard_map/all_to_all | solution.py:498
  36.8 4.4 %collective-permute-start.5 = (f32[192,128]{1,0:T(8,128)S(1)}, f32[192,128]{1,0:T(8,128)S(1)}, u32[]{:S(2)}, u32[]{:S(2)}) collective-permute-start(f32[192,128]{1,0:T(8,128)S(1)} %bitcast.4), channel_id=1, source_target_pairs={{0,224},{32,64},{64,32},{96,128},{128,96},{160,192},{192,160},{224... | collective-permute-start | bytes 294920 | tf_op jit(solution)/shard_map/ppermute | solution.py:546
  41.2 0.0 collective-permute-start.4
  41.2 1.7 %tracers.1 = (f32[32,8,128]{2,1,0:T(8,128)}, f32[32,8,128]{2,1,0:T(8,128)}) custom-call(f32[32,8,128]{2,1,0:T(8,128)S(1)} %broadcast_in_dim.4.th_ref, f32[32,8,128]{2,1,0:T(8,128)S(1)} %get-tuple-element.37.t_ref, f32[32,8,128]{2,1,0:T(8,128)S(1)} %get-tuple-element.38.s_ref, f32[32,8,128]{2,1,0:T(8,128)S(1)} %get-tuple-element.39.u_ref, ...), custom_call_target="tpu_custom_call" | custom-call | tf_op jit(solution)/shard_map/tracers/pallas_call | solution.py:547
  42.9 0.3 collective-permute-done.5.r_ref
  43.2 1.8 %collective-permute-done.4.q_ref = f32[192,128]{1,0:T(8,128)S(1)} collective-permute-done((f32[192,128]{1,0:T(8,128)S(1)}, f32[192,128]{1,0:T(8,128)S(1)}, u32[]{:S(2)}, u32[]{:S(2)}) %collective-permute-start.4) | collective-permute-done | bytes 98336 | tf_op jit(solution)/shard_map/ppermute | solution.py:545
  44.9 1.9 %slab.1 = (f32[32,1,128]{2,1,0:T(1,128)}, f32[3,8,128]{2,1,0:T(8,128)S(1)}) custom-call(f32[192,128]{1,0:T(8,128)S(1)} %bitcast.6, f32[192,128]{1,0:T(8,128)S(1)} %collective-permute-done.4.q_ref, f32[192,128]{1,0:T(8,128)S(1)} %collective-permute-done.5.r_ref, f32[3,8,128]{2,1,0:T(8,128)S(1)} %get-tuple-element.62.st_ref), custom_call_target="tpu_custom_call" | custom-call | tf_op jit(solution)/shard_map/slab/pallas_call | solution.py:551
  46.8 7.8 %all-to-all-start.1 = ((f32[32,1,128]{2,1,0:T(1,128)}), f32[32,1,128]{2,1,0:T(1,128)S(1)}, u32[]{:S(2)}, u32[]{:S(2)}) async-start(f32[32,1,128]{2,1,0:T(1,128)} %get-tuple-element.67), calls=%async_computation.1 | async-start | bytes 32768 | tf_op jit(solution)/shard_map/all_to_all | solution.py:558
  54.6 0.7 %velocity.1 = (f32[32,8,128]{2,1,0:T(8,128)}, f32[32,8,128]{2,1,0:T(8,128)}, f32[8,128]{1,0:T(8,128)}) custom-call(f32[32,8,128]{2,1,0:T(8,128)S(1)} %get-tuple-element.58.us_ref, f32[32,8,128]{2,1,0:T(8,128)S(1)} %get-tuple-element.59.vs_ref, s32[8,128]{1,0:T(8,128)S(1)} %get-tuple-element.41.d_ref, s32[8,128]{1,0:T(8,128)S(1)} %get-tuple-element.42.m_ref, ...), custom_call_target="tpu_custom_call" | custom-call | tf_op jit(solution)/shard_map/velocity/pallas_call | solution.py:562
  55.3 7.1 %all-to-all-done.1 = f32[32,1,128]{2,1,0:T(1,128)S(1)} async-done(((f32[32,1,128]{2,1,0:T(1,128)}), f32[32,1,128]{2,1,0:T(1,128)S(1)}, u32[]{:S(2)}, u32[]{:S(2)}) %all-to-all-start.1) | async-done | bytes 16416 | tf_op jit(solution)/shard_map/all_to_all | solution.py:558
  62.5 0.1 reduce_sum.11
  (2 shorter events, 0.1 us)
Async XLA Ops:
  2.0 6.6 %collective-permute-start.1 = (f32[17,8,128]{2,1,0:T(8,128)S(1)}, f32[17,8,128]{2,1,0:T(8,128)S(1)}, u32[]{:S(2)}, u32[]{:S(2)}) collective-permute-start(f32[17,8,128]{2,1,0:T(8,128)S(1)} %get-tuple-element.45), channel_id=1, source_target_pairs={{1,2},{2,1},{3,255},{5,6},{6,5},{7,251},{9,10},{10,9},{11,247},{13... | collective-permute-start | bytes 208904 | tf_op jit(solution)/shard_map/ppermute | solution.py:512
  6.6 2.0 %collective-permute-start = (f32[17,8,128]{2,1,0:T(8,128)S(1)}, f32[17,8,128]{2,1,0:T(8,128)S(1)}, u32[]{:S(2)}, u32[]{:S(2)}) collective-permute-start(f32[17,8,128]{2,1,0:T(8,128)S(1)} %get-tuple-element.45), channel_id=1, source_target_pairs={{0,1},{1,0},{2,3},{3,2},{4,5},{5,4},{6,7},{7,6},{8,9},{9,8},{10,11... | collective-permute-start | bytes 208904 | tf_op jit(solution)/shard_map/ppermute | solution.py:512
  8.7 16.0 %copy-start = (f32[32]{0:T(128)S(1)}, f32[32]{0:T(128)}, u32[]{:S(2)}) copy-start(f32[32]{0:T(128)} %param.15) | copy-start | bytes 388
  8.7 13.8 %collective-permute-start.2 = (f32[34,8,128]{2,1,0:T(8,128)S(1)}, f32[34,8,128]{2,1,0:T(8,128)S(1)}, u32[]{:S(2)}, u32[]{:S(2)}) collective-permute-start(f32[34,8,128]{2,1,0:T(8,128)S(1)} %get-tuple-element.49), channel_id=1, source_target_pairs={{0,252},{4,8},{8,4},{12,16},{16,12},{20,24},{24,20},{28,32},{32,28... | collective-permute-start | bytes 417800 | tf_op jit(solution)/shard_map/ppermute | solution.py:537
  19.1 5.6 %collective-permute-start.3 = (f32[34,8,128]{2,1,0:T(8,128)S(1)}, f32[34,8,128]{2,1,0:T(8,128)S(1)}, u32[]{:S(2)}, u32[]{:S(2)}) collective-permute-start(f32[34,8,128]{2,1,0:T(8,128)S(1)} %get-tuple-element.50), channel_id=1, source_target_pairs={{0,4},{4,0},{8,12},{12,8},{16,20},{20,16},{24,28},{28,24},{32,36},... | collective-permute-start | bytes 417800 | tf_op jit(solution)/shard_map/ppermute | solution.py:538
  36.8 6.4 %collective-permute-start.5 = (f32[192,128]{1,0:T(8,128)S(1)}, f32[192,128]{1,0:T(8,128)S(1)}, u32[]{:S(2)}, u32[]{:S(2)}) collective-permute-start(f32[192,128]{1,0:T(8,128)S(1)} %bitcast.4), channel_id=1, source_target_pairs={{0,224},{32,64},{64,32},{96,128},{128,96},{160,192},{192,160},{224... | collective-permute-start | bytes 294920 | tf_op jit(solution)/shard_map/ppermute | solution.py:546
  41.2 3.8 %collective-permute-start.4 = (f32[192,128]{1,0:T(8,128)S(1)}, f32[192,128]{1,0:T(8,128)S(1)}, u32[]{:S(2)}, u32[]{:S(2)}) collective-permute-start(f32[192,128]{1,0:T(8,128)S(1)} %bitcast.5), channel_id=1, source_target_pairs={{0,32},{32,0},{64,96},{96,64},{128,160},{160,128},{192,224},{224,1... | collective-permute-start | bytes 294920 | tf_op jit(solution)/shard_map/ppermute | solution.py:545
  46.8 15.6 %all-to-all-start.1 = ((f32[32,1,128]{2,1,0:T(1,128)}), f32[32,1,128]{2,1,0:T(1,128)S(1)}, u32[]{:S(2)}, u32[]{:S(2)}) async-start(f32[32,1,128]{2,1,0:T(1,128)} %get-tuple-element.67), calls=%async_computation.1 | async-start | bytes 32768 | tf_op jit(solution)/shard_map/all_to_all | solution.py:558

commit v8 on v7

--- a/solution.py
+++ b/solution.py
@@ -24,6 +24,7 @@
 ITERS = 4
 TILES_PER_STEP = 4
 GROUP = 8
+REACH = ITERS + 1
 LON = ("lon_hi", "lon_lo")
 F32 = jnp.float32
 
@@ -380,9 +381,14 @@
 def slab_kernel(levels, own_ref, q_ref, r_ref, st_ref, sum_ref, flat_ref, we_s, wn_s, fac_s, inv_s, r_s, d_s, z_s):
     odd_group = jnp.full((GROUP, 128), lax.axis_index(LON[0]) % 2, jnp.int32) == 1
 
+    missing = jnp.zeros((GROUP - REACH, 128), F32)
+
     def rows(i):
-        own, q, r = (ref[pl.ds(i, GROUP, stride=24), :] for ref in (own_ref, q_ref, r_ref))
-        return jnp.concatenate([jnp.where(odd_group, q, r), own, jnp.where(odd_group, r, q)], axis=0)
+        own = own_ref[pl.ds(i, GROUP, stride=24), :]
+        q, r = (ref[pl.ds(i, REACH, stride=24), :] for ref in (q_ref, r_ref))
+        west_q, west_r = (jnp.concatenate([missing, x], axis=0) for x in (q, r))
+        east_q, east_r = (jnp.concatenate([x, missing], axis=0) for x in (q, r))
+        return jnp.concatenate([jnp.where(odd_group, west_q, west_r), own, jnp.where(odd_group, east_r, east_q)], axis=0)
 
     here = GROUP + lax.axis_index(LON[1])
     right, left = here + 1, here - 1
@@ -539,11 +545,14 @@
     u_star, v_star, chunk, start = call(
         functools.partial(momentum_kernel, lat_size), "momentum", (field, field, tiles(3), tiles(3)), [VMEM] * 12
     )(thick, *own, ghost, pair_r, pair_q)
+    chunk, odd_group = lax.optimization_barrier((chunk, lax.axis_index("lon_hi") % 2 == 1))
     group = from_all(chunk, ("lon_lo",)).reshape(GROUP * 24, 128)
-    group, after = lax.optimization_barrier((group, chunk))
     groups = lon_size // GROUP
-    group_q = lax.ppermute(group, "lon_hi", [(i, i ^ 1) for i in range(groups)])
-    group_r = lax.ppermute(group, "lon_hi", [(i, (i + 1 if i % 2 else i - 1) % groups) for i in range(groups)])
+    first, final = group[: REACH * 24], group[(GROUP - REACH) * 24 :]
+    group_q, group_r = jnp.where(odd_group, first, final), jnp.where(odd_group, final, first)
+    group, group_q, group_r, after = lax.optimization_barrier((group, group_q, group_r, chunk))
+    group_q = lax.ppermute(group_q, "lon_hi", [(i, i ^ 1) for i in range(groups)])
+    group_r = lax.ppermute(group_r, "lon_hi", [(i, (i + 1 if i % 2 else i - 1) % groups) for i in range(groups)])
     new_temp, new_salt = call(tracer_kernel, "tracers", (field, field), [VMEM] * 11)(
         thick, temp, salt, u, v, strata, sea, ghost, pair_q, pair_r, after
     )

time: 64 us -> 65.2 us (1.019)
  starting transfers between devices: 27.2 us -> 30.7 us
  waiting for transfers between devices: 16.6 us -> 14.5 us
    all_to_all x1, starting transfers between devices: 7.78 us -> 11 us  [per_device(): sums = lax.all_to_all(sums, ('lon_hi', 'lat'), 0, 0, tiled=True)]
    ppermute x2, waiting for transfers between devices: 2.08 us -> 0.01 us  [the longest x1 0.01 us: per_device(): lax.ppermute(group_q, 'lon_hi', [(i, i ^ 1) for i in range(groups)])]
  transfers between devices with their start and end apart: 7 -> 7, of which waited for: 6 -> 4; matrix products, arithmetic and copies ran while one was open for 0% -> 0% of each run, Pallas kernels for 4% -> 4%
where the time goes in v8:
time: 65.2 us; the launch traced here: 65 us
  starting transfers between devices  30.7 us (47%)
  waiting for transfers between devices  14.5 us (22%)
  blocking collectives  9.18 us (14%)
  Pallas kernels  8.53 us (13%)
  between operations  1.93 us (3%)
    all_to_all x1, starting transfers between devices, per_device(): sums = lax.all_to_all(sums, ('lon_hi', 'lat'), 0, 0, tiled=True)  11 us
    ppermute x1, starting transfers between devices, per_device(): lax.ppermute(pair_r, LON, [(i, (i + 1 if i % 2 else i - 1) % lon_size) fo...  10.4 us
    all_to_all x1, blocking collectives, from_all(): return lax.all_to_all(copies, axes, 0, 0, tiled=True)  9.18 us
    all_to_all x1, waiting for transfers between devices, per_device(): sums = lax.all_to_all(sums, ('lon_hi', 'lat'), 0, 0, tiled=True)  7.08 us
    ppermute x1, starting transfers between devices, lat_swap(): lax.ppermute(x, (*LON, 'lat'), pairs_b)  4.59 us
    ppermute x1, starting transfers between devices, per_device(): lax.ppermute(group_r, 'lon_hi', [(i, (i + 1 if i % 2 else i - 1) % groups...  4.5 us
    ppermute x1, waiting for transfers between devices, per_device(): lax.ppermute(pair_r, LON, [(i, (i + 1 if i % 2 else i - 1) % lon_size) fo...  3.46 us
    pallas_call x1, Pallas kernels, per_device(): call(functools.partial(momentum_kernel, lat_size), 'momentum', (field, fi...  2.77 us
  transfers between devices with their start and end apart: 7, of which 4 were waited for; matrix products, arithmetic and copies ran while one was open for 0% of the time, Pallas kernels for 4%

profile of v8, /device:TPU:1, one launch (start us, length us, event | category | flops | bytes accessed | tf_op | source)
XLA Modules:
  0.0 65.0 jit_solution(878813824742818619)
XLA Ops:
  0.6 1.4 %lat_pack.1 = (f32[17,8,128]{2,1,0:T(8,128)S(1)}, f32[32,8,128]{2,1,0:T(8,128)S(1)}, f32[32,8,128]{2,1,0:T(8,128)S(1)}, f32[32,8,128]{2,1,0:T(8,128)S(1)}, f32[3...) custom-call(f32[32,8,128]{2,1,0:T(8,128)} %t_hbm.1, ...), custom_call_target="tpu_custom_call" | custom-call | tf_op jit(solution)/shard_map/lat_pack/pallas_call | solution.py:528
  2.0 4.6 %collective-permute-start.1 = (f32[17,8,128]{2,1,0:T(8,128)S(1)}, f32[17,8,128]{2,1,0:T(8,128)S(1)}, u32[]{:S(2)}, u32[]{:S(2)}) collective-permute-start(f32[17,8,128]{2,1,0:T(8,128)S(1)} %get-tuple-element.49), channel_id=1, source_target_pairs={{1,2},{2,1},{3,255},{5,6},{6,5},{7,251},{9,10},{10,9},{11,247},{13... | collective-permute-start | bytes 208904 | tf_op jit(solution)/shard_map/ppermute | solution.py:518
  6.6 0.1 collective-permute-start
  6.7 0.1 lon_rows.1
  6.8 1.8 %collective-permute-done.1.b_ref = f32[17,8,128]{2,1,0:T(8,128)S(1)} collective-permute-done((f32[17,8,128]{2,1,0:T(8,128)S(1)}, f32[17,8,128]{2,1,0:T(8,128)S(1)}, u32[]{:S(2)}, u32[]{:S(2)}) %collective-permute-start.1) | collective-permute-done | bytes 69664 | tf_op jit(solution)/shard_map/ppermute | solution.py:518
  8.6 0.0 collective-permute-done.a_ref
  8.7 10.4 %collective-permute-start.2 = (f32[34,8,128]{2,1,0:T(8,128)S(1)}, f32[34,8,128]{2,1,0:T(8,128)S(1)}, u32[]{:S(2)}, u32[]{:S(2)}) collective-permute-start(f32[34,8,128]{2,1,0:T(8,128)S(1)} %get-tuple-element.53), channel_id=1, source_target_pairs={{0,252},{4,8},{8,4},{12,16},{16,12},{20,24},{24,20},{28,32},{32,28... | collective-permute-start | bytes 417800 | tf_op jit(solution)/shard_map/ppermute | solution.py:543
  19.1 0.0 collective-permute-start.3
  19.1 0.0 copy-start
  19.1 3.5 %collective-permute-done.2.r_ref = f32[34,8,128]{2,1,0:T(8,128)S(1)} collective-permute-done((f32[34,8,128]{2,1,0:T(8,128)S(1)}, f32[34,8,128]{2,1,0:T(8,128)S(1)}, u32[]{:S(2)}, u32[]{:S(2)}) %collective-permute-start.2) | collective-permute-done | bytes 139296 | tf_op jit(solution)/shard_map/ppermute | solution.py:543
  22.5 2.1 %collective-permute-done.3.q_ref = f32[34,8,128]{2,1,0:T(8,128)S(1)} collective-permute-done((f32[34,8,128]{2,1,0:T(8,128)S(1)}, f32[34,8,128]{2,1,0:T(8,128)S(1)}, u32[]{:S(2)}, u32[]{:S(2)}) %collective-permute-start.3) | collective-permute-done | bytes 139296 | tf_op jit(solution)/shard_map/ppermute | solution.py:544
  24.7 0.0 copy-done
  24.7 0.1 broadcast_in_dim.4.th_ref
  24.8 2.8 %momentum.1 = (f32[32,8,128]{2,1,0:T(8,128)S(1)}, f32[32,8,128]{2,1,0:T(8,128)S(1)}, f32[3,8,128]{2,1,0:T(8,128)S(1)}, f32[3,8,128]{2,1,0:T(8,128)S(1)}) custom-call(f32[32,8,128]{2,1,0:T(8,128)S(1)} %broadcast_in_dim.4.th_ref, f32[32,8,128]{2,1,0:T(8,128)S(1)} %get-tuple-element.41.t_ref, f32[32,8,128]{2,1,0:T(8,128)S(1)} %get-tuple-element.42.s_ref, ...), custom_call_target="tpu_custom_call" | custom-call | tf_op jit(solution)/shard_map/momentum/pallas_call | solution.py:545
  27.5 9.2 %all_to_all.10 = f32[8,3,8,128]{3,2,1,0:T(8,128)S(1)} all-to-all(f32[8,3,8,128]{3,2,1,0:T(8,128)S(1)} %broadcast_in_dim.5), channel_id=1, replica_groups=mesh['lon_hi'=8,'lon_lo'=8,'lat'=4] {'lon_lo'}, dimensions={0} | all-to-all | bytes 196608 | tf_op jit(solution)/shard_map/all_to_all | solution.py:504
  36.7 0.1 collective-permute-start.4
  36.8 4.5 %collective-permute-start.5 = (f32[120,128]{1,0:T(8,128)S(1)}, f32[120,128]{1,0:T(8,128)S(1)}, u32[]{:S(2)}, u32[]{:S(2)}) collective-permute-start(f32[120,128]{1,0:T(8,128)S(1)} %bitcast.7), channel_id=1, source_target_pairs={{0,224},{32,64},{64,32},{96,128},{128,96},{160,192},{192,160},{224... | collective-permute-start | bytes 184328 | tf_op jit(solution)/shard_map/ppermute | solution.py:555
  41.3 1.7 %tracers.1 = (f32[32,8,128]{2,1,0:T(8,128)}, f32[32,8,128]{2,1,0:T(8,128)}) custom-call(f32[32,8,128]{2,1,0:T(8,128)S(1)} %broadcast_in_dim.4.th_ref, f32[32,8,128]{2,1,0:T(8,128)S(1)} %get-tuple-element.41.t_ref, f32[32,8,128]{2,1,0:T(8,128)S(1)} %get-tuple-element.42.s_ref, f32[32,8,128]{2,1,0:T(8,128)S(1)} %get-tuple-element.43.u_ref, ...), custom_call_target="tpu_custom_call" | custom-call | tf_op jit(solution)/shard_map/tracers/pallas_call | solution.py:556
  43.0 0.0 collective-permute-done.4.q_ref
  43.0 0.0 collective-permute-done.5.r_ref
  43.0 1.9 %slab.1 = (f32[32,1,128]{2,1,0:T(1,128)}, f32[3,8,128]{2,1,0:T(8,128)S(1)}) custom-call(f32[192,128]{1,0:T(8,128)S(1)} %bitcast.6, f32[120,128]{1,0:T(8,128)S(1)} %collective-permute-done.4.q_ref, f32[120,128]{1,0:T(8,128)S(1)} %collective-permute-done.5.r_ref, f32[3,8,128]{2,1,0:T(8,128)S(1)} %get-tuple-element.70.st_ref), custom_call_target="tpu_custom_call" | custom-call | tf_op jit(solution)/shard_map/slab/pallas_call | solution.py:560
  44.9 11.0 %all-to-all-start.1 = ((f32[32,1,128]{2,1,0:T(1,128)}), f32[32,1,128]{2,1,0:T(1,128)S(1)}, u32[]{:S(2)}, u32[]{:S(2)}) async-start(f32[32,1,128]{2,1,0:T(1,128)} %get-tuple-element.75), calls=%async_computation.1 | async-start | bytes 32768 | tf_op jit(solution)/shard_map/all_to_all | solution.py:567
  55.9 0.7 %velocity.1 = (f32[32,8,128]{2,1,0:T(8,128)}, f32[32,8,128]{2,1,0:T(8,128)}, f32[8,128]{1,0:T(8,128)}) custom-call(f32[32,8,128]{2,1,0:T(8,128)S(1)} %get-tuple-element.65.us_ref, f32[32,8,128]{2,1,0:T(8,128)S(1)} %get-tuple-element.66.vs_ref, s32[8,128]{1,0:T(8,128)S(1)} %get-tuple-element.45.d_ref, s32[8,128]{1,0:T(8,128)S(1)} %get-tuple-element.46.m_ref, ...), custom_call_target="tpu_custom_call" | custom-call | tf_op jit(solution)/shard_map/velocity/pallas_call | solution.py:571
  56.6 7.1 %all-to-all-done.1 = f32[32,1,128]{2,1,0:T(1,128)S(1)} async-done(((f32[32,1,128]{2,1,0:T(1,128)}), f32[32,1,128]{2,1,0:T(1,128)S(1)}, u32[]{:S(2)}, u32[]{:S(2)}) %all-to-all-start.1) | async-done | bytes 16416 | tf_op jit(solution)/shard_map/all_to_all | solution.py:567
  63.7 0.1 reduce_sum.11
  (3 shorter events, 0.1 us)
Async XLA Ops:
  2.0 6.6 %collective-permute-start.1 = (f32[17,8,128]{2,1,0:T(8,128)S(1)}, f32[17,8,128]{2,1,0:T(8,128)S(1)}, u32[]{:S(2)}, u32[]{:S(2)}) collective-permute-start(f32[17,8,128]{2,1,0:T(8,128)S(1)} %get-tuple-element.49), channel_id=1, source_target_pairs={{1,2},{2,1},{3,255},{5,6},{6,5},{7,251},{9,10},{10,9},{11,247},{13... | collective-permute-start | bytes 208904 | tf_op jit(solution)/shard_map/ppermute | solution.py:518
  6.6 2.0 %collective-permute-start = (f32[17,8,128]{2,1,0:T(8,128)S(1)}, f32[17,8,128]{2,1,0:T(8,128)S(1)}, u32[]{:S(2)}, u32[]{:S(2)}) collective-permute-start(f32[17,8,128]{2,1,0:T(8,128)S(1)} %get-tuple-element.49), channel_id=1, source_target_pairs={{0,1},{1,0},{2,3},{3,2},{4,5},{5,4},{6,7},{7,6},{8,9},{9,8},{10,11... | collective-permute-start | bytes 208904 | tf_op jit(solution)/shard_map/ppermute | solution.py:518
  8.7 13.8 %collective-permute-start.2 = (f32[34,8,128]{2,1,0:T(8,128)S(1)}, f32[34,8,128]{2,1,0:T(8,128)S(1)}, u32[]{:S(2)}, u32[]{:S(2)}) collective-permute-start(f32[34,8,128]{2,1,0:T(8,128)S(1)} %get-tuple-element.53), channel_id=1, source_target_pairs={{0,252},{4,8},{8,4},{12,16},{16,12},{20,24},{24,20},{28,32},{32,28... | collective-permute-start | bytes 417800 | tf_op jit(solution)/shard_map/ppermute | solution.py:543
  19.1 5.6 %collective-permute-start.3 = (f32[34,8,128]{2,1,0:T(8,128)S(1)}, f32[34,8,128]{2,1,0:T(8,128)S(1)}, u32[]{:S(2)}, u32[]{:S(2)}) collective-permute-start(f32[34,8,128]{2,1,0:T(8,128)S(1)} %get-tuple-element.54), channel_id=1, source_target_pairs={{0,4},{4,0},{8,12},{12,8},{16,20},{20,16},{24,28},{28,24},{32,36},... | collective-permute-start | bytes 417800 | tf_op jit(solution)/shard_map/ppermute | solution.py:544
  19.1 5.6 %copy-start = (f32[32]{0:T(128)S(1)}, f32[32]{0:T(128)}, u32[]{:S(2)}) copy-start(f32[32]{0:T(128)} %param.15) | copy-start | bytes 388
  36.7 6.3 %collective-permute-start.4 = (f32[120,128]{1,0:T(8,128)S(1)}, f32[120,128]{1,0:T(8,128)S(1)}, u32[]{:S(2)}, u32[]{:S(2)}) collective-permute-start(f32[120,128]{1,0:T(8,128)S(1)} %bitcast.8), channel_id=1, source_target_pairs={{0,32},{32,0},{64,96},{96,64},{128,160},{160,128},{192,224},{224,1... | collective-permute-start | bytes 184328 | tf_op jit(solution)/shard_map/ppermute | solution.py:554
  36.8 6.2 %collective-permute-start.5 = (f32[120,128]{1,0:T(8,128)S(1)}, f32[120,128]{1,0:T(8,128)S(1)}, u32[]{:S(2)}, u32[]{:S(2)}) collective-permute-start(f32[120,128]{1,0:T(8,128)S(1)} %bitcast.7), channel_id=1, source_target_pairs={{0,224},{32,64},{64,32},{96,128},{128,96},{160,192},{192,160},{224... | collective-permute-start | bytes 184328 | tf_op jit(solution)/shard_map/ppermute | solution.py:555
  44.9 18.8 %all-to-all-start.1 = ((f32[32,1,128]{2,1,0:T(1,128)}), f32[32,1,128]{2,1,0:T(1,128)S(1)}, u32[]{:S(2)}, u32[]{:S(2)}) async-start(f32[32,1,128]{2,1,0:T(1,128)} %get-tuple-element.75), calls=%async_computation.1 | async-start | bytes 32768 | tf_op jit(solution)/shard_map/all_to_all | solution.py:567

commit v9 on v7

--- a/solution.py
+++ b/solution.py
@@ -377,7 +377,7 @@
     lax.fori_loop(0, levels // 2 // TILES_PER_STEP, step, (zero, zero))
 
 
-def slab_kernel(levels, own_ref, q_ref, r_ref, st_ref, sum_ref, flat_ref, we_s, wn_s, fac_s, inv_s, r_s, d_s, z_s):
+def slab_kernel(levels, own_ref, r_ref, q_ref, st_ref, sum_ref, flat_ref, we_s, wn_s, fac_s, inv_s, r_s, d_s, z_s):
     odd_group = jnp.full((GROUP, 128), lax.axis_index(LON[0]) % 2, jnp.int32) == 1
 
     def rows(i):
@@ -554,7 +554,7 @@
         (jax.ShapeDtypeStruct((groups * lat_size, 1, 128), F32), tiles(3)),
         [VMEM] * 4,
         [pltpu.VMEM((8, 3 * GROUP, 256), F32)] * 7,
-    )(group, group_q, group_r, start)
+    )(group, group_r, group_q, start)
     sums = lax.all_to_all(sums, ("lon_hi", "lat"), 0, 0, tiled=True)
     total = jnp.sum(sums, axis=0)
     cells = lon_size * 8 * lat_size * 128

time: 64 us -> 64 us (level)
  no operation moved by 1% of the time
where the time goes in v9:
time: 64 us; the launch traced here: 63.7 us
  starting transfers between devices  27.2 us (42%)
  waiting for transfers between devices  16.6 us (26%)
  blocking collectives  9.18 us (14%)
  Pallas kernels  8.58 us (13%)
  between operations  1.93 us (3%)
    ppermute x1, starting transfers between devices, per_device(): lax.ppermute(pair_r, LON, [(i, (i + 1 if i % 2 else i - 1) % lon_size) fo...  10.4 us
    all_to_all x1, blocking collectives, from_all(): return lax.all_to_all(copies, axes, 0, 0, tiled=True)  9.18 us
    all_to_all x1, starting transfers between devices, per_device(): sums = lax.all_to_all(sums, ('lon_hi', 'lat'), 0, 0, tiled=True)  7.78 us
    all_to_all x1, waiting for transfers between devices, per_device(): sums = lax.all_to_all(sums, ('lon_hi', 'lat'), 0, 0, tiled=True)  7.14 us
    ppermute x1, starting transfers between devices, lat_swap(): lax.ppermute(x, (*LON, 'lat'), pairs_b)  4.59 us
    ppermute x1, starting transfers between devices, per_device(): lax.ppermute(group, 'lon_hi', [(i, (i + 1 if i % 2 else i - 1) % groups)...  4.41 us
    ppermute x1, waiting for transfers between devices, per_device(): lax.ppermute(pair_r, LON, [(i, (i + 1 if i % 2 else i - 1) % lon_size) fo...  3.47 us
    pallas_call x1, Pallas kernels, per_device(): call(functools.partial(momentum_kernel, lat_size), 'momentum', (field, fi...  2.81 us
  transfers between devices with their start and end apart: 7, of which 6 were waited for; matrix products, arithmetic and copies ran while one was open for 0% of the time, Pallas kernels for 4%

profile of v9, /device:TPU:1, one launch (start us, length us, event | category | flops | bytes accessed | tf_op | source)
XLA Modules:
  0.0 63.7 jit_solution(9803682180374347381)
XLA Ops:
  0.6 1.4 %lat_pack.1 = (f32[17,8,128]{2,1,0:T(8,128)S(1)}, f32[32,8,128]{2,1,0:T(8,128)S(1)}, f32[32,8,128]{2,1,0:T(8,128)S(1)}, f32[32,8,128]{2,1,0:T(8,128)S(1)}, f32[3...) custom-call(f32[32,8,128]{2,1,0:T(8,128)} %t_hbm.1, ...), custom_call_target="tpu_custom_call" | custom-call | tf_op jit(solution)/shard_map/lat_pack/pallas_call | solution.py:522
  2.0 4.6 %collective-permute-start.1 = (f32[17,8,128]{2,1,0:T(8,128)S(1)}, f32[17,8,128]{2,1,0:T(8,128)S(1)}, u32[]{:S(2)}, u32[]{:S(2)}) collective-permute-start(f32[17,8,128]{2,1,0:T(8,128)S(1)} %get-tuple-element.45), channel_id=1, source_target_pairs={{1,2},{2,1},{3,255},{5,6},{6,5},{7,251},{9,10},{10,9},{11,247},{13... | collective-permute-start | bytes 208904 | tf_op jit(solution)/shard_map/ppermute | solution.py:512
  6.6 0.1 collective-permute-start
  6.7 0.1 lon_rows.1
  6.8 1.8 %collective-permute-done.1.b_ref = f32[17,8,128]{2,1,0:T(8,128)S(1)} collective-permute-done((f32[17,8,128]{2,1,0:T(8,128)S(1)}, f32[17,8,128]{2,1,0:T(8,128)S(1)}, u32[]{:S(2)}, u32[]{:S(2)}) %collective-permute-start.1) | collective-permute-done | bytes 69664 | tf_op jit(solution)/shard_map/ppermute | solution.py:512
  8.6 0.0 collective-permute-done.a_ref
  8.7 0.0 copy-start
  8.7 10.4 %collective-permute-start.2 = (f32[34,8,128]{2,1,0:T(8,128)S(1)}, f32[34,8,128]{2,1,0:T(8,128)S(1)}, u32[]{:S(2)}, u32[]{:S(2)}) collective-permute-start(f32[34,8,128]{2,1,0:T(8,128)S(1)} %get-tuple-element.49), channel_id=1, source_target_pairs={{0,252},{4,8},{8,4},{12,16},{16,12},{20,24},{24,20},{28,32},{32,28... | collective-permute-start | bytes 417800 | tf_op jit(solution)/shard_map/ppermute | solution.py:537
  19.1 0.0 collective-permute-start.3
  19.1 3.5 %collective-permute-done.2.r_ref = f32[34,8,128]{2,1,0:T(8,128)S(1)} collective-permute-done((f32[34,8,128]{2,1,0:T(8,128)S(1)}, f32[34,8,128]{2,1,0:T(8,128)S(1)}, u32[]{:S(2)}, u32[]{:S(2)}) %collective-permute-start.2) | collective-permute-done | bytes 139296 | tf_op jit(solution)/shard_map/ppermute | solution.py:537
  22.5 2.1 %collective-permute-done.3.q_ref = f32[34,8,128]{2,1,0:T(8,128)S(1)} collective-permute-done((f32[34,8,128]{2,1,0:T(8,128)S(1)}, f32[34,8,128]{2,1,0:T(8,128)S(1)}, u32[]{:S(2)}, u32[]{:S(2)}) %collective-permute-start.3) | collective-permute-done | bytes 139296 | tf_op jit(solution)/shard_map/ppermute | solution.py:538
  24.7 0.0 copy-done
  24.7 0.1 broadcast_in_dim.4.th_ref
  24.8 2.8 %momentum.1 = (f32[32,8,128]{2,1,0:T(8,128)S(1)}, f32[32,8,128]{2,1,0:T(8,128)S(1)}, f32[3,8,128]{2,1,0:T(8,128)S(1)}, f32[3,8,128]{2,1,0:T(8,128)S(1)}) custom-call(f32[32,8,128]{2,1,0:T(8,128)S(1)} %broadcast_in_dim.4.th_ref, f32[32,8,128]{2,1,0:T(8,128)S(1)} %get-tuple-element.37.t_ref, f32[32,8,128]{2,1,0:T(8,128)S(1)} %get-tuple-element.38.s_ref, ...), custom_call_target="tpu_custom_call" | custom-call | tf_op jit(solution)/shard_map/momentum/pallas_call | solution.py:539
  27.6 9.2 %all_to_all.10 = f32[8,3,8,128]{3,2,1,0:T(8,128)S(1)} all-to-all(f32[8,3,8,128]{3,2,1,0:T(8,128)S(1)} %broadcast_in_dim.5), channel_id=1, replica_groups=mesh['lon_hi'=8,'lon_lo'=8,'lat'=4] {'lon_lo'}, dimensions={0} | all-to-all | bytes 196608 | tf_op jit(solution)/shard_map/all_to_all | solution.py:498
  36.8 4.4 %collective-permute-start.5 = (f32[192,128]{1,0:T(8,128)S(1)}, f32[192,128]{1,0:T(8,128)S(1)}, u32[]{:S(2)}, u32[]{:S(2)}) collective-permute-start(f32[192,128]{1,0:T(8,128)S(1)} %bitcast.4), channel_id=1, source_target_pairs={{0,224},{32,64},{64,32},{96,128},{128,96},{160,192},{192,160},{224... | collective-permute-start | bytes 294920 | tf_op jit(solution)/shard_map/ppermute | solution.py:546
  41.2 0.0 collective-permute-start.4
  41.2 1.7 %tracers.1 = (f32[32,8,128]{2,1,0:T(8,128)}, f32[32,8,128]{2,1,0:T(8,128)}) custom-call(f32[32,8,128]{2,1,0:T(8,128)S(1)} %broadcast_in_dim.4.th_ref, f32[32,8,128]{2,1,0:T(8,128)S(1)} %get-tuple-element.37.t_ref, f32[32,8,128]{2,1,0:T(8,128)S(1)} %get-tuple-element.38.s_ref, f32[32,8,128]{2,1,0:T(8,128)S(1)} %get-tuple-element.39.u_ref, ...), custom_call_target="tpu_custom_call" | custom-call | tf_op jit(solution)/shard_map/tracers/pallas_call | solution.py:547
  42.9 0.3 collective-permute-done.5.r_ref
  43.2 1.8 %collective-permute-done.4.q_ref = f32[192,128]{1,0:T(8,128)S(1)} collective-permute-done((f32[192,128]{1,0:T(8,128)S(1)}, f32[192,128]{1,0:T(8,128)S(1)}, u32[]{:S(2)}, u32[]{:S(2)}) %collective-permute-start.4) | collective-permute-done | bytes 98336 | tf_op jit(solution)/shard_map/ppermute | solution.py:545
  44.9 1.9 %slab.1 = (f32[32,1,128]{2,1,0:T(1,128)}, f32[3,8,128]{2,1,0:T(8,128)S(1)}) custom-call(f32[192,128]{1,0:T(8,128)S(1)} %bitcast.6, f32[192,128]{1,0:T(8,128)S(1)} %collective-permute-done.5.r_ref, f32[192,128]{1,0:T(8,128)S(1)} %collective-permute-done.4.q_ref, f32[3,8,128]{2,1,0:T(8,128)S(1)} %get-tuple-element.62.st_ref), custom_call_target="tpu_custom_call" | custom-call | tf_op jit(solution)/shard_map/slab/pallas_call | solution.py:551
  46.8 7.8 %all-to-all-start.1 = ((f32[32,1,128]{2,1,0:T(1,128)}), f32[32,1,128]{2,1,0:T(1,128)S(1)}, u32[]{:S(2)}, u32[]{:S(2)}) async-start(f32[32,1,128]{2,1,0:T(1,128)} %get-tuple-element.67), calls=%async_computation.1 | async-start | bytes 32768 | tf_op jit(solution)/shard_map/all_to_all | solution.py:558
  54.6 0.7 %velocity.1 = (f32[32,8,128]{2,1,0:T(8,128)}, f32[32,8,128]{2,1,0:T(8,128)}, f32[8,128]{1,0:T(8,128)}) custom-call(f32[32,8,128]{2,1,0:T(8,128)S(1)} %get-tuple-element.58.us_ref, f32[32,8,128]{2,1,0:T(8,128)S(1)} %get-tuple-element.59.vs_ref, s32[8,128]{1,0:T(8,128)S(1)} %get-tuple-element.41.d_ref, s32[8,128]{1,0:T(8,128)S(1)} %get-tuple-element.42.m_ref, ...), custom_call_target="tpu_custom_call" | custom-call | tf_op jit(solution)/shard_map/velocity/pallas_call | solution.py:562
  55.3 7.1 %all-to-all-done.1 = f32[32,1,128]{2,1,0:T(1,128)S(1)} async-done(((f32[32,1,128]{2,1,0:T(1,128)}), f32[32,1,128]{2,1,0:T(1,128)S(1)}, u32[]{:S(2)}, u32[]{:S(2)}) %all-to-all-start.1) | async-done | bytes 16416 | tf_op jit(solution)/shard_map/all_to_all | solution.py:558
  62.5 0.1 reduce_sum.11
  (2 shorter events, 0.1 us)
Async XLA Ops:
  2.0 6.6 %collective-permute-start.1 = (f32[17,8,128]{2,1,0:T(8,128)S(1)}, f32[17,8,128]{2,1,0:T(8,128)S(1)}, u32[]{:S(2)}, u32[]{:S(2)}) collective-permute-start(f32[17,8,128]{2,1,0:T(8,128)S(1)} %get-tuple-element.45), channel_id=1, source_target_pairs={{1,2},{2,1},{3,255},{5,6},{6,5},{7,251},{9,10},{10,9},{11,247},{13... | collective-permute-start | bytes 208904 | tf_op jit(solution)/shard_map/ppermute | solution.py:512
  6.6 2.0 %collective-permute-start = (f32[17,8,128]{2,1,0:T(8,128)S(1)}, f32[17,8,128]{2,1,0:T(8,128)S(1)}, u32[]{:S(2)}, u32[]{:S(2)}) collective-permute-start(f32[17,8,128]{2,1,0:T(8,128)S(1)} %get-tuple-element.45), channel_id=1, source_target_pairs={{0,1},{1,0},{2,3},{3,2},{4,5},{5,4},{6,7},{7,6},{8,9},{9,8},{10,11... | collective-permute-start | bytes 208904 | tf_op jit(solution)/shard_map/ppermute | solution.py:512
  8.7 16.0 %copy-start = (f32[32]{0:T(128)S(1)}, f32[32]{0:T(128)}, u32[]{:S(2)}) copy-start(f32[32]{0:T(128)} %param.15) | copy-start | bytes 388
  8.7 13.8 %collective-permute-start.2 = (f32[34,8,128]{2,1,0:T(8,128)S(1)}, f32[34,8,128]{2,1,0:T(8,128)S(1)}, u32[]{:S(2)}, u32[]{:S(2)}) collective-permute-start(f32[34,8,128]{2,1,0:T(8,128)S(1)} %get-tuple-element.49), channel_id=1, source_target_pairs={{0,252},{4,8},{8,4},{12,16},{16,12},{20,24},{24,20},{28,32},{32,28... | collective-permute-start | bytes 417800 | tf_op jit(solution)/shard_map/ppermute | solution.py:537
  19.1 5.6 %collective-permute-start.3 = (f32[34,8,128]{2,1,0:T(8,128)S(1)}, f32[34,8,128]{2,1,0:T(8,128)S(1)}, u32[]{:S(2)}, u32[]{:S(2)}) collective-permute-start(f32[34,8,128]{2,1,0:T(8,128)S(1)} %get-tuple-element.50), channel_id=1, source_target_pairs={{0,4},{4,0},{8,12},{12,8},{16,20},{20,16},{24,28},{28,24},{32,36},... | collective-permute-start | bytes 417800 | tf_op jit(solution)/shard_map/ppermute | solution.py:538
  36.8 6.4 %collective-permute-start.5 = (f32[192,128]{1,0:T(8,128)S(1)}, f32[192,128]{1,0:T(8,128)S(1)}, u32[]{:S(2)}, u32[]{:S(2)}) collective-permute-start(f32[192,128]{1,0:T(8,128)S(1)} %bitcast.4), channel_id=1, source_target_pairs={{0,224},{32,64},{64,32},{96,128},{128,96},{160,192},{192,160},{224... | collective-permute-start | bytes 294920 | tf_op jit(solution)/shard_map/ppermute | solution.py:546
  41.2 3.8 %collective-permute-start.4 = (f32[192,128]{1,0:T(8,128)S(1)}, f32[192,128]{1,0:T(8,128)S(1)}, u32[]{:S(2)}, u32[]{:S(2)}) collective-permute-start(f32[192,128]{1,0:T(8,128)S(1)} %bitcast.5), channel_id=1, source_target_pairs={{0,32},{32,0},{64,96},{96,64},{128,160},{160,128},{192,224},{224,1... | collective-permute-start | bytes 294920 | tf_op jit(solution)/shard_map/ppermute | solution.py:545
  46.8 15.6 %all-to-all-start.1 = ((f32[32,1,128]{2,1,0:T(1,128)}), f32[32,1,128]{2,1,0:T(1,128)S(1)}, u32[]{:S(2)}, u32[]{:S(2)}) async-start(f32[32,1,128]{2,1,0:T(1,128)} %get-tuple-element.67), calls=%async_computation.1 | async-start | bytes 32768 | tf_op jit(solution)/shard_map/all_to_all | solution.py:558
